TPU v7x, 128 devices: a whole 4x4x4 slice. The times are simulated.
128 devices in a mesh: gx: 16 (over y_hi, x, core), gy: 8 (over y_lo, z).
Axes of the slice: x: 4, y: 4 (y_hi: 2, y_lo: 2; y = y_hi * 2 + y_lo), z: 4, core: 2. Of those that a mesh axis runs over, the one named last changes fastest.
Arguments:
- held_head: float32 [16384, 8, 128], P(('gx', 'gy')), may hold values from -6 to -0.5
- held_head_old: float32 [16384, 8, 128], P(('gx', 'gy')), may hold values from -6 to -0.5
- material_ids: int32 [128, 128, 1024], P(None, 'gx', 'gy'), may hold values from 0 to 15
- block_map: int32 [128, 128], replicated, may hold values from 0 to 127, as said below
- conductivity: float32 [3, 16], replicated, may hold values from 0.1 to 10
- vg_alpha: float32 [16], replicated, may hold values from 0.5 to 4
- vg_n: float32 [16], replicated, may hold values from 1.5 to 3
- capacity: float32 [16], replicated, may hold values from 0.1 to 0.45
Outputs:
- update: float32 [128, 128, 1024], P(None, 'gx', 'gy')
Inputs may be any that keep to these rules, and one draw needn't show every extreme that they name: Every row and every column of block_map holds each brick number once.
All inputs are finite; a program needn't handle non-finite values.
Results may differ from a plain program's by a relative error of at most 0.0001.
Values sent between devices are 32-bit elements; how exact they have to be, the bound alone decides.
No kernel may reach another device: no remote copies, remote signals or barrier semaphores. Data moves between devices by JAX's collectives and lax.ppermute only.
A program may use at most 128 MiB of HBM per device.

v0:
```python
import jax
import jax.numpy as jnp
from jax import lax
from jax.sharding import PartitionSpec as P

MATERIALS = 16
ITERS = 4


STORE = 4.0


def extended(cells, sides, width):
    for axis, dim in sides:
        count = lax.axis_size(axis)
        ends = count - 1
        head = lax.slice_in_dim(cells, 0, width, axis=dim)
        tail = lax.slice_in_dim(cells, cells.shape[dim] - width, cells.shape[dim], axis=dim)
        cells = jnp.concatenate(
            [
                lax.ppermute(tail, axis, [(i, (i + 1) % count) for i in range(ends)]),
                cells,
                lax.ppermute(head, axis, [((i + 1) % count, i) for i in range(ends)]),
            ],
            axis=dim,
        )
    return cells


def retention(level, alpha_cell, expo_cell):
    scaled = alpha_cell * -level
    power = jnp.exp(expo_cell * jnp.log(scaled))
    exponent = 1.0 - 1.0 / expo_cell
    inverse = 1.0 / (1.0 + power)
    saturation = jnp.exp(exponent * jnp.log(inverse))
    inner_term = -jnp.expm1(exponent * jnp.log1p(-inverse))
    relperm = jnp.sqrt(saturation) * inner_term * inner_term
    return (saturation, relperm)


def properties(material_ids, conductivity, vg_alpha, vg_n, capacity):
    blank = jnp.zeros(material_ids.shape, conductivity.dtype)
    fields = [blank, blank, blank, blank, blank, blank]
    for m in range(MATERIALS):
        match_cell = material_ids == m
        values = (
            conductivity[0, m],
            conductivity[1, m],
            conductivity[2, m],
            vg_alpha[m],
            vg_n[m],
            capacity[m],
        )
        fields = [jnp.where(match_cell, value, field) for value, field in zip(values, fields)]
    return fields


def pair_slices(padded, axis):
    lower_index = [slice(1, -1), slice(1, -1), slice(1, -1)]
    higher_index = [slice(1, -1), slice(1, -1), slice(1, -1)]
    lower_index[axis] = slice(0, -1)
    higher_index[axis] = slice(1, None)
    return (padded[tuple(lower_index)], padded[tuple(higher_index)])


def face_terms(pad_head, pad_rel, pad_cond, axis, rise):
    head_low, head_high = pair_slices(pad_head, axis)
    rel_low, rel_high = pair_slices(pad_rel, axis)
    cond_low, cond_high = pair_slices(pad_cond, axis)
    trans = 2.0 * cond_low * cond_high / (cond_low + cond_high)
    potential = head_high - head_low + rise
    along = trans * (0.5 * (rel_low + rel_high))
    slope = trans * potential * 0.5
    return (along, slope, along * potential)


def net_inflow(flux, axis):
    extent = flux.shape[axis]
    return lax.slice_in_dim(flux, 1, extent, axis=axis) - lax.slice_in_dim(
        flux, 0, extent - 1, axis=axis
    )


def least_squares(hess, beta):
    matrix_rows = [hess[i] for i in range(ITERS + 1)]
    target = [beta] + [jnp.zeros_like(beta) for i in range(ITERS)]
    for j in range(ITERS):
        first = matrix_rows[j][j]
        second = matrix_rows[j + 1][j]
        radius = jnp.sqrt(first * first + second * second)
        cosine = first / radius
        sine_value = second / radius
        row_top, row_next = (matrix_rows[j], matrix_rows[j + 1])
        matrix_rows[j] = cosine * row_top + sine_value * row_next
        matrix_rows[j + 1] = cosine * row_next - sine_value * row_top
        goal_top, goal_next = (target[j], target[j + 1])
        target[j] = cosine * goal_top + sine_value * goal_next
        target[j + 1] = cosine * goal_next - sine_value * goal_top
    coeffs = [None] * ITERS
    for j in reversed(range(ITERS)):
        running = target[j]
        for k in range(j + 1, ITERS):
            running = running - matrix_rows[j][k] * coeffs[k]
        coeffs[j] = running / matrix_rows[j][j]
    return coeffs


def global_length(field):
    return jnp.sqrt(lax.psum(jnp.sum(field * field), ("gx", "gy")))


def body(held_head, held_head_old, material_ids, block_map, conductivity, vg_alpha, vg_n, capacity):
    devices = lax.axis_size(("gx", "gy"))
    own_index = lax.axis_index(("gx", "gy"))
    layers = held_head.shape[0]
    slab_depth = layers // devices
    brick_shape = held_head.shape
    piece_shape = (devices, slab_depth) + tuple(held_head.shape[1:])
    numbers = jnp.arange(devices, dtype=jnp.int32)
    own_row = block_map[own_index]
    send_order = jnp.sum(
        jnp.where(own_row[None, :] == numbers[:, None], numbers[None, :], 0), axis=1
    )
    outgoing_head = jnp.take(held_head.reshape(piece_shape), send_order, axis=0)
    outgoing_old = jnp.take(held_head_old.reshape(piece_shape), send_order, axis=0)
    incoming_head, incoming_old = (
        lax.all_to_all(outgoing_head, ("gx", "gy"), split_axis=0, concat_axis=0, tiled=True),
        lax.all_to_all(outgoing_old, ("gx", "gy"), split_axis=0, concat_axis=0, tiled=True),
    )
    source_of = jnp.sum(jnp.where(block_map == own_index, numbers[:, None], 0), axis=0)
    head = jnp.take(incoming_head, source_of, axis=0).reshape(brick_shape)
    head_old = jnp.take(incoming_old, source_of, axis=0).reshape(brick_shape)
    cond_x, cond_y, cond_z, alpha_cell, expo_cell, cap_cell = properties(
        material_ids, conductivity, vg_alpha, vg_n, capacity
    )
    ones_field = jnp.ones_like(head)
    (saturation, relperm), (d_sat, d_rel) = jax.jvp(
        lambda level: retention(level, alpha_cell, expo_cell), (head,), (ones_field,)
    )
    stacked = jnp.stack([head, relperm, d_rel, cond_x, cond_y])
    rimmed = extended(stacked, (("gx", 2), ("gy", 3)), 1)
    old_sat = retention(head_old, alpha_cell, expo_cell)[0]
    padded = jnp.pad(rimmed, ((0, 0), (1, 1), (0, 0), (0, 0)))
    pad_head = padded[0]
    pad_rel = padded[1]
    pad_drel = padded[2]
    layout = [(1, padded[3], 0.0), (2, padded[4], 0.0), (0, jnp.pad(cond_z, 1), 1.0)]
    coefficients = []
    total_in = None
    for axis, pad_cond, rise in layout:
        along, slope, flux = face_terms(pad_head, pad_rel, pad_cond, axis, rise)
        coefficients.append((axis, along, slope))
        inflow = net_inflow(flux, axis)
        total_in = inflow if total_in is None else total_in + inflow
    newton_residual = STORE * cap_cell * (saturation - old_sat) - total_in
    diagonal = STORE * cap_cell * d_sat
    start = -newton_residual
    beta = global_length(start)
    basis = [start / beta]
    hess = jnp.zeros((ITERS + 1, ITERS), newton_residual.dtype)
    for j in range(ITERS):
        field = basis[j]
        rim_field = extended(field, (("gx", 1), ("gy", 2)), 1)
        pad_field = jnp.pad(rim_field, ((1, 1), (0, 0), (0, 0)))
        pad_weighted = pad_drel * pad_field
        total_change = None
        for apply_axis, apply_along, apply_slope in coefficients:
            field_low, field_high = pair_slices(pad_field, apply_axis)
            weight_low, weight_high = pair_slices(pad_weighted, apply_axis)
            change = apply_along * (field_high - field_low) + apply_slope * (
                weight_low + weight_high
            )
            apply_inflow = net_inflow(change, apply_axis)
            total_change = apply_inflow if total_change is None else total_change + apply_inflow
        image = diagonal * field - total_change
        products = []
        for k in range(j + 1):
            product_value = lax.psum(jnp.sum(image * basis[k]), ("gx", "gy"))
            products.append(product_value)
            image = image - product_value * basis[k]
        norm_value = global_length(image)
        for k in range(j + 1):
            hess = hess.at[k, j].set(products[k])
        hess = hess.at[j + 1, j].set(norm_value)
        if j + 1 < ITERS:
            basis.append(image / norm_value)
    coeffs = least_squares(hess, beta)
    update = coeffs[0] * basis[0]
    for k in range(1, ITERS):
        update = update + coeffs[k] * basis[k]
    return update


def solution(mesh):
    return jax.shard_map(
        body,
        mesh=mesh,
        in_specs=(
            P(("gx", "gy"), None, None),
            P(("gx", "gy"), None, None),
            P(None, "gx", "gy"),
            P(),
            P(),
            P(),
            P(),
            P(),
        ),
        out_specs=P(None, "gx", "gy"),
        check_vma=False,
    )
```

profile of v0, /device:TPU:1, one launch (start us, length us, event | category | flops | bytes accessed | tf_op | source)
XLA Modules:
  0.0 1354.2 jit_solution(7113070374711121353)
XLA Ops:
  4.8 11.5 all-to-all-start
  20.0 12.7 select_select_fusion
  33.7 23.6 %bitcast_dynamic-update-slice_fusion.3 = (f32[5,128,8,128]{3,2,1,0:T(8,128)S(1)}, f32[128,8,128]{2,1,0:T(8,128)S(1)}, f32[128,8,128]{2,1,0:T(8,128)S(1)}) fusion(f32[5,128,8,128]{3,2,1,0:T(8,128)S(1)} %bitcast_dynamic-update-slice_fusion.4, f32[128,8,128]{2,1,0:T(8,128)S(1)} %gather_fusion.1, pred[128]{0:T(512)(128)(4,1)S(1)} %compare_and_fusion, ...), kind=kLoop, calls=%fused_computation.182 | loop fusion | flops 6029312 | bytes 4194944
  59.2 10.8 bitcast_dynamic-update-slice_fusion.1
  70.0 10.7 bitcast_dynamic-update-slice_fusion
  82.0 3.0 collective-permute-start.1
  87.5 22.6 %all-to-all-start.1 = ((f32[128,1,8,128]{3,2,1,0:T(8,128)}), f32[128,1,8,128]{3,2,1,0:T(8,128)}, u32[]{:S(2)}, u32[]{:S(2)}) async-start(f32[128,1,8,128]{3,2,1,0:T(8,128)} %get-tuple-element.347), calls=%async_computation.1 | async-start | bytes 1048576 | tf_op jit(solution)/shard_map/all_to_all | solution.py:128
  112.2 5.9 fusion.90
  118.0 3.3 copy.62
  122.6 3.3 copy.61
  125.9 4.0 collective-permute-start.2
  133.2 3.2 copy.64
  136.4 3.2 copy.63
  139.6 11.1 select_maximum_fusion
  151.7 3.0 copy-done.2
  158.9 2.8 fusion.77
  161.8 13.3 multiply_reduce_fusion.14
  175.1 67.8 %psum.105 = f32[]{:T(128)} all-reduce(f32[]{:T(128)} %get-tuple-element.205), channel_id=1, replica_groups=mesh['gx'=16,'gy'=8] {'gx','gy'}, use_global_device_ids=true, to_apply=%region_3.5 | all-reduce | flops 1 | bytes 8 | tf_op jit(solution)/shard_map/psum | solution.py:109
  246.3 3.4 collective-permute-start.5
  257.0 4.0 collective-permute-start.6
  263.9 3.9 fusion.5
  270.4 2.7 fusion.25
  273.2 2.8 fusion.29
  276.0 2.7 multiply_reduce_fusion.13
  278.6 72.1 %psum.106 = f32[]{:T(128)} all-reduce(f32[]{:T(128)} %get-tuple-element.194), channel_id=1, replica_groups=mesh['gx'=16,'gy'=8] {'gx','gy'}, use_global_device_ids=true, to_apply=%region_5.7 | all-reduce | flops 1 | bytes 8 | tf_op jit(solution)/shard_map/psum | solution.py:178
  352.2 64.4 %psum.107 = f32[]{:T(128)} all-reduce(f32[]{:T(128)} %multiply_reduce_fusion.12), channel_id=1, replica_groups=mesh['gx'=16,'gy'=8] {'gx','gy'}, use_global_device_ids=true, to_apply=%region_7.9 | all-reduce | flops 1 | bytes 8 | tf_op jit(solution)/shard_map/psum | solution.py:109
  418.2 3.0 collective-permute-start.8
  421.2 2.7 collective-permute-start.9
  430.0 4.0 collective-permute-start.10
  436.2 3.4 fusion.4
  445.2 72.8 %psum.108 = f32[]{:T(128)} all-reduce(f32[]{:T(128)} %get-tuple-element.190), channel_id=1, replica_groups=mesh['gx'=16,'gy'=8] {'gx','gy'}, use_global_device_ids=true, to_apply=%region_9.11 | all-reduce | flops 1 | bytes 8 | tf_op jit(solution)/shard_map/psum | solution.py:178
  519.4 64.4 %psum.109 = f32[]{:T(128)} all-reduce(f32[]{:T(128)} %multiply_reduce_fusion.10), channel_id=1, replica_groups=mesh['gx'=16,'gy'=8] {'gx','gy'}, use_global_device_ids=true, to_apply=%region_11.13 | all-reduce | flops 1 | bytes 8 | tf_op jit(solution)/shard_map/psum | solution.py:178
  585.9 62.5 %psum.110 = f32[]{:T(128)} all-reduce(f32[]{:T(128)} %get-tuple-element.188), channel_id=1, replica_groups=mesh['gx'=16,'gy'=8] {'gx','gy'}, use_global_device_ids=true, to_apply=%region_13.15 | all-reduce | flops 1 | bytes 8 | tf_op jit(solution)/shard_map/psum | solution.py:109
  651.7 3.1 collective-permute-start.13
  662.5 4.4 collective-permute-start.14
  670.4 3.7 fusion.3
  679.6 71.0 %psum.111 = f32[]{:T(128)} all-reduce(f32[]{:T(128)} %get-tuple-element.184), channel_id=1, replica_groups=mesh['gx'=16,'gy'=8] {'gx','gy'}, use_global_device_ids=true, to_apply=%region_16.18 | all-reduce | flops 1 | bytes 8 | tf_op jit(solution)/shard_map/psum | solution.py:178
  752.0 64.4 %psum.112 = f32[]{:T(128)} all-reduce(f32[]{:T(128)} %multiply_reduce_fusion.7), channel_id=1, replica_groups=mesh['gx'=16,'gy'=8] {'gx','gy'}, use_global_device_ids=true, to_apply=%region_18.20 | all-reduce | flops 1 | bytes 8 | tf_op jit(solution)/shard_map/psum | solution.py:178
  818.6 62.5 %psum.113 = f32[]{:T(128)} all-reduce(f32[]{:T(128)} %get-tuple-element.182), channel_id=1, replica_groups=mesh['gx'=16,'gy'=8] {'gx','gy'}, use_global_device_ids=true, to_apply=%region_20.22 | all-reduce | flops 1 | bytes 8 | tf_op jit(solution)/shard_map/psum | solution.py:178
  883.1 64.1 %psum.114 = f32[]{:T(128)} all-reduce(f32[]{:T(128)} %multiply_reduce_fusion.5), channel_id=1, replica_groups=mesh['gx'=16,'gy'=8] {'gx','gy'}, use_global_device_ids=true, to_apply=%region_22.24 | all-reduce | flops 1 | bytes 8 | tf_op jit(solution)/shard_map/psum | solution.py:109
  949.7 3.0 collective-permute-start.16
  963.0 4.0 collective-permute-start.18
  981.1 3.7 fusion.2
  989.9 69.3 %psum.115 = f32[]{:T(128)} all-reduce(f32[]{:T(128)} %get-tuple-element.178), channel_id=1, replica_groups=mesh['gx'=16,'gy'=8] {'gx','gy'}, use_global_device_ids=true, to_apply=%region_25.27 | all-reduce | flops 1 | bytes 8 | tf_op jit(solution)/shard_map/psum | solution.py:178
  1060.8 64.2 %psum.116 = f32[]{:T(128)} all-reduce(f32[]{:T(128)} %multiply_reduce_fusion.3), channel_id=1, replica_groups=mesh['gx'=16,'gy'=8] {'gx','gy'}, use_global_device_ids=true, to_apply=%region_27.29 | all-reduce | flops 1 | bytes 8 | tf_op jit(solution)/shard_map/psum | solution.py:178
  1127.1 62.5 %psum.117 = f32[]{:T(128)} all-reduce(f32[]{:T(128)} %get-tuple-element.176), channel_id=1, replica_groups=mesh['gx'=16,'gy'=8] {'gx','gy'}, use_global_device_ids=true, to_apply=%region_29.31 | all-reduce | flops 1 | bytes 8 | tf_op jit(solution)/shard_map/psum | solution.py:178
  1192.9 64.1 %psum.118 = f32[]{:T(128)} all-reduce(f32[]{:T(128)} %multiply_reduce_fusion.1), channel_id=1, replica_groups=mesh['gx'=16,'gy'=8] {'gx','gy'}, use_global_device_ids=true, to_apply=%region_31.33 | all-reduce | flops 1 | bytes 8 | tf_op jit(solution)/shard_map/psum | solution.py:178
  1262.3 62.6 %psum.119 = f32[]{:T(128)} all-reduce(f32[]{:T(128)} %multiply_reduce_fusion), channel_id=1, replica_groups=mesh['gx'=16,'gy'=8] {'gx','gy'}, use_global_device_ids=true, to_apply=%region_33.35 | all-reduce | flops 1 | bytes 8 | tf_op jit(solution)/shard_map/psum | solution.py:109
  (320 shorter events, 134.4 us)
Async XLA Ops:
  1.8 14.5 %copy-start.84 = (s32[128,128]{1,0:T(8,128)S(1)}, s32[128,128]{1,0:T(8,128)}, u32[]{:S(2)}) copy-start(s32[128,128]{1,0:T(8,128)} %param.41) | copy-start | bytes 196612
  1.8 14.6 %copy-start.80 = (f32[3,16]{1,0:T(4,128)S(1)}, f32[3,16]{1,0:T(4,128)}, u32[]{:S(2)}) copy-start(f32[3,16]{1,0:T(4,128)} %param.42) | copy-start | bytes 580
  1.8 16.7 %copy-start.81 = (f32[16]{0:T(128)S(1)}, f32[16]{0:T(128)}, u32[]{:S(2)}) copy-start(f32[16]{0:T(128)} %param.43) | copy-start | bytes 196
  1.9 17.4 %copy-start.82 = (f32[16]{0:T(128)S(1)}, f32[16]{0:T(128)}, u32[]{:S(2)}) copy-start(f32[16]{0:T(128)} %param.44) | copy-start | bytes 196
  1.9 18.2 %copy-start.79 = (s32[128,8,128]{2,1,0:T(8,128)S(1)}, s32[128,8,128]{2,1,0:T(8,128)}, u32[]{:S(2)}) copy-start(s32[128,8,128]{2,1,0:T(8,128)} %param.40) | copy-start | bytes 1572868
  4.8 27.9 %all-to-all-start = ((f32[128,1,8,128]{3,2,1,0:T(8,128)}), f32[128,1,8,128]{3,2,1,0:T(8,128)S(1)}, u32[]{:S(2)}, u32[]{:S(2)}) async-start(f32[128,1,8,128]{3,2,1,0:T(8,128)} %get-tuple-element.348), calls=%async_computation | async-start | bytes 1048576 | tf_op jit(solution)/shard_map/all_to_all | solution.py:127
  82.0 28.2 %collective-permute-start.1 = (f32[5,128,1,128]{3,2,1,0:T(1,128)}, f32[5,128,1,128]{3,2,1,0:T(1,128)}, u32[]{:S(2)}, u32[]{:S(2)}) collective-permute-start(f32[5,128,1,128]{3,2,1,0:T(1,128)} %get-tuple-element.241), channel_id=1, source_target_pairs={{8,0},{16,8},{24,16},{32,24},{40,32},{48,40},{56,48},{64,56},{72,6... | collective-permute-start | bytes 983048 | tf_op jit(solution)/shard_map/ppermute | solution.py:23
  84.9 25.2 %collective-permute-start = (f32[5,128,1,128]{3,2,1,0:T(1,128)}, f32[5,128,1,128]{3,2,1,0:T(1,128)}, u32[]{:S(2)}, u32[]{:S(2)}) collective-permute-start(f32[5,128,1,128]{3,2,1,0:T(1,128)} %get-tuple-element.240), channel_id=1, source_target_pairs={{0,8},{8,16},{16,24},{24,32},{32,40},{40,48},{48,56},{56,64},{64,7... | collective-permute-start | bytes 983048 | tf_op jit(solution)/shard_map/ppermute | solution.py:21
  87.5 43.2 %all-to-all-start.1 = ((f32[128,1,8,128]{3,2,1,0:T(8,128)}), f32[128,1,8,128]{3,2,1,0:T(8,128)}, u32[]{:S(2)}, u32[]{:S(2)}) async-start(f32[128,1,8,128]{3,2,1,0:T(8,128)} %get-tuple-element.347), calls=%async_computation.1 | async-start | bytes 1048576 | tf_op jit(solution)/shard_map/all_to_all | solution.py:128
  121.3 11.9 collective-permute-start.3
  122.6 7.4 copy-start.83
  125.9 10.4 collective-permute-start.2
  150.7 4.1 copy-start.2
  150.7 4.1 copy-start.47
  154.7 4.0 copy-start.12
  154.7 4.0 copy-start.10
  158.7 2.9 copy-start.42
  243.6 7.0 copy-start.20
  243.7 6.0 collective-permute-start.4
  246.3 4.3 collective-permute-start.5
  254.1 6.9 collective-permute-start.7
  257.0 5.5 collective-permute-start.6
  263.9 3.9 copy-start.22
  263.9 3.9 copy-start.48
  263.9 5.7 copy-start.28
  418.2 5.8 collective-permute-start.8
  421.2 3.9 collective-permute-start.9
  428.3 5.7 collective-permute-start.11
  430.0 4.8 collective-permute-start.10
  436.2 3.5 copy-start.23
  436.2 3.5 copy-start.35
  436.2 4.1 copy-start.33
  517.9 136.8 %copy-start.85 = (s32[2]{0:T(128)S(1)}, s32[2]{0:T(128)}, u32[]{:S(2)}) copy-start(s32[2]{0:T(128)} %constant.439.clone.1) | copy-start | bytes 28
  649.2 6.3 collective-permute-start.12
  651.7 4.4 collective-permute-start.13
  659.6 8.0 collective-permute-start.15
  662.5 6.5 collective-permute-start.14
  670.4 3.7 copy-start.24
  670.4 3.7 copy-start.36
  818.6 128.6 %copy-start.46 = (f32[128,8,128]{2,1,0:T(8,128)}, f32[128,8,128]{2,1,0:T(8,128)S(1)}, u32[]{:S(2)}) copy-start(f32[128,8,128]{2,1,0:T(8,128)S(1)} %get-tuple-element.183) | copy-start | bytes 1572868
  949.7 5.6 collective-permute-start.16
  952.7 3.9 collective-permute-start.17
  960.1 18.1 %collective-permute-start.19 = (f32[128,10,1]{0,1,2:T(8,128)S(1)}, f32[128,10,1]{0,1,2:T(8,128)S(1)}, u32[]{:S(2)}, u32[]{:S(2)}) collective-permute-start(f32[128,10,1]{0,1,2:T(8,128)S(1)} %copy.84), channel_id=1, source_target_pairs={{1,0},{2,1},{3,2},{4,3},{5,4},{6,5},{7,6},{9,8},{10,9},{11,10},{12... | collective-permute-start | bytes 15368 | tf_op jit(solution)/shard_map/ppermute | solution.py:23
  963.0 16.7 %collective-permute-start.18 = (f32[128,10,1]{0,1,2:T(8,128)S(1)}, f32[128,10,1]{0,1,2:T(8,128)S(1)}, u32[]{:S(2)}, u32[]{:S(2)}) collective-permute-start(f32[128,10,1]{0,1,2:T(8,128)S(1)} %copy.83), channel_id=1, source_target_pairs={{0,1},{1,2},{2,3},{3,4},{4,5},{5,6},{6,7},{8,9},{9,10},{10,11},{11... | collective-permute-start | bytes 15368 | tf_op jit(solution)/shard_map/ppermute | solution.py:21
  981.1 3.8 copy-start.25
  981.1 3.8 copy-start.37
  981.1 4.4 copy-start.32
  1192.9 161.1 %copy-start.1 = (f32[128,8,128]{2,1,0:T(8,128)S(1)}, f32[128,8,128]{2,1,0:T(8,128)}, u32[]{:S(2)}) copy-start(f32[128,8,128]{2,1,0:T(8,128)} %param.39) | copy-start | bytes 1572868
  (60 other events, 120.8 us)
where the time goes:
time: 1370 us; the launch traced here: 1350 us
  blocking collectives  989 us (72%)
  other arithmetic  151 us (11%)
  local copies, waits for them, and re-layouts  92.8 us (7%)
  starting transfers between devices  89.3 us (7%)
  between operations  28.6 us (2%)
    psum x10, blocking collectives, body(): product_value = lax.psum(jnp.sum(image * basis[k]), ('gx', 'gy'))  667 us
    psum x5, blocking collectives, global_length(): return jnp.sqrt(lax.psum(jnp.sum(field * field), ('gx', 'gy')))  321 us
    unnamed x4, other arithmetic  35.9 us
    ppermute x10, starting transfers between devices, extended(): lax.ppermute(tail, axis, [(i, (i + 1) % count) for i in range(ends)])  34.7 us
  transfers between devices with their start and end apart: 22, of which 5 were waited for; matrix products, arithmetic and copies ran while one was open for 4% of the time, Pallas kernels for 0%

commit v1 on v0

v1 whole, which is shorter than its diff:
```python
import jax
import jax.numpy as jnp
from jax import lax
from jax.experimental import pallas as pl
from jax.experimental.pallas import tpu as pltpu
from jax.sharding import PartitionSpec as P

MATERIALS = 16
STORE = 4.0
AXES = ("gx", "gy")

PIECE = 40
DEPTH = 5
EX = 8 + 2 * DEPTH
EY = 144
PY = 160
CHUNK = 24
CHUNKS = EY // CHUNK
PAIRS = [(i, j) for j in range(1, 5) for i in range(0, j + 1)]


def f32(*shape):
    return jax.ShapeDtypeStruct(shape, jnp.float32)


def params(mib):
    return pltpu.CompilerParams(vmem_limit_bytes=mib << 20)


VMEM = pl.BlockSpec(memory_space=pltpu.VMEM)
SMEM = pl.BlockSpec(memory_space=pltpu.SMEM)


def iota(shape, axis):
    return lax.broadcasted_iota(jnp.int32, shape, axis)


def loop(count, body):
    lax.fori_loop(0, count, lambda i, c: (body(i), c)[1], 0)


def pack_kernel(slot_of, head, old, out, edge):
    sub = iota((8, 128), 0)

    def brick(b):
        own = slot_of[b]
        below = slot_of[jnp.maximum(b - 8, 0)]
        above = slot_of[jnp.minimum(b + 8, 127)]
        head_below, head_above = head[below], head[above]
        old_below, old_above = old[below], old[above]

        def put(tile, value):
            out[pl.ds(pl.multiple_of(b * PIECE + 8 * tile, 8), 8), :] = value

        put(0, head[own])
        put(1, old[own])
        put(2, jnp.where(sub >= 3, head_below, head_above))
        put(3, jnp.where(sub < 3, old_above, jnp.where(sub < 5, head_above, old_below)))
        put(4, jnp.where(sub == 3, old_above, old_below))

    def four(i):
        for k in range(4):
            brick(4 * i + k)

    loop(32, four)
    lane = iota((128, 128), 1)
    edge[0:16, :] = jnp.full((16, 128), -1.0, jnp.float32)
    edge[144:160, :] = jnp.full((16, 128), -1.0, jnp.float32)
    for field, (y_row, corner_row) in enumerate(((32, 34), (33, 37))):
        columns = jnp.zeros((128, 128), jnp.float32)
        for x in range(8):
            rows = out[pl.ds(8 * field + x, 128, stride=PIECE), :]
            low = pltpu.roll(rows, (8 * x + 8) % 128, 1)
            high = pltpu.roll(rows, 64 + 8 * x, 1)
            columns = jnp.where((lane >= 8 * x) & (lane < 8 * x + 8), low, columns)
            columns = jnp.where((lane >= 64 + 8 * x) & (lane < 72 + 8 * x), high, columns)
        edge[16:144, :] = columns
        out[pl.ds(y_row, 128, stride=PIECE), :] = jnp.where(lane < 64, edge[15:143, :], edge[17:145, :])
        out[pl.ds(corner_row, 128, stride=PIECE), :] = jnp.where(
            lane < 64,
            jnp.where(lane < 32, edge[23:151, :], edge[7:135, :]),
            jnp.where(lane < 96, edge[25:153, :], edge[9:137, :]),
        )


def turn_ids_kernel(ids, out):
    for x in range(8):
        out[x] = ids[pl.ds(x, 128, stride=8), :].astype(jnp.float32).T


def properties_kernel(
    place, conductivity, vg_alpha, vg_n, capacity, below, own, above, y_low, y_high,
    alpha, expo, exponent, cap, trans_x, trans_y, trans_z, cond_x, cond_y,
):
    def lookup(ids, rows):
        fields = [jnp.zeros(ids.shape, jnp.float32) for _ in range(6)]
        for m in range(MATERIALS):
            match = ids == float(m)
            values = (
                conductivity[0, m], conductivity[1, m], conductivity[2, m],
                vg_alpha[m], vg_n[m], capacity[m],
            )
            fields = [jnp.where(match, value, field) for value, field in zip(values, fields)]
        return fields

    lane = iota((8, 128), 1)

    def fill(xi, tile, ids):
        rows = pl.ds(8 * tile if isinstance(tile, int) else pl.multiple_of(8 * tile, 8), 8)
        next_rows = pl.ds(8 + 8 * tile if isinstance(tile, int) else pl.multiple_of(8 + 8 * tile, 8), 8)
        kx, ky, kz, a, n, c = lookup(ids, rows)
        alpha[xi, rows, :] = a
        expo[xi, rows, :] = n
        exponent[xi, rows, :] = 1.0 - 1.0 / n
        cap[xi, rows, :] = STORE * c
        cond_x[xi, rows, :] = kx
        cond_y[xi, next_rows, :] = ky
        kz_up = pltpu.roll(kz, 127, 1)
        trans_z[xi, rows, :] = jnp.where(lane < 127, 2.0 * kz * kz_up / (kz + kz_up), 0.0)

    def fill_row(xi, source, x):
        fill(xi, 0, y_low[xi])
        fill(xi, 17, y_high[xi])

        def tiles(t):
            for k in range(2):
                fill(xi, 1 + 2 * t + k, source[x, pl.ds(pl.multiple_of(16 * t + 8 * k, 8), 8), :])

        loop(8, tiles)

    loop(5, lambda x: fill_row(x, below, x))
    loop(8, lambda x: fill_row(x + 5, own, x))
    loop(5, lambda x: fill_row(x + 13, above, x))

    x_first = place[0] * 8 - DEPTH
    y_first = place[1] * 128 - 8
    row = iota((CHUNK, 128), 0)

    def faces(xi):
        x = x_first + xi
        inside = jnp.where((x >= 0) & (x + 1 < place[2] * 8), 1.0, 0.0)
        for c in range(CHUNKS):
            rows = slice(CHUNK * c, CHUNK * (c + 1))
            a, b = cond_x[xi, rows, :], cond_x[jnp.minimum(xi + 1, EX - 1), rows, :]
            trans_x[xi, rows, :] = inside * (2.0 * a * b / (a + b))
            a = cond_y[xi, 8 + CHUNK * c : 8 + CHUNK * (c + 1), :]
            b = cond_y[xi, 9 + CHUNK * c : 9 + CHUNK * (c + 1), :]
            y = y_first + CHUNK * c + row
            trans_y[xi, 8 + CHUNK * c : 8 + CHUNK * (c + 1), :] = jnp.where(
                (y >= 0) & (y + 1 < place[3] * 128), 2.0 * a * b / (a + b), 0.0
            )

    loop(EX, faces)


def wetness(level, alpha, expo, exponent):
    power = jnp.exp(expo * jnp.log(alpha * -level))
    return power, -jnp.log(1.0 + power)


def retention(level, alpha, expo, exponent):
    log_scaled = expo * jnp.log(alpha * -level)
    power = jnp.exp(log_scaled)
    total = 1.0 + power
    inverse = 1.0 / total
    log_inverse = -jnp.log(total)
    root = jnp.exp(0.5 * exponent * log_inverse)
    saturation = root * root
    rest = power * inverse
    z = 1.0 / (1.0 + 2.0 * power)
    zz = z * z
    series = 1.0 / 15.0
    for k in (13.0, 11.0, 9.0, 7.0, 5.0, 3.0, 1.0):
        series = series * zz + 1.0 / k
    log_rest = jnp.where(power >= 1.0, -2.0 * z * series, log_scaled + log_inverse)
    e = exponent * log_rest
    rest_power = jnp.exp(e)
    taylor = 1.0 + e * (1.0 / 8.0)
    for k in (7.0, 6.0, 5.0, 4.0, 3.0, 2.0):
        taylor = 1.0 + (e * (1.0 / k)) * taylor
    inner = jnp.where(e > -0.35, -e * taylor, 1.0 - rest_power)
    relperm = root * inner * inner
    rate = (expo - 1.0) / -level
    d_sat = saturation * rest * rate
    d_rel = root * inner * rate * (0.5 * inner * rest + 2.0 * inverse * rest_power)
    return saturation, relperm, d_sat, d_rel


def split(a, factor):
    c = a * factor
    high = c - (c - a)
    return high, a - high


def two_sum(a, b):
    s = a + b
    t = s - a
    return s, (a - (s - t)) + (b - t)


def df_add(a, b):
    s, e = two_sum(a[0], b[0])
    e = e + (a[1] + b[1])
    t = s + e
    return t, e - (t - s)


def df_mul(a, b):
    ah, al = split(a[0], 4097.0)
    bh, bl = split(b[0], 4097.0)
    p = a[0] * b[0]
    e = ((ah * bh - p) + ah * bl + al * bh) + al * bl
    e = e + (a[0] * b[1] + a[1] * b[0])
    t = p + e
    return t, e - (t - p)


def df_neg(a):
    return -a[0], -a[1]


def df_div(a, b):
    q = a[0] / b[0]
    zero = jnp.zeros_like(q)
    r = df_add(a, df_neg(df_mul((q, zero), b)))
    q2 = r[0] / b[0]
    r = df_add(r, df_neg(df_mul((q2, zero), b)))
    q3 = r[0] / b[0]
    s, e = two_sum(q, q2)
    return two_sum(s, e + q3)


def main_kernel(
    source, recv, alpha, expo, exponent, cap, trans_x, trans_y, trans_z, kept, sums,
    ordered, head, old, rel, d_rel, own_c, cxp, cxm, cyp, cym, czp, czm, k0, k1, k2, k3, k4,
):
    sub = iota((8, 128), 0)
    lane = iota((8, 128), 1)

    def layer(z):
        def tile(k, t):
            return recv[pl.ds(pl.multiple_of(source[k, z] * PIECE + 8 * t, 8), 8), :]

        def put(t, value):
            ordered[pl.ds(pl.multiple_of(z * PIECE + 8 * t, 8), 8), :] = value

        put(0, tile(0, 0))
        put(1, tile(0, 1))
        put(2, jnp.where(sub >= 3, tile(1, 2), tile(2, 2)))
        put(3, jnp.where(sub < 5, tile(2, 3), tile(1, 3)))
        sides = jnp.where(lane < 64, tile(3, 4), tile(4, 4))
        corners = jnp.where(
            lane < 64,
            jnp.where(lane < 32, tile(5, 4), tile(6, 4)),
            jnp.where(lane < 96, tile(7, 4), tile(8, 4)),
        )
        put(
            4,
            jnp.where(
                sub < 2, sides, jnp.where(sub == 3, tile(2, 4), jnp.where(sub == 4, tile(1, 4), corners))
            ),
        )

    def two_layers(i):
        layer(2 * i)
        layer(2 * i + 1)

    loop(64, two_layers)

    def plane(r):
        return ordered[pl.ds(r, 128, stride=PIECE), :].T

    for xi, r in enumerate([19, 20, 21, 22, 23] + list(range(8)) + [16, 17, 18, 27, 28]):
        head[xi, 16:144, :] = plane(r)
    for xi, r in enumerate([36, 29, 30, 31] + list(range(8, 16)) + [24, 25, 26, 35]):
        old[xi + 1, 16:144, :] = plane(r)
    for field, (y_row, corner_row) in ((head, (32, 34)), (old, (33, 37))):
        sides = plane(y_row)
        for x in range(8):
            field[5 + x, 8:16, :] = sides[8 * x : 8 * x + 8]
            field[5 + x, 144:152, :] = sides[64 + 8 * x : 72 + 8 * x]
        corners = plane(corner_row)
        for k in range(4):
            field[13 + k, 8:16, :] = corners[8 * k : 8 * k + 8]
            field[1 + k, 8:16, :] = corners[32 + 8 * k : 40 + 8 * k]
            field[13 + k, 144:152, :] = corners[64 + 8 * k : 72 + 8 * k]
            field[1 + k, 144:152, :] = corners[96 + 8 * k : 104 + 8 * k]
    for xi in (0, 17):
        head[xi, 8:16, :] = jnp.full((8, 128), -1.0, jnp.float32)
        head[xi, 144:152, :] = jnp.full((8, 128), -1.0, jnp.float32)

    def curves(xi):
        for c in range(CHUNKS):
            at = slice(CHUNK * c, CHUNK * (c + 1))
            to = slice(8 + CHUNK * c, 8 + CHUNK * (c + 1))
            sat_v, rel_v, dsat_v, drel_v = retention(
                head[xi, to, :], alpha[xi, at, :], expo[xi, at, :], exponent[xi, at, :]
            )
            k0[xi, to, :] = sat_v
            rel[xi, to, :] = rel_v
            d_rel[xi, to, :] = drel_v
            own_c[xi, to, :] = cap[xi, at, :] * dsat_v

    loop(EX, curves)

    def face(t, h_a, h_b, r_a, r_b, d_a, d_b, rise):
        potential = h_b - h_a
        if rise:
            potential = potential + rise
        along = t * (0.5 * (r_a + r_b))
        slope = (0.5 * t) * potential
        return along, slope, along * potential, slope * (d_a + d_b)

    def coefficients(i):
        xi = i + 1
        for c in range(CHUNKS):
            at = slice(CHUNK * c, CHUNK * (c + 1))
            to = slice(8 + CHUNK * c, 8 + CHUNK * (c + 1))
            up = slice(9 + CHUNK * c, 9 + CHUNK * (c + 1))
            down = slice(7 + CHUNK * c, 7 + CHUNK * (c + 1))
            _, log_old = wetness(old[xi, to, :], alpha[xi, at, :], expo[xi, at, :], exponent[xi, at, :])
            old_sat = jnp.exp(exponent[xi, at, :] * log_old)
            start = cap[xi, at, :] * (old_sat - k0[xi, to, :])
            h, r, d = head[xi, to, :], rel[xi, to, :], d_rel[xi, to, :]
            centre = own_c[xi, to, :]
            around = (
                (
                    trans_x[xi, at, :], trans_x[xi - 1, at, :], 0.0, cxp, cxm,
                    [f[xi + 1, to, :] for f in (head, rel, d_rel)],
                    [f[xi - 1, to, :] for f in (head, rel, d_rel)],
                ),
                (
                    trans_y[xi, to, :], trans_y[xi, down, :], 0.0, cyp, cym,
                    [f[xi, up, :] for f in (head, rel, d_rel)],
                    [f[xi, down, :] for f in (head, rel, d_rel)],
                ),
                (
                    trans_z[xi, at, :], pltpu.roll(trans_z[xi, at, :], 1, 1), 1.0, czp, czm,
                    [pltpu.roll(f, 127, 1) for f in (h, r, d)],
                    [pltpu.roll(f, 1, 1) for f in (h, r, d)],
                ),
            )
            for t_p, t_m, rise, c_p, c_m, (h_p, r_p, d_p), (h_m, r_m, d_m) in around:
                along, slope, flux, both = face(t_p, h, h_p, r, r_p, d, d_p, rise)
                along_m, slope_m, flux_m, both_m = face(t_m, h_m, h, r_m, r, d_m, d, rise)
                c_p[xi, to, :] = along + slope * d_p
                c_m[xi, to, :] = along_m - slope_m * d_m
                start = start + (flux - flux_m)
                centre = centre - (both - both_m)
            own_c[xi, to, :] = centre
            k0[xi, to, :] = start

    loop(16, coefficients)

    vectors = (k0, k1, k2, k3, k4)
    for step in range(4):
        v_ref, w_ref = vectors[step], vectors[step + 1]

        def apply(i):
            xi = i + 2 + step
            for c in range(CHUNKS):
                to = slice(8 + CHUNK * c, 8 + CHUNK * (c + 1))
                up = slice(9 + CHUNK * c, 9 + CHUNK * (c + 1))
                down = slice(7 + CHUNK * c, 7 + CHUNK * (c + 1))
                v = v_ref[xi, to, :]
                w = own_c[xi, to, :] * v
                w = w + cxp[xi, to, :] * (v - v_ref[xi + 1, to, :])
                w = w + cxm[xi, to, :] * (v - v_ref[xi - 1, to, :])
                w = w + cyp[xi, to, :] * (v - v_ref[xi, up, :])
                w = w + cym[xi, to, :] * (v - v_ref[xi, down, :])
                w = w + czp[xi, to, :] * (v - pltpu.roll(v, 127, 1))
                w = w + czm[xi, to, :] * (v - pltpu.roll(v, 1, 1))
                w_ref[xi, to, :] = w

        loop(14 - 2 * step, apply)

    def largest(i, tops):
        xi = 5 + i
        for c in range(16):
            at = slice(16 + 8 * c, 24 + 8 * c)
            tops = [jnp.maximum(top, jnp.abs(v[xi, at, :])) for top, v in zip(tops, vectors)]
        return tops

    tops = lax.fori_loop(0, 8, largest, [jnp.zeros((8, 128), jnp.float32) for _ in range(5)])
    scales, inverses = [], []
    for top in tops:
        top = jnp.broadcast_to(jnp.max(top, keepdims=True), (8, 128))
        scale = jnp.full((8, 128), 2.0**96, jnp.float32)
        inverse = jnp.full((8, 128), 2.0**-96, jnp.float32)
        for j in range(-5, 7):
            over = top >= 2.0 ** (16 * j - 8)
            scale = jnp.where(over, 2.0 ** (-16 * j), scale)
            inverse = jnp.where(over, 2.0 ** (16 * j), inverse)
        scales.append(scale)
        inverses.append(inverse)

    def products(i, totals):
        leading, rest = totals
        xi = 5 + i // 8
        first = 16 + 16 * (i % 8)
        for k in range(2):
            at = pl.ds(pl.multiple_of(first + 8 * k, 8), 8)
            values = [v[xi, at, :] * scale for v, scale in zip(vectors, scales)]
            halves = [split(value, 65537.0) for value in values]
            leading, rest = list(leading), list(rest)
            for e, (p, q) in enumerate(PAIRS):
                leading[e] = leading[e] + halves[p][0] * halves[q][0]
                rest[e] = rest[e] + (halves[p][0] * halves[q][1] + halves[p][1] * values[q])
        return leading, rest

    zeros = [jnp.zeros((8, 128), jnp.float32) for _ in PAIRS]
    leading, rest = lax.fori_loop(0, 64, products, (zeros, list(zeros)))
    groups = []
    for g in range(2):
        high = jnp.zeros((8, 128), jnp.float32)
        low = jnp.zeros((8, 128), jnp.float32)
        for e in range(8 * g, min(8 * g + 8, len(PAIRS))):
            pair = two_sum(leading[e], rest[e])
            for shift in (4, 2, 1):
                pair = df_add(pair, (pltpu.roll(pair[0], shift, 0), pltpu.roll(pair[1], shift, 0)))
            high = jnp.where(sub == e - 8 * g, pair[0], high)
            low = jnp.where(sub == e - 8 * g, pair[1], low)
        pair = (high, low)
        for shift in (64, 32, 16, 8, 4, 2, 1):
            pair = df_add(pair, (pltpu.roll(pair[0], shift, 1), pltpu.roll(pair[1], shift, 1)))
        groups.append(pair)
    line = jnp.zeros((8, 128), jnp.float32)
    for e in range(len(PAIRS)):
        pair = groups[e // 8]
        for half in range(2):
            line = jnp.where(lane == 16 * half + e, pair[half][e % 8 : e % 8 + 1, :], line)
    for k in range(5):
        line = jnp.where(lane == 32 + k, inverses[k], line)
        line = jnp.where(lane == 40 + k, scales[k], line)
    for t in range(16):
        sums[8 * t : 8 * t + 8, :] = line

    def keep(x):
        for k in range(4):
            kept[k, x] = vectors[k][x + 5, 16:144, :]

    loop(8, keep)


def turn_back_kernel(kept, out):
    for k in range(4):
        for x in range(8):
            out[k, pl.ds(x, 128, stride=8), :] = kept[k, x].T


def finish_kernel(recv, vectors, out):
    data = recv[...]
    lane = iota((128, 128), 1)
    smallest = jnp.min(data, axis=0, keepdims=True)
    factor = data * jnp.broadcast_to(pltpu.roll(jnp.broadcast_to(smallest, (8, 128)), 120, 1)[0:1], (128, 128))
    left = jnp.zeros((128, 128), jnp.float32)
    right = jnp.zeros((128, 128), jnp.float32)
    for k in range(5):
        column = jnp.broadcast_to(factor[:, 32 + k : 33 + k], (128, 128))
        for e, (p, q) in enumerate(PAIRS):
            if p == k:
                left = jnp.where(lane % 16 == e, column, left)
            if q == k:
                right = jnp.where(lane % 16 == e, column, right)
    scaled = data * left * right
    low = pltpu.roll(scaled, 112, 1)
    pair = (scaled[0:8], low[0:8])
    for t in range(1, 16):
        pair = df_add(pair, (scaled[8 * t : 8 * t + 8], low[8 * t : 8 * t + 8]))
    for shift in (4, 2, 1):
        pair = df_add(pair, (pltpu.roll(pair[0], shift, 0), pltpu.roll(pair[1], shift, 0)))
    entry = {}
    for e, (p, q) in enumerate(PAIRS):
        entry[p, q] = tuple(jnp.broadcast_to(half[:, e : e + 1], (8, 128)) for half in pair)

    def scale_of(k):
        return jnp.broadcast_to(smallest[:, k : k + 1], (8, 128))

    rows = {(i, j): entry[i + 1, j + 1] for i in range(4) for j in range(i, 4)}
    right_side = [entry[0, j + 1] for j in range(4)]
    for k in range(4):
        for i in range(k + 1, 4):
            ratio = df_neg(df_div(rows[k, i], rows[k, k]))
            for j in range(i, 4):
                rows[i, j] = df_add(rows[i, j], df_mul(ratio, rows[k, j]))
            right_side[i] = df_add(right_side[i], df_mul(ratio, right_side[k]))
    coeffs = [None] * 4
    for k in reversed(range(4)):
        running = right_side[k]
        for j in range(k + 1, 4):
            running = df_add(running, df_neg(df_mul(rows[k, j], coeffs[j])))
        coeffs[k] = df_div(running, rows[k, k])
    inverse_first = jnp.max(jnp.where(lane == 32, data, 0.0), axis=0, keepdims=True)
    inverse_first = jnp.broadcast_to(jnp.max(inverse_first, axis=1, keepdims=True), (8, 128))
    weights = [(coeffs[k][0] * scale_of(41 + k)) * inverse_first for k in range(4)]

    def rows_of(t):
        for k in range(4):
            at = pl.ds(pl.multiple_of(32 * t + 8 * k, 8), 8)
            total = weights[0] * vectors[0, at, :]
            for j in range(1, 4):
                total = total + weights[j] * vectors[j, at, :]
            out[at, :] = total

    loop(32, rows_of)


def call(kernel, out_shape, in_specs, out_specs, scratch, mib, cost):
    return pl.pallas_call(
        kernel,
        out_shape=out_shape,
        in_specs=in_specs,
        out_specs=out_specs,
        scratch_shapes=scratch,
        compiler_params=params(mib),
        cost_estimate=pl.CostEstimate(flops=cost[0], bytes_accessed=cost[1], transcendentals=0),
    )


def body(held_head, held_head_old, material_ids, block_map, conductivity, vg_alpha, vg_n, capacity):
    count_x, count_y = lax.axis_size("gx"), lax.axis_size("gy")
    devices = count_x * count_y
    at_x, at_y = lax.axis_index("gx"), lax.axis_index("gy")
    own_index = at_x * count_y + at_y
    numbers = jnp.arange(devices, dtype=jnp.int32)
    own_row = block_map[own_index]
    slot_of = jnp.sum(jnp.where(own_row[None, :] == numbers[:, None], numbers[None, :], 0), axis=1)
    scratch = lambda *shape: pltpu.VMEM(shape, jnp.float32)

    packed = call(
        pack_kernel, f32(devices * PIECE, 128), [SMEM, VMEM, VMEM], VMEM, [scratch(PY, 128)], 16, (10**6, 4 * 10**6)
    )(slot_of, held_head, held_head_old)
    arrived = lax.all_to_all(packed, AXES, split_axis=0, concat_axis=0, tiled=True)

    offsets = (0, -count_y, count_y, -1, 1, count_y - 1, -count_y - 1, count_y + 1, -count_y + 1)
    bricks = own_index + jnp.array(offsets, jnp.int32)
    source = jnp.sum(
        jnp.where(block_map[None] == bricks[:, None, None], numbers[None, :, None], 0), axis=1
    )

    ids = call(
        turn_ids_kernel, f32(8, 128, 128), [VMEM], VMEM, [], 8, (10**6, 10**6)
    )(material_ids.reshape(1024, 128))
    up_x = [(i, i + 1) for i in range(count_x - 1)]
    down_x = [(i + 1, i) for i in range(count_x - 1)]
    up_y = [(i, i + 1) for i in range(count_y - 1)]
    down_y = [(i + 1, i) for i in range(count_y - 1)]
    below = lax.ppermute(ids[8 - DEPTH :], "gx", up_x)
    above = lax.ppermute(ids[:DEPTH], "gx", down_x)
    last = jnp.concatenate([part[:, 120:] for part in (below, ids, above)], axis=0)
    first = jnp.concatenate([part[:, :8] for part in (below, ids, above)], axis=0)
    y_low = lax.ppermute(last, "gy", up_y)
    y_high = lax.ppermute(first, "gy", down_y)
    place = jnp.stack([at_x, at_y, jnp.int32(count_x), jnp.int32(count_y)])
    fields = call(
        properties_kernel,
        [f32(EX, EY, 128)] * 5 + [f32(EX, PY, 128), f32(EX, EY, 128)],
        [SMEM] * 5 + [VMEM] * 5,
        [VMEM] * 7,
        [scratch(EX, EY, 128), scratch(EX, PY, 128)],
        24,
        (40 * 10**6, 12 * 10**6),
    )(place, conductivity, vg_alpha, vg_n, capacity, below, ids, above, y_low, y_high)

    kept, sums = call(
        main_kernel,
        [f32(4, 8, 128, 128), f32(devices, 128)],
        [SMEM] + [VMEM] * 8,
        [VMEM] * 2,
        [scratch(devices * PIECE, 128)] + [scratch(EX, PY, 128)] * 16,
        56,
        (200 * 10**6, 16 * 10**6),
    )(source, arrived, *fields)
    gathered = lax.all_to_all(sums.reshape(devices, 1, 128), AXES, split_axis=0, concat_axis=0, tiled=True)
    turned = call(turn_back_kernel, f32(4, 1024, 128), [VMEM], VMEM, [], 8, (10**6, 4 * 10**6))(kept)
    update = call(finish_kernel, f32(1024, 128), [VMEM] * 2, VMEM, [], 16, (10**6, 3 * 10**6))(
        gathered.reshape(devices, 128), turned
    )
    return update.reshape(128, 8, 128)


def solution(mesh):
    return jax.shard_map(
        body,
        mesh=mesh,
        in_specs=(
            P(("gx", "gy"), None, None),
            P(("gx", "gy"), None, None),
            P(None, "gx", "gy"),
            P(),
            P(),
            P(),
            P(),
            P(),
        ),
        out_specs=P(None, "gx", "gy"),
        check_vma=False,
    )
```

time: 1370 us -> 135 us (0.10); the launches traced: 1350 us -> 135 us
  blocking collectives: 989 us -> 0 us
  other arithmetic: 151 us -> 0.94 us
  local copies, waits for them, and re-layouts: 92.8 us -> 13.6 us
  starting transfers between devices: 89.3 us -> 33.1 us
  Pallas kernels: 0 us -> 48.7 us
  waiting for transfers between devices: 4.17 us -> 37.9 us
  between operations: 28.6 us -> 0.24 us
    psum x15 -> x0, blocking collectives: 989 us -> none  [the longest x10 667 us: body(): product_value = lax.psum(jnp.sum(image * basis[k]), ('gx', 'gy'))]
    pallas_call x0 -> x6, Pallas kernels: none -> 48.7 us  [the longest x1 26.1 us: body(): call(main_kernel, [f32(4, 8, 128, 128), f32(devices, 128)], [SMEM] + [VME...]
    ppermute x20 -> x4, starting transfers between devices: 55.1 us -> 10.1 us  [the longest x1 3.23 us: body(): y_low = lax.ppermute(last, 'gy', up_y)]
    slice x34 -> x4, local copies, waits for them, and re-layouts: 41.7 us -> 0.07 us  [the longest x1 0.05 us: body(): above = lax.ppermute(ids[:DEPTH], 'gx', down_x)]
    unnamed x4 -> x0, other arithmetic: 35.9 us -> none
    reduce_sum x16 -> x1, other arithmetic: 35.9 us -> 0.74 us  [body(): jnp.sum(jnp.where(block_map[None] == bricks[:, None, None], numbers[None,...]
    ppermute x20 -> x4, waiting for transfers between devices: 4.17 us -> 30.6 us  [the longest x1 26.9 us: body(): above = lax.ppermute(ids[:DEPTH], 'gx', down_x)]
    mul x7 -> x0, other arithmetic: 21.5 us -> none  [the longest x4 14.8 us: body(): pad_weighted = pad_drel * pad_field]
  transfers between devices with their start and end apart: 22 -> 6, of which waited for: 5 -> 3; matrix products, arithmetic and copies ran while one was open for 4% -> 1% of each run, Pallas kernels for 0% -> 13%
where the time goes in v1:
time: 135 us
  Pallas kernels  48.7 us (36%)
  waiting for transfers between devices  37.9 us (28%)
  starting transfers between devices  33.1 us (25%)
  local copies, waits for them, and re-layouts  13.6 us (10%)
    ppermute x1, waiting for transfers between devices, body(): above = lax.ppermute(ids[:DEPTH], 'gx', down_x)  26.9 us
    pallas_call x1, Pallas kernels, body(): call(main_kernel, [f32(4, 8, 128, 128), f32(devices, 128)], [SMEM] + [VME...  26.1 us
    pallas_call x1, Pallas kernels, body(): call(properties_kernel, [f32(EX, EY, 128)] * 5 + [f32(EX, PY, 128), f32(E...  16.2 us
    unnamed x36, local copies, waits for them, and re-layouts  12.9 us
    all_to_all x1, starting transfers between devices, body(): lax.all_to_all(sums.reshape(devices, 1, 128), AXES, split_axis=0, concat_...  11.5 us
    all_to_all x1, starting transfers between devices, body(): lax.all_to_all(packed, AXES, split_axis=0, concat_axis=0, tiled=True)  11.5 us
    all_to_all x1, waiting for transfers between devices, body(): lax.all_to_all(sums.reshape(devices, 1, 128), AXES, split_axis=0, concat_...  7.32 us
    ppermute x1, waiting for transfers between devices, body(): y_high = lax.ppermute(first, 'gy', down_y)  3.71 us
  transfers between devices with their start and end apart: 6, of which 3 were waited for; matrix products, arithmetic and copies ran while one was open for 1% of the time, Pallas kernels for 13%

profile of v1, /device:TPU:1, one launch (start us, length us, event | category | flops | bytes accessed | tf_op | source)
XLA Modules:
  0.0 134.6 jit_solution(6048358645385054757)
XLA Ops:
  0.0 0.7 dynamic-slice_bitcast_fusion
  0.7 0.1 select_reduce_fusion.1.slot_of
  0.8 0.0 copy-start.9
  0.8 1.0 copy-done.9
  1.9 1.0 copy-done.10
  2.9 3.5 %shard_map.91 = f32[5120,128]{1,0:T(8,128)} custom-call(s32[128]{0:T(128)S(1)} %select_reduce_fusion.1.slot_of, f32[128,8,128]{2,1,0:T(8,128)S(1)} %copy-done.9, f32[128,8,128]{2,1,0:T(8,128)S(1)} %copy-done.10), custom_call_target="tpu_custom_call" | custom-call | flops 1000000 | bytes 4000000 | tf_op jit(solution)/shard_map/pallas_call | solution.py:530
  6.4 11.5 %all-to-all-start = ((f32[128,40,128]{2,1,0:T(8,128)}), f32[128,40,128]{2,1,0:T(8,128)S(1)}, u32[]{:S(2)}, u32[]{:S(2)}) async-start(f32[128,40,128]{2,1,0:T(8,128)} %bitcast.1), calls=%async_computation | async-start | bytes 5242880 | tf_op jit(solution)/shard_map/all_to_all | solution.py:533
  18.0 0.0 copy-start.17
  18.0 0.0 copy-start.16
  18.0 0.0 copy-done.8
  18.0 0.0 copy-start.11
  18.0 0.0 copy-start.12
  18.0 0.0 copy-start.13
  18.0 0.0 copy-start.14
  18.0 0.2 shard_map.92.own
  18.2 0.1 fusion.1
  18.3 3.0 %collective-permute-start.1 = (f32[5,128,128]{2,1,0:T(8,128)S(1)}, f32[5,128,128]{2,1,0:T(8,128)S(1)}, u32[]{:S(2)}, u32[]{:S(2)}) collective-permute-start(f32[5,128,128]{2,1,0:T(8,128)S(1)} %get-tuple-element.25), channel_id=1, source_target_pairs={{8,0},{16,8},{24,16},{32,24},{40,32},{48,40},{56,48},{64,56},{72,6... | collective-permute-start | bytes 983048 | tf_op jit(solution)/shard_map/ppermute | solution.py:549
  21.3 2.6 %collective-permute-start = (f32[5,128,128]{2,1,0:T(8,128)S(1)}, f32[5,128,128]{2,1,0:T(8,128)S(1)}, u32[]{:S(2)}, u32[]{:S(2)}) collective-permute-start(f32[5,128,128]{2,1,0:T(8,128)S(1)} %get-tuple-element.26), channel_id=1, source_target_pairs={{0,8},{8,16},{16,24},{24,32},{32,40},{40,48},{48,56},{56,64},{64,7... | collective-permute-start | bytes 983048 | tf_op jit(solution)/shard_map/ppermute | solution.py:548
  23.9 0.0 copy-done.17
  23.9 0.0 copy-done.16
  23.9 0.7 select_reduce_fusion.source
  24.7 26.9 %collective-permute-done.1.above = f32[5,128,128]{2,1,0:T(8,128)S(1)} collective-permute-done((f32[5,128,128]{2,1,0:T(8,128)S(1)}, f32[5,128,128]{2,1,0:T(8,128)S(1)}, u32[]{:S(2)}, u32[]{:S(2)}) %collective-permute-start.1) | collective-permute-done | bytes 327712 | tf_op jit(solution)/shard_map/ppermute | solution.py:549
  51.5 0.0 collective-permute-done.below
  51.6 3.2 %collective-permute-start.2 = (f32[18,8,128]{2,1,0:T(8,128)S(1)}, f32[18,8,128]{2,1,0:T(8,128)S(1)}, u32[]{:S(2)}, u32[]{:S(2)}) collective-permute-start(f32[18,8,128]{2,1,0:T(8,128)S(1)} %pad_maximum_fusion), channel_id=1, source_target_pairs={{0,1},{1,2},{2,3},{3,4},{4,5},{5,6},{6,7},{8,9},{9,10},{10,11},{11... | collective-permute-start | bytes 221192 | tf_op jit(solution)/shard_map/ppermute | solution.py:552
  54.8 1.3 collective-permute-start.3
  56.1 0.1 pad_add_fusion.place
  56.2 0.0 collective-permute-done.2.y_low
  56.2 3.7 %collective-permute-done.3.y_high = f32[18,8,128]{2,1,0:T(8,128)S(1)} collective-permute-done((f32[18,8,128]{2,1,0:T(8,128)S(1)}, f32[18,8,128]{2,1,0:T(8,128)S(1)}, u32[]{:S(2)}, u32[]{:S(2)}) %collective-permute-start.3) | collective-permute-done | bytes 73760 | tf_op jit(solution)/shard_map/ppermute | solution.py:553
  59.9 0.0 copy-done.11
  59.9 0.0 copy-done.12
  59.9 0.0 copy-done.13
  59.9 0.0 copy-done.14
  59.9 16.2 %shard_map.93 = (f32[18,144,128]{2,1,0:T(8,128)S(1)}, f32[18,144,128]{2,1,0:T(8,128)S(1)}, f32[18,144,128]{2,1,0:T(8,128)S(1)}, f32[18,144,128]{2,1,0:T(8,128)S(...) custom-call(s32[4]{0:T(128)S(1)} %pad_add_fusion.place, ...), custom_call_target="tpu_custom_call" | custom-call | flops 40000000 | bytes 12000000 | tf_op jit(solution)/shard_map/pallas_call | solution.py:555
  76.2 1.2 copy-done.1
  77.3 1.1 copy-done.2
  78.4 1.1 copy-done.3
  79.6 1.0 copy-done.4
  80.6 1.1 copy-done.5
  81.7 1.1 copy-done.6
  82.8 1.1 copy-done.7
  83.8 0.0 all-to-all-done
  83.9 1.5 %copy-done.15 = f32[128,40,128]{2,1,0:T(8,128)} copy-done((f32[128,40,128]{2,1,0:T(8,128)}, f32[128,40,128]{2,1,0:T(8,128)S(1)}, u32[]{:S(2)}) %copy-start.15) | copy-done | bytes 2621464
  85.3 26.1 %shard_map.94 = (f32[4,8,128,128]{3,2,1,0:T(8,128)}, f32[128,128]{1,0:T(8,128)}) custom-call(s32[9,128]{1,0:T(8,128)} %select_reduce_fusion.source, f32[5120,128]{1,0:T(8,128)} %bitcast.14, f32[18,144,128]{2,1,0:T(8,128)} %copy-done.2, f32[18,144,128]{2,1,0:T(8,128)} %copy-done.3, f32[18,144,128]{2,1,0:T(8,128)} %copy-done.4, f32[18,144,128]{2,1,0:T(8,128)} %copy-done.5, ...), custom_call_target="tpu_custom_call" | custom-call | flops 200000000 | bytes 16000000 | tf_op jit(solution)/shard_map/pallas_call | solution.py:565
  111.4 11.5 %all-to-all-start.1 = ((f32[128,1,128]{2,1,0:T(1,128)}), f32[128,1,128]{2,1,0:T(1,128)S(1)}, u32[]{:S(2)}, u32[]{:S(2)}) async-start(f32[128,1,128]{2,1,0:T(1,128)} %bitcast.15), calls=%async_computation.1 | async-start | bytes 131072 | tf_op jit(solution)/shard_map/all_to_all | solution.py:574
  123.0 1.6 %copy-done = f32[4,8,128,128]{3,2,1,0:T(8,128)S(1)} copy-done((f32[4,8,128,128]{3,2,1,0:T(8,128)S(1)}, f32[4,8,128,128]{3,2,1,0:T(8,128)}, u32[]{:S(2)}) %copy-start) | copy-done | bytes 2097176
  124.6 0.6 shard_map.95.vectors
  125.2 7.3 %all-to-all-done.1 = f32[128,1,128]{2,1,0:T(1,128)S(1)} async-done(((f32[128,1,128]{2,1,0:T(1,128)}), f32[128,1,128]{2,1,0:T(1,128)S(1)}, u32[]{:S(2)}, u32[]{:S(2)}) %all-to-all-start.1) | async-done | bytes 65568 | tf_op jit(solution)/shard_map/all_to_all | solution.py:574
  132.5 2.1 %shard_map.96 = f32[1024,128]{1,0:T(8,128)} custom-call(f32[128,128]{1,0:T(8,128)S(1)} %bitcast.13, f32[4,1024,128]{2,1,0:T(8,128)S(1)} %shard_map.95.vectors), custom_call_target="tpu_custom_call" | custom-call | flops 1000000 | bytes 3000000 | tf_op jit(solution)/shard_map/pallas_call | solution.py:576
  (17 shorter events, 0.1 us)
Async XLA Ops:
  0.8 1.1 copy-start.9
  1.9 1.0 copy-start.10
  6.4 11.5 %copy-start.8 = (s32[128,8,128]{2,1,0:T(8,128)S(1)}, s32[128,8,128]{2,1,0:T(8,128)}, u32[]{:S(2)}) copy-start(s32[128,8,128]{2,1,0:T(8,128)} %param.11) | copy-start | bytes 1572868
  6.4 77.4 %all-to-all-start = ((f32[128,40,128]{2,1,0:T(8,128)}), f32[128,40,128]{2,1,0:T(8,128)S(1)}, u32[]{:S(2)}, u32[]{:S(2)}) async-start(f32[128,40,128]{2,1,0:T(8,128)} %bitcast.1), calls=%async_computation | async-start | bytes 5242880 | tf_op jit(solution)/shard_map/all_to_all | solution.py:533
  18.0 5.9 %copy-start.17 = (s32[9]{0:T(128)S(1)}, s32[9]{0:T(128)}, u32[]{:S(2)}) copy-start(s32[9]{0:T(128)} %constant.21.clone) | copy-start | bytes 112
  18.0 5.9 %copy-start.16 = (s32[128,128]{1,0:T(8,128)S(1)}, s32[128,128]{1,0:T(8,128)}, u32[]{:S(2)}) copy-start(s32[128,128]{1,0:T(8,128)} %param.12) | copy-start | bytes 196612
  18.0 41.9 %copy-start.11 = (f32[3,16]{1,0:T(4,128)S(1)}, f32[3,16]{1,0:T(4,128)}, u32[]{:S(2)}) copy-start(f32[3,16]{1,0:T(4,128)} %conductivity.1) | copy-start | bytes 580
  18.0 41.9 %copy-start.12 = (f32[16]{0:T(128)S(1)}, f32[16]{0:T(128)}, u32[]{:S(2)}) copy-start(f32[16]{0:T(128)} %vg_alpha.1) | copy-start | bytes 196
  18.0 41.9 %copy-start.13 = (f32[16]{0:T(128)S(1)}, f32[16]{0:T(128)}, u32[]{:S(2)}) copy-start(f32[16]{0:T(128)} %vg_n.1) | copy-start | bytes 196
  18.0 41.9 %copy-start.14 = (f32[16]{0:T(128)S(1)}, f32[16]{0:T(128)}, u32[]{:S(2)}) copy-start(f32[16]{0:T(128)} %capacity.1) | copy-start | bytes 196
  18.3 33.2 %collective-permute-start.1 = (f32[5,128,128]{2,1,0:T(8,128)S(1)}, f32[5,128,128]{2,1,0:T(8,128)S(1)}, u32[]{:S(2)}, u32[]{:S(2)}) collective-permute-start(f32[5,128,128]{2,1,0:T(8,128)S(1)} %get-tuple-element.25), channel_id=1, source_target_pairs={{8,0},{16,8},{24,16},{32,24},{40,32},{48,40},{56,48},{64,56},{72,6... | collective-permute-start | bytes 983048 | tf_op jit(solution)/shard_map/ppermute | solution.py:549
  21.3 30.2 %collective-permute-start = (f32[5,128,128]{2,1,0:T(8,128)S(1)}, f32[5,128,128]{2,1,0:T(8,128)S(1)}, u32[]{:S(2)}, u32[]{:S(2)}) collective-permute-start(f32[5,128,128]{2,1,0:T(8,128)S(1)} %get-tuple-element.26), channel_id=1, source_target_pairs={{0,8},{8,16},{16,24},{24,32},{32,40},{40,48},{48,56},{56,64},{64,7... | collective-permute-start | bytes 983048 | tf_op jit(solution)/shard_map/ppermute | solution.py:548
  51.6 4.6 %collective-permute-start.2 = (f32[18,8,128]{2,1,0:T(8,128)S(1)}, f32[18,8,128]{2,1,0:T(8,128)S(1)}, u32[]{:S(2)}, u32[]{:S(2)}) collective-permute-start(f32[18,8,128]{2,1,0:T(8,128)S(1)} %pad_maximum_fusion), channel_id=1, source_target_pairs={{0,1},{1,2},{2,3},{3,4},{4,5},{5,6},{6,7},{8,9},{9,10},{10,11},{11... | collective-permute-start | bytes 221192 | tf_op jit(solution)/shard_map/ppermute | solution.py:552
  54.8 5.1 %collective-permute-start.3 = (f32[18,8,128]{2,1,0:T(8,128)S(1)}, f32[18,8,128]{2,1,0:T(8,128)S(1)}, u32[]{:S(2)}, u32[]{:S(2)}) collective-permute-start(f32[18,8,128]{2,1,0:T(8,128)S(1)} %pad_maximum_fusion.1), channel_id=1, source_target_pairs={{1,0},{2,1},{3,2},{4,3},{5,4},{6,5},{7,6},{9,8},{10,9},{11,10},{12... | collective-permute-start | bytes 221192 | tf_op jit(solution)/shard_map/ppermute | solution.py:553
  76.2 1.2 copy-start.1
  77.3 1.1 copy-start.2
  78.4 1.2 copy-start.3
  79.6 1.0 copy-start.4
  80.6 1.1 copy-start.5
  81.7 1.1 copy-start.6
  82.8 1.1 copy-start.7
  83.9 1.5 %copy-start.15 = (f32[128,40,128]{2,1,0:T(8,128)}, f32[128,40,128]{2,1,0:T(8,128)S(1)}, u32[]{:S(2)}) copy-start(f32[128,40,128]{2,1,0:T(8,128)S(1)} %all-to-all-done) | copy-start | bytes 7864324
  111.4 21.1 %all-to-all-start.1 = ((f32[128,1,128]{2,1,0:T(1,128)}), f32[128,1,128]{2,1,0:T(1,128)S(1)}, u32[]{:S(2)}, u32[]{:S(2)}) async-start(f32[128,1,128]{2,1,0:T(1,128)} %bitcast.15), calls=%async_computation.1 | async-start | bytes 131072 | tf_op jit(solution)/shard_map/all_to_all | solution.py:574
  123.0 1.6 %copy-start = (f32[4,8,128,128]{3,2,1,0:T(8,128)S(1)}, f32[4,8,128,128]{3,2,1,0:T(8,128)}, u32[]{:S(2)}) copy-start(f32[4,8,128,128]{3,2,1,0:T(8,128)} %get-tuple-element.22.kept) | copy-start | bytes 6291460

commit v2 on v1

--- a/solution.py
+++ b/solution.py
@@ -29,6 +29,7 @@
 
 VMEM = pl.BlockSpec(memory_space=pltpu.VMEM)
 SMEM = pl.BlockSpec(memory_space=pltpu.SMEM)
+HBM = pl.BlockSpec(memory_space=pltpu.HBM)
 
 
 def iota(shape, axis):
@@ -39,7 +40,7 @@
     lax.fori_loop(0, count, lambda i, c: (body(i), c)[1], 0)
 
 
-def pack_kernel(slot_of, head, old, out, edge):
+def pack_kernel(slot_of, head, old, packed, out, edge, sem):
     sub = iota((8, 128), 0)
 
     def brick(b):
@@ -81,17 +82,41 @@
             jnp.where(lane < 32, edge[23:151, :], edge[7:135, :]),
             jnp.where(lane < 96, edge[25:153, :], edge[9:137, :]),
         )
-
-
-def turn_ids_kernel(ids, out):
+    copy = pltpu.make_async_copy(out, packed, sem)
+    copy.start()
+    copy.wait()
+
+
+def turn_ids_kernel(ids, out, first, last):
     for x in range(8):
-        out[x] = ids[pl.ds(x, 128, stride=8), :].astype(jnp.float32).T
+        plane = ids[pl.ds(x, 128, stride=8), :].astype(jnp.float32).T
+        out[x] = plane
+        first[x] = plane[:8]
+        last[x] = plane[120:]
+
+
+def widen_ids_kernel(y_low, own, y_high, wide, first, last):
+    for x in range(8):
+        wide[x, 0:8, :] = y_low[x]
+        wide[x, 8:136, :] = own[x]
+        wide[x, 136:144, :] = y_high[x]
+    for x in range(DEPTH):
+        for to, k in ((first, x), (last, x + 8 - DEPTH)):
+            to[x, 0:8, :] = y_low[k]
+            to[x, 8:136, :] = own[k]
+            to[x, 136:144, :] = y_high[k]
 
 
 def properties_kernel(
-    place, conductivity, vg_alpha, vg_n, capacity, below, own, above, y_low, y_high,
-    alpha, expo, exponent, cap, trans_x, trans_y, trans_z, cond_x, cond_y,
+    place, conductivity, vg_alpha, vg_n, capacity, below, own, above,
+    out_a, out_n, out_m, out_c, out_x, out_y, out_z,
+    alpha, expo, exponent, cap, trans_x, trans_y, trans_z, cond_x, cond_y, sems,
 ):
+    def copies(first, last):
+        made = (alpha, expo, exponent, cap, trans_x, trans_y, trans_z)
+        outs = (out_a, out_n, out_m, out_c, out_x, out_y, out_z)
+        return [pltpu.make_async_copy(made[k], outs[k], sems.at[k]) for k in range(first, last)]
+
     def lookup(ids, rows):
         fields = [jnp.zeros(ids.shape, jnp.float32) for _ in range(6)]
         for m in range(MATERIALS):
@@ -119,19 +144,18 @@
         trans_z[xi, rows, :] = jnp.where(lane < 127, 2.0 * kz * kz_up / (kz + kz_up), 0.0)
 
     def fill_row(xi, source, x):
-        fill(xi, 0, y_low[xi])
-        fill(xi, 17, y_high[xi])
-
         def tiles(t):
             for k in range(2):
-                fill(xi, 1 + 2 * t + k, source[x, pl.ds(pl.multiple_of(16 * t + 8 * k, 8), 8), :])
-
-        loop(8, tiles)
+                fill(xi, 2 * t + k, source[x, pl.ds(pl.multiple_of(16 * t + 8 * k, 8), 8), :])
+
+        loop(9, tiles)
 
     loop(5, lambda x: fill_row(x, below, x))
     loop(8, lambda x: fill_row(x + 5, own, x))
     loop(5, lambda x: fill_row(x + 13, above, x))
 
+    for copy in copies(0, 4):
+        copy.start()
     x_first = place[0] * 8 - DEPTH
     y_first = place[1] * 128 - 8
     row = iota((CHUNK, 128), 0)
@@ -151,6 +175,10 @@
             )
 
     loop(EX, faces)
+    for copy in copies(4, 7):
+        copy.start()
+    for copy in copies(0, 7):
+        copy.wait()
 
 
 def wetness(level, alpha, expo, exponent):
@@ -231,11 +259,18 @@
 
 
 def main_kernel(
-    source, recv, alpha, expo, exponent, cap, trans_x, trans_y, trans_z, kept, sums,
-    ordered, head, old, rel, d_rel, own_c, cxp, cxm, cyp, cym, czp, czm, k0, k1, k2, k3, k4,
+    source, recv, in_a, in_n, in_m, in_c, in_x, in_y, in_z, kept, sums,
+    alpha, expo, exponent, cap, trans_x, trans_y, trans_z, sems, ordered, head, old, rel, d_rel, own_c, cxp, cxm, cyp, cym, czp, czm, k0, k1, k2, k3, k4,
 ):
     sub = iota((8, 128), 0)
     lane = iota((8, 128), 1)
+    refs = (
+        (in_a, alpha), (in_n, expo), (in_m, exponent), (in_c, cap),
+        (in_x, trans_x), (in_y, trans_y), (in_z, trans_z),
+    )
+    copies = [pltpu.make_async_copy(a, b, sems.at[k]) for k, (a, b) in enumerate(refs)]
+    for copy in copies:
+        copy.start()
 
     def layer(z):
         def tile(k, t):
@@ -301,6 +336,8 @@
             d_rel[xi, to, :] = drel_v
             own_c[xi, to, :] = cap[xi, at, :] * dsat_v
 
+    for copy in copies:
+        copy.wait()
     loop(EX, curves)
 
     def face(t, h_a, h_b, r_a, r_b, d_a, d_b, rise):
@@ -374,6 +411,12 @@
 
         loop(14 - 2 * step, apply)
 
+    keeps = [
+        pltpu.make_async_copy(vectors[k].at[5:13, 16:144, :], kept.at[k], sems.at[7 + k]) for k in range(4)
+    ]
+    for copy in keeps:
+        copy.start()
+
     def largest(i, tops):
         xi = 5 + i
         for c in range(16):
@@ -435,11 +478,8 @@
     for t in range(16):
         sums[8 * t : 8 * t + 8, :] = line
 
-    def keep(x):
-        for k in range(4):
-            kept[k, x] = vectors[k][x + 5, 16:144, :]
-
-    loop(8, keep)
+    for copy in keeps:
+        copy.wait()
 
 
 def turn_back_kernel(kept, out):
@@ -527,9 +567,32 @@
     slot_of = jnp.sum(jnp.where(own_row[None, :] == numbers[:, None], numbers[None, :], 0), axis=1)
     scratch = lambda *shape: pltpu.VMEM(shape, jnp.float32)
 
+    up_x = [(i, i + 1) for i in range(count_x - 1)]
+    down_x = [(i + 1, i) for i in range(count_x - 1)]
+    up_y = [(i, i + 1) for i in range(count_y - 1)]
+    down_y = [(i + 1, i) for i in range(count_y - 1)]
+    ids, first, last = call(
+        turn_ids_kernel, [f32(8, 128, 128)] + [f32(8, 8, 128)] * 2, [VMEM], [VMEM] * 3, [], 8, (10**6, 10**6)
+    )(material_ids.reshape(1024, 128))
+    y_low = lax.ppermute(last, "gy", up_y)
+    y_high = lax.ppermute(first, "gy", down_y)
+    ids, first, last = call(
+        widen_ids_kernel, [f32(8, EY, 128)] + [f32(DEPTH, EY, 128)] * 2, [VMEM] * 3, [VMEM] * 3, [], 8, (10**6, 10**6)
+    )(y_low, ids, y_high)
+    slot_of, first, last = lax.optimization_barrier((slot_of, first, last))
+    below = lax.ppermute(last, "gx", up_x)
+    above = lax.ppermute(first, "gx", down_x)
+
     packed = call(
-        pack_kernel, f32(devices * PIECE, 128), [SMEM, VMEM, VMEM], VMEM, [scratch(PY, 128)], 16, (10**6, 4 * 10**6)
+        pack_kernel,
+        f32(devices * PIECE, 128),
+        [SMEM, VMEM, VMEM],
+        HBM,
+        [scratch(devices * PIECE, 128), scratch(PY, 128), pltpu.SemaphoreType.DMA],
+        63,
+        (10**6, 4 * 10**6),
     )(slot_of, held_head, held_head_old)
+    packed, below, above = lax.optimization_barrier((packed, below, above))
     arrived = lax.all_to_all(packed, AXES, split_axis=0, concat_axis=0, tiled=True)
 
     offsets = (0, -count_y, count_y, -1, 1, count_y - 1, -count_y - 1, count_y + 1, -count_y + 1)
@@ -537,43 +600,31 @@
     source = jnp.sum(
         jnp.where(block_map[None] == bricks[:, None, None], numbers[None, :, None], 0), axis=1
     )
-
-    ids = call(
-        turn_ids_kernel, f32(8, 128, 128), [VMEM], VMEM, [], 8, (10**6, 10**6)
-    )(material_ids.reshape(1024, 128))
-    up_x = [(i, i + 1) for i in range(count_x - 1)]
-    down_x = [(i + 1, i) for i in range(count_x - 1)]
-    up_y = [(i, i + 1) for i in range(count_y - 1)]
-    down_y = [(i + 1, i) for i in range(count_y - 1)]
-    below = lax.ppermute(ids[8 - DEPTH :], "gx", up_x)
-    above = lax.ppermute(ids[:DEPTH], "gx", down_x)
-    last = jnp.concatenate([part[:, 120:] for part in (below, ids, above)], axis=0)
-    first = jnp.concatenate([part[:, :8] for part in (below, ids, above)], axis=0)
-    y_low = lax.ppermute(last, "gy", up_y)
-    y_high = lax.ppermute(first, "gy", down_y)
     place = jnp.stack([at_x, at_y, jnp.int32(count_x), jnp.int32(count_y)])
     fields = call(
         properties_kernel,
         [f32(EX, EY, 128)] * 5 + [f32(EX, PY, 128), f32(EX, EY, 128)],
-        [SMEM] * 5 + [VMEM] * 5,
-        [VMEM] * 7,
-        [scratch(EX, EY, 128), scratch(EX, PY, 128)],
-        24,
+        [SMEM] * 5 + [VMEM] * 3,
+        [HBM] * 7,
+        [scratch(EX, EY, 128)] * 5 + [scratch(EX, PY, 128)] + [scratch(EX, EY, 128)] * 2
+        + [scratch(EX, PY, 128), pltpu.SemaphoreType.DMA((7,))],
+        63,
         (40 * 10**6, 12 * 10**6),
-    )(place, conductivity, vg_alpha, vg_n, capacity, below, ids, above, y_low, y_high)
+    )(place, conductivity, vg_alpha, vg_n, capacity, below, ids, above)
 
     kept, sums = call(
         main_kernel,
         [f32(4, 8, 128, 128), f32(devices, 128)],
-        [SMEM] + [VMEM] * 8,
-        [VMEM] * 2,
-        [scratch(devices * PIECE, 128)] + [scratch(EX, PY, 128)] * 16,
-        56,
+        [SMEM, VMEM] + [HBM] * 7,
+        [HBM, VMEM],
+        [scratch(EX, EY, 128)] * 5 + [scratch(EX, PY, 128), scratch(EX, EY, 128)]
+        + [pltpu.SemaphoreType.DMA((11,)), scratch(devices * PIECE, 128)] + [scratch(EX, PY, 128)] * 16,
+        63,
         (200 * 10**6, 16 * 10**6),
     )(source, arrived, *fields)
     gathered = lax.all_to_all(sums.reshape(devices, 1, 128), AXES, split_axis=0, concat_axis=0, tiled=True)
     turned = call(turn_back_kernel, f32(4, 1024, 128), [VMEM], VMEM, [], 8, (10**6, 4 * 10**6))(kept)
-    update = call(finish_kernel, f32(1024, 128), [VMEM] * 2, VMEM, [], 16, (10**6, 3 * 10**6))(
+    update = call(finish_kernel, f32(1024, 128), [VMEM] * 2, VMEM, [], 8, (10**6, 3 * 10**6))(
         gathered.reshape(devices, 128), turned
     )
     return update.reshape(128, 8, 128)

time: 135 us -> 114 us (0.84)
  waiting for transfers between devices: 37.9 us -> 26.8 us
  local copies, waits for them, and re-layouts: 13.6 us -> 4.13 us
  starting transfers between devices: 33.1 us -> 30.1 us
  Pallas kernels: 48.7 us -> 50.1 us
    ppermute x2, waiting for transfers between devices: 26.9 us -> 2.74 us  [the longest x1 2.74 us: body(): above = lax.ppermute(first, 'gx', down_x)]
    all_to_all x1, waiting for transfers between devices: 0.01 us -> 14.5 us  [body(): lax.all_to_all(packed, AXES, split_axis=0, concat_axis=0, tiled=True)]
    unnamed x36 -> x10, local copies, waits for them, and re-layouts: 12.9 us -> 3.44 us
    all_to_all x1, starting transfers between devices: 11.5 us -> 4.52 us  [body(): lax.all_to_all(sums.reshape(devices, 1, 128), AXES, split_axis=0, concat_...]
    pallas_call x1, Pallas kernels: 16.2 us -> 19.6 us  [body(): call(properties_kernel, [f32(EX, EY, 128)] * 5 + [f32(EX, PY, 128), f32(E...]
    pallas_call x4 -> x5, Pallas kernels: 31.9 us -> 29.9 us  [the longest x1 23.3 us: body(): call(main_kernel, [f32(4, 8, 128, 128), f32(devices, 128)], [SMEM, VMEM]...]
    ppermute x1, waiting for transfers between devices: 3.71 us -> 2.15 us  [body(): y_high = lax.ppermute(first, 'gy', down_y)]
    all_to_all x1, starting transfers between devices: 11.5 us -> 13.1 us  [body(): lax.all_to_all(packed, AXES, split_axis=0, concat_axis=0, tiled=True)]
  transfers between devices with their start and end apart: 6 -> 6, of which waited for: 3 -> 4; matrix products, arithmetic and copies ran while one was open for 1% -> 2% of each run, Pallas kernels for 13% -> 22%
where the time goes in v2:
time: 114 us; the launch traced here: 113 us
  Pallas kernels  50.1 us (44%)
  starting transfers between devices  30.1 us (26%)
  waiting for transfers between devices  26.8 us (24%)
  local copies, waits for them, and re-layouts  4.13 us (4%)
  other arithmetic  2.03 us (2%)
    pallas_call x1, Pallas kernels, body(): call(main_kernel, [f32(4, 8, 128, 128), f32(devices, 128)], [SMEM, VMEM]...  23.3 us
    pallas_call x1, Pallas kernels, body(): call(properties_kernel, [f32(EX, EY, 128)] * 5 + [f32(EX, PY, 128), f32(E...  19.6 us
    all_to_all x1, waiting for transfers between devices, body(): lax.all_to_all(packed, AXES, split_axis=0, concat_axis=0, tiled=True)  14.5 us
    all_to_all x1, starting transfers between devices, body(): lax.all_to_all(packed, AXES, split_axis=0, concat_axis=0, tiled=True)  13.1 us
    all_to_all x1, waiting for transfers between devices, body(): lax.all_to_all(sums.reshape(devices, 1, 128), AXES, split_axis=0, concat_...  7.46 us
    ppermute x1, starting transfers between devices, body(): below = lax.ppermute(last, 'gx', up_x)  4.91 us
    all_to_all x1, starting transfers between devices, body(): lax.all_to_all(sums.reshape(devices, 1, 128), AXES, split_axis=0, concat_...  4.52 us
    ppermute x1, starting transfers between devices, body(): y_low = lax.ppermute(last, 'gy', up_y)  4.37 us
  transfers between devices with their start and end apart: 6, of which 4 were waited for; matrix products, arithmetic and copies ran while one was open for 2% of the time, Pallas kernels for 22%

profile of v2, /device:TPU:1, one launch (start us, length us, event | category | flops | bytes accessed | tf_op | source)
XLA Modules:
  0.0 113.3 jit_solution(4642362358990045342)
XLA Ops:
  0.0 0.0 copy-start.2
  0.0 1.0 copy-done.2
  1.0 0.2 shard_map.91
  1.2 4.4 %collective-permute-start = (f32[8,8,128]{2,1,0:T(8,128)S(1)}, f32[8,8,128]{2,1,0:T(8,128)S(1)}, u32[]{:S(2)}, u32[]{:S(2)}) collective-permute-start(f32[8,8,128]{2,1,0:T(8,128)S(1)} %get-tuple-element.26), channel_id=1, source_target_pairs={{0,1},{1,2},{2,3},{3,4},{4,5},{5,6},{6,7},{8,9},{9,10},{10,11},{11... | collective-permute-start | bytes 98312 | tf_op jit(solution)/shard_map/ppermute | solution.py:577
  5.6 1.3 %collective-permute-start.1 = (f32[8,8,128]{2,1,0:T(8,128)S(1)}, f32[8,8,128]{2,1,0:T(8,128)S(1)}, u32[]{:S(2)}, u32[]{:S(2)}) collective-permute-start(f32[8,8,128]{2,1,0:T(8,128)S(1)} %get-tuple-element.28), channel_id=1, source_target_pairs={{1,0},{2,1},{3,2},{4,3},{5,4},{6,5},{7,6},{9,8},{10,9},{11,10},{12... | collective-permute-start | bytes 98312 | tf_op jit(solution)/shard_map/ppermute | solution.py:578
  6.9 0.7 dynamic-slice_bitcast_fusion
  7.6 0.7 select_reduce_fusion.1.slot_of
  8.3 0.0 collective-permute-done.y_low
  8.3 2.1 %collective-permute-done.1.y_high = f32[8,8,128]{2,1,0:T(8,128)S(1)} collective-permute-done((f32[8,8,128]{2,1,0:T(8,128)S(1)}, f32[8,8,128]{2,1,0:T(8,128)S(1)}, u32[]{:S(2)}, u32[]{:S(2)}) %collective-permute-start.1) | collective-permute-done | bytes 32800 | tf_op jit(solution)/shard_map/ppermute | solution.py:578
  10.5 0.1 shard_map.92
  10.6 0.0 copy-start.1
  10.6 0.8 copy-done.1
  11.4 4.9 %collective-permute-start.2 = (f32[5,144,128]{2,1,0:T(8,128)S(1)}, f32[5,144,128]{2,1,0:T(8,128)}, u32[]{:S(2)}, u32[]{:S(2)}) collective-permute-start(f32[5,144,128]{2,1,0:T(8,128)S(1)} %get-tuple-element.32), channel_id=1, source_target_pairs={{0,8},{8,16},{16,24},{24,32},{32,40},{40,48},{48,56},{56,64},{64,7... | collective-permute-start | bytes 1105928 | tf_op jit(solution)/shard_map/ppermute | solution.py:583
  16.3 1.9 %collective-permute-start.3 = (f32[5,144,128]{2,1,0:T(8,128)S(1)}, f32[5,144,128]{2,1,0:T(8,128)}, u32[]{:S(2)}, u32[]{:S(2)}) collective-permute-start(f32[5,144,128]{2,1,0:T(8,128)S(1)} %get-tuple-element.33), channel_id=1, source_target_pairs={{8,0},{16,8},{24,16},{32,24},{40,32},{48,40},{56,48},{64,56},{72,6... | collective-permute-start | bytes 1105928 | tf_op jit(solution)/shard_map/ppermute | solution.py:584
  18.2 4.3 %shard_map.93 = f32[5120,128]{1,0:T(8,128)} custom-call(s32[128]{0:T(128)} %select_reduce_fusion.1.slot_of, f32[128,8,128]{2,1,0:T(8,128)} %head.1, f32[128,8,128]{2,1,0:T(8,128)} %old.1), custom_call_target="tpu_custom_call" | custom-call | flops 1000000 | bytes 4000000 | tf_op jit(solution)/shard_map/pallas_call | solution.py:586
  22.5 0.0 collective-permute-done.2.below
  22.5 2.7 %collective-permute-done.3.above = f32[5,144,128]{2,1,0:T(8,128)} collective-permute-done((f32[5,144,128]{2,1,0:T(8,128)S(1)}, f32[5,144,128]{2,1,0:T(8,128)}, u32[]{:S(2)}, u32[]{:S(2)}) %collective-permute-start.3) | collective-permute-done | bytes 368672 | tf_op jit(solution)/shard_map/ppermute | solution.py:584
  25.2 0.0 copy-start.4
  25.2 0.0 copy-start.3
  25.2 13.1 %all-to-all-start = ((f32[128,40,128]{2,1,0:T(8,128)}), f32[128,40,128]{2,1,0:T(8,128)}, u32[]{:S(2)}, u32[]{:S(2)}) async-start(f32[128,40,128]{2,1,0:T(8,128)} %bitcast.14), calls=%async_computation | async-start | bytes 5242880 | tf_op jit(solution)/shard_map/all_to_all | solution.py:596
  38.3 0.6 pad_add_fusion.place
  38.9 0.0 copy-done.4
  38.9 0.0 copy-done.3
  38.9 0.7 select_reduce_fusion.source
  39.6 19.6 %shard_map.94 = (f32[18,144,128]{2,1,0:T(8,128)}, f32[18,144,128]{2,1,0:T(8,128)}, f32[18,144,128]{2,1,0:T(8,128)}, f32[18,144,128]{2,1,0:T(8,128)}, f32[18,144,...) custom-call(s32[4]{0:T(128)} %pad_add_fusion.place, f32[3,16]{1,0:T(4,128)} %conductivity.1, ...), custom_call_target="tpu_custom_call" | custom-call | flops 40000000 | bytes 12000000 | tf_op jit(solution)/shard_map/pallas_call | solution.py:604
  59.3 14.5 %all-to-all-done = f32[128,40,128]{2,1,0:T(8,128)} async-done(((f32[128,40,128]{2,1,0:T(8,128)}), f32[128,40,128]{2,1,0:T(8,128)}, u32[]{:S(2)}, u32[]{:S(2)}) %all-to-all-start) | async-done | bytes 2621472 | tf_op jit(solution)/shard_map/all_to_all | solution.py:596
  73.7 23.3 %shard_map.95 = (f32[4,8,128,128]{3,2,1,0:T(8,128)}, f32[128,128]{1,0:T(8,128)}) custom-call(s32[9,128]{1,0:T(8,128)} %select_reduce_fusion.source, f32[5120,128]{1,0:T(8,128)} %bitcast.3.recv, f32[18,144,128]{2,1,0:T(8,128)} %get-tuple-element.38.in_a, f32[18,144,128]{2,1,0:T(8,128)} %get-tuple-element.39.in_n, f32[18,144,128]{2,1,0:T(8,128)} %get-tuple-element.40.in_m, ...), custom_call_target="tpu_custom_call" | custom-call | flops 200000000 | bytes 16000000 | tf_op jit(solution)/shard_map/pallas_call | solution.py:615
  97.0 4.5 %all-to-all-start.1 = ((f32[128,1,128]{2,1,0:T(1,128)}), f32[128,1,128]{2,1,0:T(1,128)S(1)}, u32[]{:S(2)}, u32[]{:S(2)}) async-start(f32[128,1,128]{2,1,0:T(1,128)} %bitcast.15), calls=%async_computation.1 | async-start | bytes 131072 | tf_op jit(solution)/shard_map/all_to_all | solution.py:625
  101.6 0.0 copy-start
  101.6 1.6 %copy-done = f32[4,8,128,128]{3,2,1,0:T(8,128)S(1)} copy-done((f32[4,8,128,128]{3,2,1,0:T(8,128)S(1)}, f32[4,8,128,128]{3,2,1,0:T(8,128)}, u32[]{:S(2)}) %copy-start) | copy-done | bytes 2097176
  103.2 0.6 shard_map.96.vectors
  103.8 7.5 %all-to-all-done.1 = f32[128,1,128]{2,1,0:T(1,128)S(1)} async-done(((f32[128,1,128]{2,1,0:T(1,128)}), f32[128,1,128]{2,1,0:T(1,128)S(1)}, u32[]{:S(2)}, u32[]{:S(2)}) %all-to-all-start.1) | async-done | bytes 65568 | tf_op jit(solution)/shard_map/all_to_all | solution.py:625
  111.2 2.1 %shard_map.97 = f32[1024,128]{1,0:T(8,128)} custom-call(f32[128,128]{1,0:T(8,128)S(1)} %bitcast.13, f32[4,1024,128]{2,1,0:T(8,128)S(1)} %shard_map.96.vectors), custom_call_target="tpu_custom_call" | custom-call | flops 1000000 | bytes 3000000 | tf_op jit(solution)/shard_map/pallas_call | solution.py:627
  (1 shorter events, 0.0 us)
Async XLA Ops:
  0.0 1.0 copy-start.2
  1.2 7.1 %collective-permute-start = (f32[8,8,128]{2,1,0:T(8,128)S(1)}, f32[8,8,128]{2,1,0:T(8,128)S(1)}, u32[]{:S(2)}, u32[]{:S(2)}) collective-permute-start(f32[8,8,128]{2,1,0:T(8,128)S(1)} %get-tuple-element.26), channel_id=1, source_target_pairs={{0,1},{1,2},{2,3},{3,4},{4,5},{5,6},{6,7},{8,9},{9,10},{10,11},{11... | collective-permute-start | bytes 98312 | tf_op jit(solution)/shard_map/ppermute | solution.py:577
  5.6 4.8 %collective-permute-start.1 = (f32[8,8,128]{2,1,0:T(8,128)S(1)}, f32[8,8,128]{2,1,0:T(8,128)S(1)}, u32[]{:S(2)}, u32[]{:S(2)}) collective-permute-start(f32[8,8,128]{2,1,0:T(8,128)S(1)} %get-tuple-element.28), channel_id=1, source_target_pairs={{1,0},{2,1},{3,2},{4,3},{5,4},{6,5},{7,6},{9,8},{10,9},{11,10},{12... | collective-permute-start | bytes 98312 | tf_op jit(solution)/shard_map/ppermute | solution.py:578
  10.6 0.8 copy-start.1
  11.4 11.1 %collective-permute-start.2 = (f32[5,144,128]{2,1,0:T(8,128)S(1)}, f32[5,144,128]{2,1,0:T(8,128)}, u32[]{:S(2)}, u32[]{:S(2)}) collective-permute-start(f32[5,144,128]{2,1,0:T(8,128)S(1)} %get-tuple-element.32), channel_id=1, source_target_pairs={{0,8},{8,16},{16,24},{24,32},{32,40},{40,48},{48,56},{56,64},{64,7... | collective-permute-start | bytes 1105928 | tf_op jit(solution)/shard_map/ppermute | solution.py:583
  16.3 8.9 %collective-permute-start.3 = (f32[5,144,128]{2,1,0:T(8,128)S(1)}, f32[5,144,128]{2,1,0:T(8,128)}, u32[]{:S(2)}, u32[]{:S(2)}) collective-permute-start(f32[5,144,128]{2,1,0:T(8,128)S(1)} %get-tuple-element.33), channel_id=1, source_target_pairs={{8,0},{16,8},{24,16},{32,24},{40,32},{48,40},{56,48},{64,56},{72,6... | collective-permute-start | bytes 1105928 | tf_op jit(solution)/shard_map/ppermute | solution.py:584
  25.2 13.7 %copy-start.4 = (s32[9]{0:T(128)S(1)}, s32[9]{0:T(128)}, u32[]{:S(2)}) copy-start(s32[9]{0:T(128)} %constant.21.clone) | copy-start | bytes 112
  25.2 13.7 %copy-start.3 = (s32[128,128]{1,0:T(8,128)S(1)}, s32[128,128]{1,0:T(8,128)}, u32[]{:S(2)}) copy-start(s32[128,128]{1,0:T(8,128)} %param.12) | copy-start | bytes 196612
  25.2 48.5 %all-to-all-start = ((f32[128,40,128]{2,1,0:T(8,128)}), f32[128,40,128]{2,1,0:T(8,128)}, u32[]{:S(2)}, u32[]{:S(2)}) async-start(f32[128,40,128]{2,1,0:T(8,128)} %bitcast.14), calls=%async_computation | async-start | bytes 5242880 | tf_op jit(solution)/shard_map/all_to_all | solution.py:596
  97.0 14.2 %all-to-all-start.1 = ((f32[128,1,128]{2,1,0:T(1,128)}), f32[128,1,128]{2,1,0:T(1,128)S(1)}, u32[]{:S(2)}, u32[]{:S(2)}) async-start(f32[128,1,128]{2,1,0:T(1,128)} %bitcast.15), calls=%async_computation.1 | async-start | bytes 131072 | tf_op jit(solution)/shard_map/all_to_all | solution.py:625
  101.6 1.6 %copy-start = (f32[4,8,128,128]{3,2,1,0:T(8,128)S(1)}, f32[4,8,128,128]{3,2,1,0:T(8,128)}, u32[]{:S(2)}) copy-start(f32[4,8,128,128]{3,2,1,0:T(8,128)} %get-tuple-element.46.kept) | copy-start | bytes 6291460

commit v3 on v2

--- a/solution.py
+++ b/solution.py
@@ -91,93 +91,102 @@
     for x in range(8):
         plane = ids[pl.ds(x, 128, stride=8), :].astype(jnp.float32).T
         out[x] = plane
-        first[x] = plane[:8]
-        last[x] = plane[120:]
-
-
-def widen_ids_kernel(y_low, own, y_high, wide, first, last):
-    for x in range(8):
-        wide[x, 0:8, :] = y_low[x]
-        wide[x, 8:136, :] = own[x]
-        wide[x, 136:144, :] = y_high[x]
-    for x in range(DEPTH):
-        for to, k in ((first, x), (last, x + 8 - DEPTH)):
-            to[x, 0:8, :] = y_low[k]
-            to[x, 8:136, :] = own[k]
-            to[x, 136:144, :] = y_high[k]
+        if x < DEPTH:
+            first[x] = plane
+        if x >= 8 - DEPTH:
+            last[x - 8 + DEPTH] = plane
+
+
+def edge_ids_kernel(below, own, above, first, last):
+    for k, part in ((0, below), (5, own), (13, above)):
+        for x in range(part.shape[0]):
+            first[k + x] = part[x, 0:8, :]
+            last[k + x] = part[x, 120:128, :]
+
+
+def tables_of(conductivity, vg_alpha, vg_n, capacity):
+    lane = iota((8, 128), 1)
+    reads = [
+        lambda m: conductivity[0, m], lambda m: conductivity[1, m], lambda m: conductivity[2, m],
+        lambda m: vg_alpha[m], lambda m: vg_n[m], lambda m: capacity[m],
+    ]
+    tables = []
+    for read in reads:
+        table = jnp.zeros((8, 128), jnp.float32)
+        for m in range(MATERIALS):
+            table = jnp.where(lane == m, read(m), table)
+        tables.append(table)
+    return tables
+
+
+def lookup(tables, ids):
+    index = ids.astype(jnp.int32)
+    return [jnp.take_along_axis(table, index, axis=1) for table in tables]
+
+
+def harmonic(a, b):
+    return 2.0 * a * b / (a + b)
+
+
+def upward_faces(kz):
+    return jnp.where(iota(kz.shape, 1) < 127, harmonic(kz, pltpu.roll(kz, 127, 1)), 0.0)
+
+
+def x_inside(place, xi):
+    x = place[0] * 8 - DEPTH + xi
+    return jnp.where((x >= 0) & (x + 1 < place[2] * 8), 1.0, 0.0)
+
+
+def y_inside(place, shape, first):
+    y = place[1] * 128 - 8 + first + iota(shape, 0)
+    return (y >= 0) & (y + 1 < place[3] * 128)
 
 
 def properties_kernel(
     place, conductivity, vg_alpha, vg_n, capacity, below, own, above,
-    out_a, out_n, out_m, out_c, out_x, out_y, out_z,
-    alpha, expo, exponent, cap, trans_x, trans_y, trans_z, cond_x, cond_y, sems,
+    out_a, out_n, out_m, out_c, out_x, out_y, out_z, out_e,
+    alpha, expo, exponent, cap, trans_x, trans_y, trans_z, edges, cond_x, cond_y, sems,
 ):
     def copies(first, last):
-        made = (alpha, expo, exponent, cap, trans_x, trans_y, trans_z)
-        outs = (out_a, out_n, out_m, out_c, out_x, out_y, out_z)
+        made = (alpha, expo, exponent, cap, trans_x, trans_y, trans_z, edges)
+        outs = (out_a, out_n, out_m, out_c, out_x, out_y, out_z, out_e)
         return [pltpu.make_async_copy(made[k], outs[k], sems.at[k]) for k in range(first, last)]
 
-    def lookup(ids, rows):
-        fields = [jnp.zeros(ids.shape, jnp.float32) for _ in range(6)]
-        for m in range(MATERIALS):
-            match = ids == float(m)
-            values = (
-                conductivity[0, m], conductivity[1, m], conductivity[2, m],
-                vg_alpha[m], vg_n[m], capacity[m],
-            )
-            fields = [jnp.where(match, value, field) for value, field in zip(values, fields)]
-        return fields
-
-    lane = iota((8, 128), 1)
-
-    def fill(xi, tile, ids):
-        rows = pl.ds(8 * tile if isinstance(tile, int) else pl.multiple_of(8 * tile, 8), 8)
-        next_rows = pl.ds(8 + 8 * tile if isinstance(tile, int) else pl.multiple_of(8 + 8 * tile, 8), 8)
-        kx, ky, kz, a, n, c = lookup(ids, rows)
-        alpha[xi, rows, :] = a
-        expo[xi, rows, :] = n
-        exponent[xi, rows, :] = 1.0 - 1.0 / n
-        cap[xi, rows, :] = STORE * c
-        cond_x[xi, rows, :] = kx
-        cond_y[xi, next_rows, :] = ky
-        kz_up = pltpu.roll(kz, 127, 1)
-        trans_z[xi, rows, :] = jnp.where(lane < 127, 2.0 * kz * kz_up / (kz + kz_up), 0.0)
+    tables = tables_of(conductivity, vg_alpha, vg_n, capacity)
 
     def fill_row(xi, source, x):
-        def tiles(t):
-            for k in range(2):
-                fill(xi, 2 * t + k, source[x, pl.ds(pl.multiple_of(16 * t + 8 * k, 8), 8), :])
-
-        loop(9, tiles)
+        for t in range(16):
+            at = slice(8 * t, 8 * t + 8)
+            kx, ky, kz, a, n, c = lookup(tables, source[x, at, :])
+            alpha[xi, at, :] = a
+            expo[xi, at, :] = n
+            exponent[xi, at, :] = 1.0 - 1.0 / n
+            cap[xi, at, :] = STORE * c
+            cond_x[xi, at, :] = kx
+            cond_y[xi, at, :] = ky
+            trans_z[xi, at, :] = upward_faces(kz)
+            if t in (0, 15):
+                edges[xi, t // 15] = ky
 
     loop(5, lambda x: fill_row(x, below, x))
     loop(8, lambda x: fill_row(x + 5, own, x))
     loop(5, lambda x: fill_row(x + 13, above, x))
-
     for copy in copies(0, 4):
         copy.start()
-    x_first = place[0] * 8 - DEPTH
-    y_first = place[1] * 128 - 8
-    row = iota((CHUNK, 128), 0)
 
     def faces(xi):
-        x = x_first + xi
-        inside = jnp.where((x >= 0) & (x + 1 < place[2] * 8), 1.0, 0.0)
-        for c in range(CHUNKS):
-            rows = slice(CHUNK * c, CHUNK * (c + 1))
-            a, b = cond_x[xi, rows, :], cond_x[jnp.minimum(xi + 1, EX - 1), rows, :]
-            trans_x[xi, rows, :] = inside * (2.0 * a * b / (a + b))
-            a = cond_y[xi, 8 + CHUNK * c : 8 + CHUNK * (c + 1), :]
-            b = cond_y[xi, 9 + CHUNK * c : 9 + CHUNK * (c + 1), :]
-            y = y_first + CHUNK * c + row
-            trans_y[xi, 8 + CHUNK * c : 8 + CHUNK * (c + 1), :] = jnp.where(
-                (y >= 0) & (y + 1 < place[3] * 128), 2.0 * a * b / (a + b), 0.0
-            )
+        inside = x_inside(place, xi)
+        above_xi = jnp.minimum(xi + 1, EX - 1)
+        for c in range(4):
+            at = slice(32 * c, 32 * c + 32)
+            trans_x[xi, at, :] = inside * harmonic(cond_x[xi, at, :], cond_x[above_xi, at, :])
+            up = slice(32 * c + 1, 32 * c + 33)
+            trans_y[xi, at, :] = harmonic(cond_y[xi, at, :], cond_y[xi, up, :])
 
     loop(EX, faces)
-    for copy in copies(4, 7):
+    for copy in copies(4, 8):
         copy.start()
-    for copy in copies(0, 7):
+    for copy in copies(0, 8):
         copy.wait()
 
 
@@ -259,8 +268,10 @@
 
 
 def main_kernel(
-    source, recv, in_a, in_n, in_m, in_c, in_x, in_y, in_z, kept, sums,
+    source, place, conductivity, vg_alpha, vg_n, capacity,
+    recv, y_low, y_high, edges, in_a, in_n, in_m, in_c, in_x, in_y, in_z, kept, sums,
     alpha, expo, exponent, cap, trans_x, trans_y, trans_z, sems, ordered, head, old, rel, d_rel, own_c, cxp, cxm, cyp, cym, czp, czm, k0, k1, k2, k3, k4,
+    side_x, side_y,
 ):
     sub = iota((8, 128), 0)
     lane = iota((8, 128), 1)
@@ -268,7 +279,10 @@
         (in_a, alpha), (in_n, expo), (in_m, exponent), (in_c, cap),
         (in_x, trans_x), (in_y, trans_y), (in_z, trans_z),
     )
-    copies = [pltpu.make_async_copy(a, b, sems.at[k]) for k, (a, b) in enumerate(refs)]
+    copies = [
+        pltpu.make_async_copy(a, b.at[:, 16:144] if b is trans_y else b.at[:, 8:136], sems.at[k])
+        for k, (a, b) in enumerate(refs)
+    ]
     for copy in copies:
         copy.start()
 
@@ -336,8 +350,36 @@
             d_rel[xi, to, :] = drel_v
             own_c[xi, to, :] = cap[xi, at, :] * dsat_v
 
+    tables = tables_of(conductivity, vg_alpha, vg_n, capacity)
+
+    def side_rows(xi):
+        for source_ids, at in ((y_low, slice(0, 8)), (y_high, slice(136, 144))):
+            to = slice(at.start + 8, at.stop + 8)
+            kx, ky, kz, a, n, c = lookup(tables, source_ids[xi])
+            alpha[xi, at, :] = a
+            expo[xi, at, :] = n
+            exponent[xi, at, :] = 1.0 - 1.0 / n
+            cap[xi, at, :] = STORE * c
+            trans_z[xi, at, :] = upward_faces(kz)
+            side_x[xi, at.start // 17 : at.start // 17 + 8, :] = kx
+            side_y[xi, to, :] = ky
+        side_y[xi, 16:24, :] = edges[xi, 0]
+        side_y[xi, 136:144, :] = edges[xi, 1]
+
+    loop(EX, side_rows)
     for copy in copies:
         copy.wait()
+
+    def side_faces(xi):
+        pair = x_inside(place, xi) * harmonic(side_x[xi], side_x[jnp.minimum(xi + 1, EX - 1)])
+        trans_x[xi, 0:8, :] = pair[0:8]
+        trans_x[xi, 136:144, :] = pair[8:16]
+        for first, last in ((8, 16), (136, 152)):
+            here = slice(first, last)
+            value = harmonic(side_y[xi, here, :], side_y[xi, first + 1 : last + 1, :])
+            trans_y[xi, here, :] = jnp.where(y_inside(place, value.shape, first - 8), value, 0.0)
+
+    loop(EX, side_faces)
     loop(EX, curves)
 
     def face(t, h_a, h_b, r_a, r_b, d_a, d_b, rise):
@@ -572,13 +614,8 @@
     up_y = [(i, i + 1) for i in range(count_y - 1)]
     down_y = [(i + 1, i) for i in range(count_y - 1)]
     ids, first, last = call(
-        turn_ids_kernel, [f32(8, 128, 128)] + [f32(8, 8, 128)] * 2, [VMEM], [VMEM] * 3, [], 8, (10**6, 10**6)
+        turn_ids_kernel, [f32(8, 128, 128)] + [f32(DEPTH, 128, 128)] * 2, [VMEM], [VMEM] * 3, [], 8, (10**6, 10**6)
     )(material_ids.reshape(1024, 128))
-    y_low = lax.ppermute(last, "gy", up_y)
-    y_high = lax.ppermute(first, "gy", down_y)
-    ids, first, last = call(
-        widen_ids_kernel, [f32(8, EY, 128)] + [f32(DEPTH, EY, 128)] * 2, [VMEM] * 3, [VMEM] * 3, [], 8, (10**6, 10**6)
-    )(y_low, ids, y_high)
     slot_of, first, last = lax.optimization_barrier((slot_of, first, last))
     below = lax.ppermute(last, "gx", up_x)
     above = lax.ppermute(first, "gx", down_x)
@@ -601,13 +638,18 @@
         jnp.where(block_map[None] == bricks[:, None, None], numbers[None, :, None], 0), axis=1
     )
     place = jnp.stack([at_x, at_y, jnp.int32(count_x), jnp.int32(count_y)])
-    fields = call(
+    first, last = call(
+        edge_ids_kernel, [f32(EX, 8, 128)] * 2, [VMEM] * 3, [VMEM] * 2, [], 8, (10**5, 10**6)
+    )(below, ids, above)
+    y_low = lax.ppermute(last, "gy", up_y)
+    y_high = lax.ppermute(first, "gy", down_y)
+    *fields, edges = call(
         properties_kernel,
-        [f32(EX, EY, 128)] * 5 + [f32(EX, PY, 128), f32(EX, EY, 128)],
+        [f32(EX, 128, 128)] * 7 + [f32(EX, 2, 8, 128)],
         [SMEM] * 5 + [VMEM] * 3,
-        [HBM] * 7,
-        [scratch(EX, EY, 128)] * 5 + [scratch(EX, PY, 128)] + [scratch(EX, EY, 128)] * 2
-        + [scratch(EX, PY, 128), pltpu.SemaphoreType.DMA((7,))],
+        [HBM] * 8,
+        [scratch(EX, 128, 128)] * 7 + [scratch(EX, 2, 8, 128), scratch(EX, 128, 128), scratch(EX, 136, 128)]
+        + [pltpu.SemaphoreType.DMA((8,))],
         63,
         (40 * 10**6, 12 * 10**6),
     )(place, conductivity, vg_alpha, vg_n, capacity, below, ids, above)
@@ -615,13 +657,14 @@
     kept, sums = call(
         main_kernel,
         [f32(4, 8, 128, 128), f32(devices, 128)],
-        [SMEM, VMEM] + [HBM] * 7,
+        [SMEM] * 6 + [VMEM] * 4 + [HBM] * 7,
         [HBM, VMEM],
         [scratch(EX, EY, 128)] * 5 + [scratch(EX, PY, 128), scratch(EX, EY, 128)]
-        + [pltpu.SemaphoreType.DMA((11,)), scratch(devices * PIECE, 128)] + [scratch(EX, PY, 128)] * 16,
+        + [pltpu.SemaphoreType.DMA((11,)), scratch(devices * PIECE, 128)] + [scratch(EX, PY, 128)] * 16
+        + [scratch(EX, 16, 128), scratch(EX, PY, 128)],
         63,
         (200 * 10**6, 16 * 10**6),
-    )(source, arrived, *fields)
+    )(source, place, conductivity, vg_alpha, vg_n, capacity, arrived, y_low, y_high, edges, *fields)
     gathered = lax.all_to_all(sums.reshape(devices, 1, 128), AXES, split_axis=0, concat_axis=0, tiled=True)
     turned = call(turn_back_kernel, f32(4, 1024, 128), [VMEM], VMEM, [], 8, (10**6, 4 * 10**6))(kept)
     update = call(finish_kernel, f32(1024, 128), [VMEM] * 2, VMEM, [], 8, (10**6, 3 * 10**6))(

time: 114 us -> 109 us (0.956)
  Pallas kernels: 50.1 us -> 46.4 us
    ppermute x1, waiting for transfers between devices: 0.01 us -> 8.04 us  [body(): y_low = lax.ppermute(last, 'gy', up_y)]
    all_to_all x1, waiting for transfers between devices: 14.5 us -> 7.89 us  [body(): lax.all_to_all(packed, AXES, split_axis=0, concat_axis=0, tiled=True)]
    pallas_call x4, Pallas kernels: 43.2 us -> 39.4 us  [the longest x1 25.8 us: body(): call(main_kernel, [f32(4, 8, 128, 128), f32(devices, 128)], [SMEM] * 6 +...]
    all_to_all x1, starting transfers between devices: 4.52 us -> 6.12 us  [body(): lax.all_to_all(sums.reshape(devices, 1, 128), AXES, split_axis=0, concat_...]
    ppermute x1, waiting for transfers between devices: 2.15 us -> 0.83 us  [body(): y_high = lax.ppermute(first, 'gy', down_y)]
    unnamed x10 -> x16, local copies, waits for them, and re-layouts: 3.44 us -> 2.65 us
  transfers between devices with their start and end apart: 6 -> 6, of which waited for: 4 -> 5; matrix products, arithmetic and copies ran while one was open for 2% -> 1% of each run, Pallas kernels for 22% -> 16%
where the time goes in v3:
time: 109 us
  Pallas kernels  46.4 us (43%)
  starting transfers between devices  30.2 us (28%)
  waiting for transfers between devices  26.7 us (24%)
  local copies, waits for them, and re-layouts  3.34 us (3%)
  other arithmetic  1.97 us (2%)
    pallas_call x1, Pallas kernels, body(): call(main_kernel, [f32(4, 8, 128, 128), f32(devices, 128)], [SMEM] * 6 +...  25.8 us
    all_to_all x1, starting transfers between devices, body(): lax.all_to_all(packed, AXES, split_axis=0, concat_axis=0, tiled=True)  13 us
    pallas_call x1, Pallas kernels, body(): call(properties_kernel, [f32(EX, 128, 128)] * 7 + [f32(EX, 2, 8, 128)], [...  11 us
    ppermute x1, waiting for transfers between devices, body(): y_low = lax.ppermute(last, 'gy', up_y)  8.04 us
    all_to_all x1, waiting for transfers between devices, body(): lax.all_to_all(packed, AXES, split_axis=0, concat_axis=0, tiled=True)  7.89 us
    all_to_all x1, waiting for transfers between devices, body(): lax.all_to_all(sums.reshape(devices, 1, 128), AXES, split_axis=0, concat_...  7.4 us
    all_to_all x1, starting transfers between devices, body(): lax.all_to_all(sums.reshape(devices, 1, 128), AXES, split_axis=0, concat_...  6.12 us
    ppermute x1, starting transfers between devices, body(): below = lax.ppermute(last, 'gx', up_x)  4.5 us
  transfers between devices with their start and end apart: 6, of which 5 were waited for; matrix products, arithmetic and copies ran while one was open for 1% of the time, Pallas kernels for 16%

profile of v3, /device:TPU:1, one launch (start us, length us, event | category | flops | bytes accessed | tf_op | source)
XLA Modules:
  0.0 108.7 jit_solution(15720055298733210539)
XLA Ops:
  0.0 0.7 dynamic-slice_bitcast_fusion
  0.7 0.7 select_reduce_fusion.1.slot_of
  1.3 0.0 copy-start.3
  1.3 1.0 copy-done.3
  2.4 1.0 shard_map.91
  3.4 0.0 copy-start.1
  3.4 4.5 %collective-permute-start = (f32[5,128,128]{2,1,0:T(8,128)}, f32[5,128,128]{2,1,0:T(8,128)S(1)}, u32[]{:S(2)}, u32[]{:S(2)}) collective-permute-start(f32[5,128,128]{2,1,0:T(8,128)} %get-tuple-element.29), channel_id=1, source_target_pairs={{0,8},{8,16},{16,24},{24,32},{32,40},{40,48},{48,56},{56,64},{64,7... | collective-permute-start | bytes 983048 | tf_op jit(solution)/shard_map/ppermute | solution.py:620
  7.9 1.9 %collective-permute-start.1 = (f32[5,128,128]{2,1,0:T(8,128)}, f32[5,128,128]{2,1,0:T(8,128)}, u32[]{:S(2)}, u32[]{:S(2)}) collective-permute-start(f32[5,128,128]{2,1,0:T(8,128)} %get-tuple-element.30), channel_id=1, source_target_pairs={{8,0},{16,8},{24,16},{32,24},{40,32},{48,40},{56,48},{64,56},{72,6... | collective-permute-start | bytes 983048 | tf_op jit(solution)/shard_map/ppermute | solution.py:621
  9.8 4.2 %shard_map.92 = f32[5120,128]{1,0:T(8,128)} custom-call(s32[128]{0:T(128)} %select_reduce_fusion.1.slot_of, f32[128,8,128]{2,1,0:T(8,128)} %head.1, f32[128,8,128]{2,1,0:T(8,128)} %old.1), custom_call_target="tpu_custom_call" | custom-call | flops 1000000 | bytes 4000000 | tf_op jit(solution)/shard_map/pallas_call | solution.py:623
  14.1 0.0 collective-permute-done.below
  14.1 0.0 copy-start.2
  14.1 2.5 %collective-permute-done.1.above = f32[5,128,128]{2,1,0:T(8,128)} collective-permute-done((f32[5,128,128]{2,1,0:T(8,128)}, f32[5,128,128]{2,1,0:T(8,128)}, u32[]{:S(2)}, u32[]{:S(2)}) %collective-permute-start.1) | collective-permute-done | bytes 327712 | tf_op jit(solution)/shard_map/ppermute | solution.py:621
  16.6 0.0 copy-start.7
  16.6 0.0 copy-start.6
  16.6 13.0 %all-to-all-start = ((f32[128,40,128]{2,1,0:T(8,128)}), f32[128,40,128]{2,1,0:T(8,128)}, u32[]{:S(2)}, u32[]{:S(2)}) async-start(f32[128,40,128]{2,1,0:T(8,128)} %bitcast.14), calls=%async_computation | async-start | bytes 5242880 | tf_op jit(solution)/shard_map/all_to_all | solution.py:633
  29.6 0.0 copy-done.7
  29.6 0.0 copy-done.6
  29.6 0.7 select_reduce_fusion.source
  30.4 0.0 copy-done.1
  30.4 0.0 copy-done.2
  30.4 1.6 %shard_map.93 = (f32[18,8,128]{2,1,0:T(8,128)S(1)}, f32[18,8,128]{2,1,0:T(8,128)}) custom-call(f32[5,128,128]{2,1,0:T(8,128)S(1)} %collective-permute-done.below, f32[8,128,128]{2,1,0:T(8,128)S(1)} %get-tuple-element.33.own, f32[5,128,128]{2,1,0:T(8,128)} %collective-permute-done.1.above), custom_call_target="tpu_custom_call" | custom-call | flops 100000 | bytes 1000000 | tf_op jit(solution)/shard_map/pallas_call | solution.py:641
  32.0 3.4 %collective-permute-start.2 = (f32[18,8,128]{2,1,0:T(8,128)}, f32[18,8,128]{2,1,0:T(8,128)S(1)}, u32[]{:S(2)}, u32[]{:S(2)}) collective-permute-start(f32[18,8,128]{2,1,0:T(8,128)} %get-tuple-element.35), channel_id=1, source_target_pairs={{0,1},{1,2},{2,3},{3,4},{4,5},{5,6},{6,7},{8,9},{9,10},{10,11},{11... | collective-permute-start | bytes 221192 | tf_op jit(solution)/shard_map/ppermute | solution.py:644
  35.4 1.3 %collective-permute-start.3 = (f32[18,8,128]{2,1,0:T(8,128)S(1)}, f32[18,8,128]{2,1,0:T(8,128)S(1)}, u32[]{:S(2)}, u32[]{:S(2)}) collective-permute-start(f32[18,8,128]{2,1,0:T(8,128)S(1)} %get-tuple-element.36), channel_id=1, source_target_pairs={{1,0},{2,1},{3,2},{4,3},{5,4},{6,5},{7,6},{9,8},{10,9},{11,10},{12... | collective-permute-start | bytes 221192 | tf_op jit(solution)/shard_map/ppermute | solution.py:645
  36.7 0.6 pad_add_fusion.place
  37.3 11.0 %shard_map.94 = (f32[18,128,128]{2,1,0:T(8,128)}, f32[18,128,128]{2,1,0:T(8,128)}, f32[18,128,128]{2,1,0:T(8,128)}, f32[18,128,128]{2,1,0:T(8,128)}, f32[18,128,...) custom-call(s32[4]{0:T(128)} %pad_add_fusion.place, ...), custom_call_target="tpu_custom_call" | custom-call | flops 40000000 | bytes 12000000 | tf_op jit(solution)/shard_map/pallas_call | solution.py:646
  48.3 8.0 %collective-permute-done.2.y_low = f32[18,8,128]{2,1,0:T(8,128)S(1)} collective-permute-done((f32[18,8,128]{2,1,0:T(8,128)}, f32[18,8,128]{2,1,0:T(8,128)S(1)}, u32[]{:S(2)}, u32[]{:S(2)}) %collective-permute-start.2) | collective-permute-done | bytes 73760 | tf_op jit(solution)/shard_map/ppermute | solution.py:644
  56.3 0.0 copy-start.4
  56.3 0.8 collective-permute-done.3.y_high
  57.1 0.0 copy-start.5
  57.1 7.9 %all-to-all-done = f32[128,40,128]{2,1,0:T(8,128)} async-done(((f32[128,40,128]{2,1,0:T(8,128)}), f32[128,40,128]{2,1,0:T(8,128)}, u32[]{:S(2)}, u32[]{:S(2)}) %all-to-all-start) | async-done | bytes 2621472 | tf_op jit(solution)/shard_map/all_to_all | solution.py:633
  65.0 0.0 copy-done.4
  65.0 0.0 copy-done.5
  65.0 25.8 %shard_map.95 = (f32[4,8,128,128]{3,2,1,0:T(8,128)}, f32[128,128]{1,0:T(8,128)}) custom-call(s32[9,128]{1,0:T(8,128)} %select_reduce_fusion.source, s32[4]{0:T(128)} %pad_add_fusion.place, f32[3,16]{1,0:T(4,128)} %conductivity.3, f32[16]{0:T(128)} %vg_alpha.3, f32[16]{0:T(128)} %vg_n.3, f32[16]{0:T(128)} %capacity.3, f32[5120,128]{1,0:T(8,128)} %bitcast.5.recv, ...), custom_call_target="tpu_custom_call" | custom-call | flops 200000000 | bytes 16000000 | tf_op jit(solution)/shard_map/pallas_call | solution.py:657
  90.9 6.1 %all-to-all-start.1 = ((f32[128,1,128]{2,1,0:T(1,128)}), f32[128,1,128]{2,1,0:T(1,128)S(1)}, u32[]{:S(2)}, u32[]{:S(2)}) async-start(f32[128,1,128]{2,1,0:T(1,128)} %bitcast.15), calls=%async_computation.1 | async-start | bytes 131072 | tf_op jit(solution)/shard_map/all_to_all | solution.py:668
  97.0 0.0 copy-start
  97.0 1.6 %copy-done = f32[4,8,128,128]{3,2,1,0:T(8,128)S(1)} copy-done((f32[4,8,128,128]{3,2,1,0:T(8,128)S(1)}, f32[4,8,128,128]{3,2,1,0:T(8,128)}, u32[]{:S(2)}) %copy-start) | copy-done | bytes 2097176
  98.6 0.6 shard_map.96.vectors
  99.2 7.4 %all-to-all-done.1 = f32[128,1,128]{2,1,0:T(1,128)S(1)} async-done(((f32[128,1,128]{2,1,0:T(1,128)}), f32[128,1,128]{2,1,0:T(1,128)S(1)}, u32[]{:S(2)}, u32[]{:S(2)}) %all-to-all-start.1) | async-done | bytes 65568 | tf_op jit(solution)/shard_map/all_to_all | solution.py:668
  106.6 2.1 %shard_map.97 = f32[1024,128]{1,0:T(8,128)} custom-call(f32[128,128]{1,0:T(8,128)S(1)} %bitcast.13, f32[4,1024,128]{2,1,0:T(8,128)S(1)} %shard_map.96.vectors), custom_call_target="tpu_custom_call" | custom-call | flops 1000000 | bytes 3000000 | tf_op jit(solution)/shard_map/pallas_call | solution.py:670
  (1 shorter events, 0.0 us)
Async XLA Ops:
  1.3 1.0 copy-start.3
  3.4 27.0 %copy-start.1 = (f32[8,128,128]{2,1,0:T(8,128)}, f32[8,128,128]{2,1,0:T(8,128)S(1)}, u32[]{:S(2)}) copy-start(f32[8,128,128]{2,1,0:T(8,128)S(1)} %get-tuple-element.33.own) | copy-start | bytes 1572868
  3.4 10.7 %collective-permute-start = (f32[5,128,128]{2,1,0:T(8,128)}, f32[5,128,128]{2,1,0:T(8,128)S(1)}, u32[]{:S(2)}, u32[]{:S(2)}) collective-permute-start(f32[5,128,128]{2,1,0:T(8,128)} %get-tuple-element.29), channel_id=1, source_target_pairs={{0,8},{8,16},{16,24},{24,32},{32,40},{40,48},{48,56},{56,64},{64,7... | collective-permute-start | bytes 983048 | tf_op jit(solution)/shard_map/ppermute | solution.py:620
  7.9 8.7 %collective-permute-start.1 = (f32[5,128,128]{2,1,0:T(8,128)}, f32[5,128,128]{2,1,0:T(8,128)}, u32[]{:S(2)}, u32[]{:S(2)}) collective-permute-start(f32[5,128,128]{2,1,0:T(8,128)} %get-tuple-element.30), channel_id=1, source_target_pairs={{8,0},{16,8},{24,16},{32,24},{40,32},{48,40},{56,48},{64,56},{72,6... | collective-permute-start | bytes 983048 | tf_op jit(solution)/shard_map/ppermute | solution.py:621
  14.1 16.3 %copy-start.2 = (f32[5,128,128]{2,1,0:T(8,128)}, f32[5,128,128]{2,1,0:T(8,128)S(1)}, u32[]{:S(2)}) copy-start(f32[5,128,128]{2,1,0:T(8,128)S(1)} %collective-permute-done.below) | copy-start | bytes 983044
  16.6 13.0 %copy-start.7 = (s32[9]{0:T(128)S(1)}, s32[9]{0:T(128)}, u32[]{:S(2)}) copy-start(s32[9]{0:T(128)} %constant.21.clone) | copy-start | bytes 112
  16.6 13.0 %copy-start.6 = (s32[128,128]{1,0:T(8,128)S(1)}, s32[128,128]{1,0:T(8,128)}, u32[]{:S(2)}) copy-start(s32[128,128]{1,0:T(8,128)} %param.12) | copy-start | bytes 196612
  16.6 48.4 %all-to-all-start = ((f32[128,40,128]{2,1,0:T(8,128)}), f32[128,40,128]{2,1,0:T(8,128)}, u32[]{:S(2)}, u32[]{:S(2)}) async-start(f32[128,40,128]{2,1,0:T(8,128)} %bitcast.14), calls=%async_computation | async-start | bytes 5242880 | tf_op jit(solution)/shard_map/all_to_all | solution.py:633
  32.0 24.3 %collective-permute-start.2 = (f32[18,8,128]{2,1,0:T(8,128)}, f32[18,8,128]{2,1,0:T(8,128)S(1)}, u32[]{:S(2)}, u32[]{:S(2)}) collective-permute-start(f32[18,8,128]{2,1,0:T(8,128)} %get-tuple-element.35), channel_id=1, source_target_pairs={{0,1},{1,2},{2,3},{3,4},{4,5},{5,6},{6,7},{8,9},{9,10},{10,11},{11... | collective-permute-start | bytes 221192 | tf_op jit(solution)/shard_map/ppermute | solution.py:644
  35.4 21.8 %collective-permute-start.3 = (f32[18,8,128]{2,1,0:T(8,128)S(1)}, f32[18,8,128]{2,1,0:T(8,128)S(1)}, u32[]{:S(2)}, u32[]{:S(2)}) collective-permute-start(f32[18,8,128]{2,1,0:T(8,128)S(1)} %get-tuple-element.36), channel_id=1, source_target_pairs={{1,0},{2,1},{3,2},{4,3},{5,4},{6,5},{7,6},{9,8},{10,9},{11,10},{12... | collective-permute-start | bytes 221192 | tf_op jit(solution)/shard_map/ppermute | solution.py:645
  56.3 8.7 %copy-start.4 = (f32[18,8,128]{2,1,0:T(8,128)}, f32[18,8,128]{2,1,0:T(8,128)S(1)}, u32[]{:S(2)}) copy-start(f32[18,8,128]{2,1,0:T(8,128)S(1)} %collective-permute-done.2.y_low) | copy-start | bytes 221188
  57.1 7.9 %copy-start.5 = (f32[18,8,128]{2,1,0:T(8,128)}, f32[18,8,128]{2,1,0:T(8,128)S(1)}, u32[]{:S(2)}) copy-start(f32[18,8,128]{2,1,0:T(8,128)S(1)} %collective-permute-done.3.y_high) | copy-start | bytes 221188
  90.9 15.7 %all-to-all-start.1 = ((f32[128,1,128]{2,1,0:T(1,128)}), f32[128,1,128]{2,1,0:T(1,128)S(1)}, u32[]{:S(2)}, u32[]{:S(2)}) async-start(f32[128,1,128]{2,1,0:T(1,128)} %bitcast.15), calls=%async_computation.1 | async-start | bytes 131072 | tf_op jit(solution)/shard_map/all_to_all | solution.py:668
  97.0 1.6 %copy-start = (f32[4,8,128,128]{3,2,1,0:T(8,128)S(1)}, f32[4,8,128,128]{3,2,1,0:T(8,128)}, u32[]{:S(2)}) copy-start(f32[4,8,128,128]{3,2,1,0:T(8,128)} %get-tuple-element.46.kept) | copy-start | bytes 6291460

commit v4 on v3

--- a/solution.py
+++ b/solution.py
@@ -36,17 +36,22 @@
     return lax.broadcasted_iota(jnp.int32, shape, axis)
 
 
-def loop(count, body):
-    lax.fori_loop(0, count, lambda i, c: (body(i), c)[1], 0)
+def loop(count, body, unroll=1):
+    def several(i, carry):
+        for k in range(unroll):
+            body(unroll * i + k)
+        return carry
+
+    lax.fori_loop(0, count // unroll, several, 0)
 
 
 def pack_kernel(slot_of, head, old, packed, out, edge, sem):
     sub = iota((8, 128), 0)
 
     def brick(b):
-        own = slot_of[b]
-        below = slot_of[jnp.maximum(b - 8, 0)]
-        above = slot_of[jnp.minimum(b + 8, 127)]
+        own = slot_of[0, b]
+        below = slot_of[0, jnp.maximum(b - 8, 0)]
+        above = slot_of[0, jnp.minimum(b + 8, 127)]
         head_below, head_above = head[below], head[above]
         old_below, old_above = old[below], old[above]
 
@@ -59,35 +64,33 @@
         put(3, jnp.where(sub < 3, old_above, jnp.where(sub < 5, head_above, old_below)))
         put(4, jnp.where(sub == 3, old_above, old_below))
 
-    def four(i):
-        for k in range(4):
-            brick(4 * i + k)
-
-    loop(32, four)
+    loop(128, brick, 8)
     lane = iota((128, 128), 1)
+    low = lane % 16 < 8
     edge[0:16, :] = jnp.full((16, 128), -1.0, jnp.float32)
     edge[144:160, :] = jnp.full((16, 128), -1.0, jnp.float32)
     for field, (y_row, corner_row) in enumerate(((32, 34), (33, 37))):
         columns = jnp.zeros((128, 128), jnp.float32)
         for x in range(8):
             rows = out[pl.ds(8 * field + x, 128, stride=PIECE), :]
-            low = pltpu.roll(rows, (8 * x + 8) % 128, 1)
-            high = pltpu.roll(rows, 64 + 8 * x, 1)
-            columns = jnp.where((lane >= 8 * x) & (lane < 8 * x + 8), low, columns)
-            columns = jnp.where((lane >= 64 + 8 * x) & (lane < 72 + 8 * x), high, columns)
+            columns = jnp.where(lane // 16 == x, pltpu.roll(rows, 16 * x + 8, 1), columns)
         edge[16:144, :] = columns
-        out[pl.ds(y_row, 128, stride=PIECE), :] = jnp.where(lane < 64, edge[15:143, :], edge[17:145, :])
+        out[pl.ds(y_row, 128, stride=PIECE), :] = jnp.where(low, edge[15:143, :], edge[17:145, :])
         out[pl.ds(corner_row, 128, stride=PIECE), :] = jnp.where(
             lane < 64,
-            jnp.where(lane < 32, edge[23:151, :], edge[7:135, :]),
-            jnp.where(lane < 96, edge[25:153, :], edge[9:137, :]),
+            jnp.where(low, edge[23:151, :], edge[25:153, :]),
+            jnp.where(low, edge[7:135, :], edge[9:137, :]),
         )
     copy = pltpu.make_async_copy(out, packed, sem)
     copy.start()
     copy.wait()
 
 
-def turn_ids_kernel(ids, out, first, last):
+def turn_ids_kernel(block_map, ids, slot_of, out, first, last):
+    row = jnp.broadcast_to(block_map[pl.ds(lax.axis_index(AXES), 1), :], (128, 128))
+    match = row == iota((128, 128), 0)
+    slot = jnp.sum(jnp.where(match, iota((128, 128), 1), 0).astype(jnp.float32), axis=1, keepdims=True)
+    slot_of[...] = jnp.broadcast_to(slot, (128, 128)).T[0:8].astype(jnp.int32)
     for x in range(8):
         plane = ids[pl.ds(x, 128, stride=8), :].astype(jnp.float32).T
         out[x] = plane
@@ -124,26 +127,26 @@
     return [jnp.take_along_axis(table, index, axis=1) for table in tables]
 
 
-def harmonic(a, b):
-    return 2.0 * a * b / (a + b)
+def half_mean(a, b):
+    return a * b / (a + b)
 
 
 def upward_faces(kz):
-    return jnp.where(iota(kz.shape, 1) < 127, harmonic(kz, pltpu.roll(kz, 127, 1)), 0.0)
-
-
-def x_inside(place, xi):
-    x = place[0] * 8 - DEPTH + xi
-    return jnp.where((x >= 0) & (x + 1 < place[2] * 8), 1.0, 0.0)
-
-
-def y_inside(place, shape, first):
-    y = place[1] * 128 - 8 + first + iota(shape, 0)
-    return (y >= 0) & (y + 1 < place[3] * 128)
+    return jnp.where(iota(kz.shape, 1) < 127, half_mean(kz, pltpu.roll(kz, 127, 1)), 0.0)
+
+
+def x_inside(xi):
+    x = lax.axis_index("gx") * 8 - DEPTH + xi
+    return jnp.where((x >= 0) & (x + 1 < lax.axis_size("gx") * 8), 1.0, 0.0)
+
+
+def y_inside(shape, first):
+    y = lax.axis_index("gy") * 128 - 8 + first + iota(shape, 0)
+    return (y >= 0) & (y + 1 < lax.axis_size("gy") * 128)
 
 
 def properties_kernel(
-    place, conductivity, vg_alpha, vg_n, capacity, below, own, above,
+    conductivity, vg_alpha, vg_n, capacity, below, own, above,
     out_a, out_n, out_m, out_c, out_x, out_y, out_z, out_e,
     alpha, expo, exponent, cap, trans_x, trans_y, trans_z, edges, cond_x, cond_y, sems,
 ):
@@ -175,13 +178,13 @@
         copy.start()
 
     def faces(xi):
-        inside = x_inside(place, xi)
+        inside = x_inside(xi)
         above_xi = jnp.minimum(xi + 1, EX - 1)
         for c in range(4):
             at = slice(32 * c, 32 * c + 32)
-            trans_x[xi, at, :] = inside * harmonic(cond_x[xi, at, :], cond_x[above_xi, at, :])
+            trans_x[xi, at, :] = inside * half_mean(cond_x[xi, at, :], cond_x[above_xi, at, :])
             up = slice(32 * c + 1, 32 * c + 33)
-            trans_y[xi, at, :] = harmonic(cond_y[xi, at, :], cond_y[xi, up, :])
+            trans_y[xi, at, :] = half_mean(cond_y[xi, at, :], cond_y[xi, up, :])
 
     loop(EX, faces)
     for copy in copies(4, 8):
@@ -268,7 +271,7 @@
 
 
 def main_kernel(
-    source, place, conductivity, vg_alpha, vg_n, capacity,
+    source, conductivity, vg_alpha, vg_n, capacity,
     recv, y_low, y_high, edges, in_a, in_n, in_m, in_c, in_x, in_y, in_z, kept, sums,
     alpha, expo, exponent, cap, trans_x, trans_y, trans_z, sems, ordered, head, old, rel, d_rel, own_c, cxp, cxm, cyp, cym, czp, czm, k0, k1, k2, k3, k4,
     side_x, side_y,
@@ -286,6 +289,8 @@
     for copy in copies:
         copy.start()
 
+    low = lane % 16 < 8
+
     def layer(z):
         def tile(k, t):
             return recv[pl.ds(pl.multiple_of(source[k, z] * PIECE + 8 * t, 8), 8), :]
@@ -297,11 +302,9 @@
         put(1, tile(0, 1))
         put(2, jnp.where(sub >= 3, tile(1, 2), tile(2, 2)))
         put(3, jnp.where(sub < 5, tile(2, 3), tile(1, 3)))
-        sides = jnp.where(lane < 64, tile(3, 4), tile(4, 4))
+        sides = jnp.where(low, tile(3, 4), tile(4, 4))
         corners = jnp.where(
-            lane < 64,
-            jnp.where(lane < 32, tile(5, 4), tile(6, 4)),
-            jnp.where(lane < 96, tile(7, 4), tile(8, 4)),
+            lane < 64, jnp.where(low, tile(5, 4), tile(7, 4)), jnp.where(low, tile(6, 4), tile(8, 4))
         )
         put(
             4,
@@ -310,11 +313,7 @@
             ),
         )
 
-    def two_layers(i):
-        layer(2 * i)
-        layer(2 * i + 1)
-
-    loop(64, two_layers)
+    loop(128, layer, 4)
 
     def plane(r):
         return ordered[pl.ds(r, 128, stride=PIECE), :].T
@@ -326,14 +325,13 @@
     for field, (y_row, corner_row) in ((head, (32, 34)), (old, (33, 37))):
         sides = plane(y_row)
         for x in range(8):
-            field[5 + x, 8:16, :] = sides[8 * x : 8 * x + 8]
-            field[5 + x, 144:152, :] = sides[64 + 8 * x : 72 + 8 * x]
+            field[5 + x, 8:16, :] = sides[16 * x : 16 * x + 8]
+            field[5 + x, 144:152, :] = sides[16 * x + 8 : 16 * x + 16]
         corners = plane(corner_row)
-        for k in range(4):
-            field[13 + k, 8:16, :] = corners[8 * k : 8 * k + 8]
-            field[1 + k, 8:16, :] = corners[32 + 8 * k : 40 + 8 * k]
-            field[13 + k, 144:152, :] = corners[64 + 8 * k : 72 + 8 * k]
-            field[1 + k, 144:152, :] = corners[96 + 8 * k : 104 + 8 * k]
+        for x in range(8):
+            xi = 13 + x if x < 4 else x - 3
+            field[xi, 8:16, :] = corners[16 * x : 16 * x + 8]
+            field[xi, 144:152, :] = corners[16 * x + 8 : 16 * x + 16]
     for xi in (0, 17):
         head[xi, 8:16, :] = jnp.full((8, 128), -1.0, jnp.float32)
         head[xi, 144:152, :] = jnp.full((8, 128), -1.0, jnp.float32)
@@ -366,29 +364,46 @@
         side_y[xi, 16:24, :] = edges[xi, 0]
         side_y[xi, 136:144, :] = edges[xi, 1]
 
-    loop(EX, side_rows)
-    for copy in copies:
+    loop(EX, side_rows, 3)
+    for copy in copies[:4]:
         copy.wait()
+    loop(EX, curves, 2)
+    for copy in copies[4:]:
+        copy.wait()
 
     def side_faces(xi):
-        pair = x_inside(place, xi) * harmonic(side_x[xi], side_x[jnp.minimum(xi + 1, EX - 1)])
+        pair = x_inside(xi) * half_mean(side_x[xi], side_x[jnp.minimum(xi + 1, EX - 1)])
         trans_x[xi, 0:8, :] = pair[0:8]
         trans_x[xi, 136:144, :] = pair[8:16]
         for first, last in ((8, 16), (136, 152)):
             here = slice(first, last)
-            value = harmonic(side_y[xi, here, :], side_y[xi, first + 1 : last + 1, :])
-            trans_y[xi, here, :] = jnp.where(y_inside(place, value.shape, first - 8), value, 0.0)
-
-    loop(EX, side_faces)
-    loop(EX, curves)
-
-    def face(t, h_a, h_b, r_a, r_b, d_a, d_b, rise):
+            value = half_mean(side_y[xi, here, :], side_y[xi, first + 1 : last + 1, :])
+            trans_y[xi, here, :] = jnp.where(y_inside(value.shape, first - 8), value, 0.0)
+
+    loop(EX, side_faces, 3)
+
+    def face(half, h_a, h_b, r_a, r_b, d_a, d_b, rise):
         potential = h_b - h_a
         if rise:
             potential = potential + rise
-        along = t * (0.5 * (r_a + r_b))
-        slope = (0.5 * t) * potential
-        return along, slope, along * potential, slope * (d_a + d_b)
+        along = half * (r_a + r_b)
+        slope = half * potential
+        return along + slope * d_b, along - slope * d_a, along * potential, slope * (d_a + d_b)
+
+    def x_faces(xi, to, at, h, r, d):
+        c_p, c_m, flux, both = face(
+            trans_x[xi, at, :], h, head[xi + 1, to, :], r, rel[xi + 1, to, :], d, d_rel[xi + 1, to, :], 0.0
+        )
+        cxp[xi, to, :] = c_p
+        cxm[xi + 1, to, :] = c_m
+        k1[xi, to, :] = flux
+        k2[xi, to, :] = both
+        return flux, both
+
+    for c in range(CHUNKS):
+        at = slice(CHUNK * c, CHUNK * (c + 1))
+        to = slice(8 + CHUNK * c, 8 + CHUNK * (c + 1))
+        x_faces(0, to, at, head[0, to, :], rel[0, to, :], d_rel[0, to, :])
 
     def coefficients(i):
         xi = i + 1
@@ -401,35 +416,27 @@
             old_sat = jnp.exp(exponent[xi, at, :] * log_old)
             start = cap[xi, at, :] * (old_sat - k0[xi, to, :])
             h, r, d = head[xi, to, :], rel[xi, to, :], d_rel[xi, to, :]
-            centre = own_c[xi, to, :]
-            around = (
-                (
-                    trans_x[xi, at, :], trans_x[xi - 1, at, :], 0.0, cxp, cxm,
-                    [f[xi + 1, to, :] for f in (head, rel, d_rel)],
-                    [f[xi - 1, to, :] for f in (head, rel, d_rel)],
-                ),
-                (
-                    trans_y[xi, to, :], trans_y[xi, down, :], 0.0, cyp, cym,
-                    [f[xi, up, :] for f in (head, rel, d_rel)],
-                    [f[xi, down, :] for f in (head, rel, d_rel)],
-                ),
-                (
-                    trans_z[xi, at, :], pltpu.roll(trans_z[xi, at, :], 1, 1), 1.0, czp, czm,
-                    [pltpu.roll(f, 127, 1) for f in (h, r, d)],
-                    [pltpu.roll(f, 1, 1) for f in (h, r, d)],
-                ),
+            flux, both = x_faces(xi, to, at, h, r, d)
+            start = start + (flux - k1[xi - 1, to, :])
+            centre = own_c[xi, to, :] - (both - k2[xi - 1, to, :])
+            c_p, c_m, flux, both = face(
+                trans_y[xi, to, :], h, head[xi, up, :], r, rel[xi, up, :], d, d_rel[xi, up, :], 0.0
             )
-            for t_p, t_m, rise, c_p, c_m, (h_p, r_p, d_p), (h_m, r_m, d_m) in around:
-                along, slope, flux, both = face(t_p, h, h_p, r, r_p, d, d_p, rise)
-                along_m, slope_m, flux_m, both_m = face(t_m, h_m, h, r_m, r, d_m, d, rise)
-                c_p[xi, to, :] = along + slope * d_p
-                c_m[xi, to, :] = along_m - slope_m * d_m
-                start = start + (flux - flux_m)
-                centre = centre - (both - both_m)
-            own_c[xi, to, :] = centre
-            k0[xi, to, :] = start
-
-    loop(16, coefficients)
+            cyp[xi, to, :] = c_p
+            cym[xi, up, :] = c_m
+            k3[xi, to, :] = flux
+            k4[xi, to, :] = both
+            start = start + (flux - k3[xi, down, :])
+            centre = centre - (both - k4[xi, down, :])
+            c_p, c_m, flux, both = face(
+                trans_z[xi, at, :], h, pltpu.roll(h, 127, 1), r, pltpu.roll(r, 127, 1), d, pltpu.roll(d, 127, 1), 1.0
+            )
+            czp[xi, to, :] = c_p
+            czm[xi, to, :] = pltpu.roll(c_m, 1, 1)
+            own_c[xi, to, :] = centre - (both - pltpu.roll(both, 1, 1))
+            k0[xi, to, :] = start + (flux - pltpu.roll(flux, 1, 1))
+
+    loop(16, coefficients, 2)
 
     vectors = (k0, k1, k2, k3, k4)
     for step in range(4):
@@ -451,7 +458,7 @@
                 w = w + czm[xi, to, :] * (v - pltpu.roll(v, 1, 1))
                 w_ref[xi, to, :] = w
 
-        loop(14 - 2 * step, apply)
+        loop(14 - 2 * step, apply, 7 - step)
 
     keeps = [
         pltpu.make_async_copy(vectors[k].at[5:13, 16:144, :], kept.at[k], sems.at[7 + k]) for k in range(4)
@@ -602,21 +609,23 @@
 def body(held_head, held_head_old, material_ids, block_map, conductivity, vg_alpha, vg_n, capacity):
     count_x, count_y = lax.axis_size("gx"), lax.axis_size("gy")
     devices = count_x * count_y
-    at_x, at_y = lax.axis_index("gx"), lax.axis_index("gy")
-    own_index = at_x * count_y + at_y
+    own_index = lax.axis_index(AXES)
     numbers = jnp.arange(devices, dtype=jnp.int32)
-    own_row = block_map[own_index]
-    slot_of = jnp.sum(jnp.where(own_row[None, :] == numbers[:, None], numbers[None, :], 0), axis=1)
     scratch = lambda *shape: pltpu.VMEM(shape, jnp.float32)
 
     up_x = [(i, i + 1) for i in range(count_x - 1)]
     down_x = [(i + 1, i) for i in range(count_x - 1)]
     up_y = [(i, i + 1) for i in range(count_y - 1)]
     down_y = [(i + 1, i) for i in range(count_y - 1)]
-    ids, first, last = call(
-        turn_ids_kernel, [f32(8, 128, 128)] + [f32(DEPTH, 128, 128)] * 2, [VMEM], [VMEM] * 3, [], 8, (10**6, 10**6)
-    )(material_ids.reshape(1024, 128))
-    slot_of, first, last = lax.optimization_barrier((slot_of, first, last))
+    slot_of, ids, first, last = call(
+        turn_ids_kernel,
+        [jax.ShapeDtypeStruct((8, 128), jnp.int32), f32(8, 128, 128)] + [f32(DEPTH, 128, 128)] * 2,
+        [VMEM, VMEM],
+        [VMEM] * 4,
+        [],
+        63,
+        (10**6, 10**6),
+    )(block_map, material_ids.reshape(1024, 128))
     below = lax.ppermute(last, "gx", up_x)
     above = lax.ppermute(first, "gx", down_x)
 
@@ -637,7 +646,6 @@
     source = jnp.sum(
         jnp.where(block_map[None] == bricks[:, None, None], numbers[None, :, None], 0), axis=1
     )
-    place = jnp.stack([at_x, at_y, jnp.int32(count_x), jnp.int32(count_y)])
     first, last = call(
         edge_ids_kernel, [f32(EX, 8, 128)] * 2, [VMEM] * 3, [VMEM] * 2, [], 8, (10**5, 10**6)
     )(below, ids, above)
@@ -646,25 +654,25 @@
     *fields, edges = call(
         properties_kernel,
         [f32(EX, 128, 128)] * 7 + [f32(EX, 2, 8, 128)],
-        [SMEM] * 5 + [VMEM] * 3,
+        [SMEM] * 4 + [VMEM] * 3,
         [HBM] * 8,
         [scratch(EX, 128, 128)] * 7 + [scratch(EX, 2, 8, 128), scratch(EX, 128, 128), scratch(EX, 136, 128)]
         + [pltpu.SemaphoreType.DMA((8,))],
         63,
         (40 * 10**6, 12 * 10**6),
-    )(place, conductivity, vg_alpha, vg_n, capacity, below, ids, above)
+    )(conductivity, vg_alpha, vg_n, capacity, below, ids, above)
 
     kept, sums = call(
         main_kernel,
         [f32(4, 8, 128, 128), f32(devices, 128)],
-        [SMEM] * 6 + [VMEM] * 4 + [HBM] * 7,
+        [SMEM] * 5 + [VMEM] * 4 + [HBM] * 7,
         [HBM, VMEM],
         [scratch(EX, EY, 128)] * 5 + [scratch(EX, PY, 128), scratch(EX, EY, 128)]
         + [pltpu.SemaphoreType.DMA((11,)), scratch(devices * PIECE, 128)] + [scratch(EX, PY, 128)] * 16
         + [scratch(EX, 16, 128), scratch(EX, PY, 128)],
         63,
         (200 * 10**6, 16 * 10**6),
-    )(source, place, conductivity, vg_alpha, vg_n, capacity, arrived, y_low, y_high, edges, *fields)
+    )(source, conductivity, vg_alpha, vg_n, capacity, arrived, y_low, y_high, edges, *fields)
     gathered = lax.all_to_all(sums.reshape(devices, 1, 128), AXES, split_axis=0, concat_axis=0, tiled=True)
     turned = call(turn_back_kernel, f32(4, 1024, 128), [VMEM], VMEM, [], 8, (10**6, 4 * 10**6))(kept)
     update = call(finish_kernel, f32(1024, 128), [VMEM] * 2, VMEM, [], 8, (10**6, 3 * 10**6))(

time: 109 us -> 105 us (0.963)
  Pallas kernels: 46.4 us -> 42.9 us
  waiting for transfers between devices: 26.7 us -> 28.4 us
  other arithmetic: 1.97 us -> 0.74 us
    pallas_call x2, Pallas kernels: 26.8 us -> 24.8 us  [the longest x1 22.4 us: body(): call(main_kernel, [f32(4, 8, 128, 128), f32(devices, 128)], [SMEM] * 5 +...]
    ppermute x1, waiting for transfers between devices: 8.04 us -> 9.55 us  [body(): y_low = lax.ppermute(last, 'gy', up_y)]
    unnamed x16 -> x18, local copies, waits for them, and re-layouts: 2.65 us -> 2.34 us
  transfers between devices with their start and end apart: 6 -> 6, of which waited for: 5 -> 5; matrix products, arithmetic and copies ran while one was open for 1% -> 1% of each run, Pallas kernels for 16% -> 15%
where the time goes in v4:
time: 105 us
  Pallas kernels  42.9 us (41%)
  starting transfers between devices  30.2 us (29%)
  waiting for transfers between devices  28.4 us (27%)
  local copies, waits for them, and re-layouts  2.34 us (2%)
    pallas_call x1, Pallas kernels, body(): call(main_kernel, [f32(4, 8, 128, 128), f32(devices, 128)], [SMEM] * 5 +...  22.4 us
    all_to_all x1, starting transfers between devices, body(): lax.all_to_all(packed, AXES, split_axis=0, concat_axis=0, tiled=True)  13 us
    pallas_call x1, Pallas kernels, body(): call(properties_kernel, [f32(EX, 128, 128)] * 7 + [f32(EX, 2, 8, 128)], [...  11 us
    ppermute x1, waiting for transfers between devices, body(): y_low = lax.ppermute(last, 'gy', up_y)  9.55 us
    all_to_all x1, waiting for transfers between devices, body(): lax.all_to_all(packed, AXES, split_axis=0, concat_axis=0, tiled=True)  7.89 us
    all_to_all x1, waiting for transfers between devices, body(): lax.all_to_all(sums.reshape(devices, 1, 128), AXES, split_axis=0, concat_...  7.35 us
    all_to_all x1, starting transfers between devices, body(): lax.all_to_all(sums.reshape(devices, 1, 128), AXES, split_axis=0, concat_...  6.13 us
    ppermute x1, starting transfers between devices, body(): below = lax.ppermute(last, 'gx', up_x)  4.5 us
  transfers between devices with their start and end apart: 6, of which 5 were waited for; matrix products, arithmetic and copies ran while one was open for 1% of the time, Pallas kernels for 15%

profile of v4, /device:TPU:1, one launch (start us, length us, event | category | flops | bytes accessed | tf_op | source)
XLA Modules:
  0.0 104.8 jit_solution(5233544256736319252)
XLA Ops:
  0.0 2.4 %shard_map.91 = (s32[8,128]{1,0:T(8,128)}, f32[8,128,128]{2,1,0:T(8,128)}, f32[5,128,128]{2,1,0:T(8,128)}, f32[5,128,128]{2,1,0:T(8,128)}) custom-call(s32[128,128]{1,0:T(8,128)} %block_map.1, s32[1024,128]{1,0:T(8,128)} %bitcast.10), custom_call_target="tpu_custom_call" | custom-call | flops 1000000 | bytes 1000000 | tf_op jit(solution)/shard_map/pallas_call | solution.py:620
  2.4 4.5 %collective-permute-start = (f32[5,128,128]{2,1,0:T(8,128)}, f32[5,128,128]{2,1,0:T(8,128)S(1)}, u32[]{:S(2)}, u32[]{:S(2)}) collective-permute-start(f32[5,128,128]{2,1,0:T(8,128)} %get-tuple-element.25), channel_id=1, source_target_pairs={{0,8},{8,16},{16,24},{24,32},{32,40},{40,48},{48,56},{56,64},{64,7... | collective-permute-start | bytes 983048 | tf_op jit(solution)/shard_map/ppermute | solution.py:629
  6.9 1.9 %collective-permute-start.1 = (f32[5,128,128]{2,1,0:T(8,128)}, f32[5,128,128]{2,1,0:T(8,128)S(1)}, u32[]{:S(2)}, u32[]{:S(2)}) collective-permute-start(f32[5,128,128]{2,1,0:T(8,128)} %get-tuple-element.26), channel_id=1, source_target_pairs={{8,0},{16,8},{24,16},{32,24},{40,32},{48,40},{56,48},{64,56},{72,6... | collective-permute-start | bytes 983048 | tf_op jit(solution)/shard_map/ppermute | solution.py:630
  8.8 3.9 %shard_map.92 = f32[5120,128]{1,0:T(8,128)} custom-call(s32[8,128]{1,0:T(8,128)} %get-tuple-element.24.slot_of, f32[128,8,128]{2,1,0:T(8,128)} %head.1, f32[128,8,128]{2,1,0:T(8,128)} %old.1), custom_call_target="tpu_custom_call" | custom-call | flops 1000000 | bytes 4000000 | tf_op jit(solution)/shard_map/pallas_call | solution.py:632
  12.7 0.0 collective-permute-done.below
  12.7 0.0 copy-start.2
  12.7 2.8 %collective-permute-done.1.above = f32[5,128,128]{2,1,0:T(8,128)S(1)} collective-permute-done((f32[5,128,128]{2,1,0:T(8,128)}, f32[5,128,128]{2,1,0:T(8,128)S(1)}, u32[]{:S(2)}, u32[]{:S(2)}) %collective-permute-start.1) | collective-permute-done | bytes 327712 | tf_op jit(solution)/shard_map/ppermute | solution.py:630
  15.5 0.0 copy-start.3
  15.5 0.7 copy-done.3
  16.2 0.0 copy-start.8
  16.2 0.0 copy-start
  16.2 0.0 copy-start.4
  16.2 13.0 %all-to-all-start = ((f32[128,40,128]{2,1,0:T(8,128)}), f32[128,40,128]{2,1,0:T(8,128)}, u32[]{:S(2)}, u32[]{:S(2)}) async-start(f32[128,40,128]{2,1,0:T(8,128)} %bitcast.9), calls=%async_computation | async-start | bytes 5242880 | tf_op jit(solution)/shard_map/all_to_all | solution.py:642
  29.2 0.0 copy-start.5
  29.2 0.0 copy-done.8
  29.2 0.0 copy-done.2
  29.2 0.0 copy-done
  29.2 0.0 copy-done.4
  29.3 0.6 shard_map.93
  29.9 3.4 %collective-permute-start.2 = (f32[18,8,128]{2,1,0:T(8,128)}, f32[18,8,128]{2,1,0:T(8,128)S(1)}, u32[]{:S(2)}, u32[]{:S(2)}) collective-permute-start(f32[18,8,128]{2,1,0:T(8,128)} %get-tuple-element.31), channel_id=1, source_target_pairs={{0,1},{1,2},{2,3},{3,4},{4,5},{5,6},{6,7},{8,9},{9,10},{10,11},{11... | collective-permute-start | bytes 221192 | tf_op jit(solution)/shard_map/ppermute | solution.py:652
  33.3 1.3 %collective-permute-start.3 = (f32[18,8,128]{2,1,0:T(8,128)S(1)}, f32[18,8,128]{2,1,0:T(8,128)S(1)}, u32[]{:S(2)}, u32[]{:S(2)}) collective-permute-start(f32[18,8,128]{2,1,0:T(8,128)S(1)} %get-tuple-element.32), channel_id=1, source_target_pairs={{1,0},{2,1},{3,2},{4,3},{5,4},{6,5},{7,6},{9,8},{10,9},{11,10},{12... | collective-permute-start | bytes 221192 | tf_op jit(solution)/shard_map/ppermute | solution.py:653
  34.6 0.0 copy-done.5
  34.6 0.7 select_reduce_fusion.source
  35.3 11.0 %shard_map.94 = (f32[18,128,128]{2,1,0:T(8,128)}, f32[18,128,128]{2,1,0:T(8,128)}, f32[18,128,128]{2,1,0:T(8,128)}, f32[18,128,128]{2,1,0:T(8,128)}, f32[18,128,...) custom-call(f32[3,16]{1,0:T(4,128)} %conductivity.3, ...), custom_call_target="tpu_custom_call" | custom-call | flops 40000000 | bytes 12000000 | tf_op jit(solution)/shard_map/pallas_call | solution.py:654
  46.3 9.5 %collective-permute-done.2.y_low = f32[18,8,128]{2,1,0:T(8,128)S(1)} collective-permute-done((f32[18,8,128]{2,1,0:T(8,128)}, f32[18,8,128]{2,1,0:T(8,128)S(1)}, u32[]{:S(2)}, u32[]{:S(2)}) %collective-permute-start.2) | collective-permute-done | bytes 73760 | tf_op jit(solution)/shard_map/ppermute | solution.py:652
  55.9 0.0 copy-start.6
  55.9 0.8 collective-permute-done.3.y_high
  56.7 0.0 copy-start.7
  56.7 7.9 %all-to-all-done = f32[128,40,128]{2,1,0:T(8,128)} async-done(((f32[128,40,128]{2,1,0:T(8,128)}), f32[128,40,128]{2,1,0:T(8,128)}, u32[]{:S(2)}, u32[]{:S(2)}) %all-to-all-start) | async-done | bytes 2621472 | tf_op jit(solution)/shard_map/all_to_all | solution.py:642
  64.6 0.0 copy-done.6
  64.6 0.0 copy-done.7
  64.6 22.4 %shard_map.95 = (f32[4,8,128,128]{3,2,1,0:T(8,128)}, f32[128,128]{1,0:T(8,128)}) custom-call(s32[9,128]{1,0:T(8,128)} %select_reduce_fusion.source, f32[3,16]{1,0:T(4,128)} %conductivity.3, f32[16]{0:T(128)} %vg_alpha.3, f32[16]{0:T(128)} %vg_n.3, f32[16]{0:T(128)} %capacity.3, f32[5120,128]{1,0:T(8,128)} %bitcast.2.recv, f32[18,8,128]{2,1,0:T(8,128)} %copy-done.6, ...), custom_call_target="tpu_custom_call" | custom-call | flops 200000000 | bytes 16000000 | tf_op jit(solution)/shard_map/pallas_call | solution.py:665
  87.0 6.1 %all-to-all-start.1 = ((f32[128,1,128]{2,1,0:T(1,128)}), f32[128,1,128]{2,1,0:T(1,128)S(1)}, u32[]{:S(2)}, u32[]{:S(2)}) async-start(f32[128,1,128]{2,1,0:T(1,128)} %bitcast.11), calls=%async_computation.1 | async-start | bytes 131072 | tf_op jit(solution)/shard_map/all_to_all | solution.py:676
  93.2 0.0 copy-start.1
  93.2 1.6 %copy-done.1 = f32[4,8,128,128]{3,2,1,0:T(8,128)S(1)} copy-done((f32[4,8,128,128]{3,2,1,0:T(8,128)S(1)}, f32[4,8,128,128]{3,2,1,0:T(8,128)}, u32[]{:S(2)}) %copy-start.1) | copy-done | bytes 2097176
  94.8 0.6 shard_map.96.vectors
  95.4 7.4 %all-to-all-done.1 = f32[128,1,128]{2,1,0:T(1,128)S(1)} async-done(((f32[128,1,128]{2,1,0:T(1,128)}), f32[128,1,128]{2,1,0:T(1,128)S(1)}, u32[]{:S(2)}, u32[]{:S(2)}) %all-to-all-start.1) | async-done | bytes 65568 | tf_op jit(solution)/shard_map/all_to_all | solution.py:676
  102.7 2.1 %shard_map.97 = f32[1024,128]{1,0:T(8,128)} custom-call(f32[128,128]{1,0:T(8,128)S(1)} %bitcast.8, f32[4,1024,128]{2,1,0:T(8,128)S(1)} %shard_map.96.vectors), custom_call_target="tpu_custom_call" | custom-call | flops 1000000 | bytes 3000000 | tf_op jit(solution)/shard_map/pallas_call | solution.py:678
  (1 shorter events, 0.0 us)
Async XLA Ops:
  2.4 10.3 %collective-permute-start = (f32[5,128,128]{2,1,0:T(8,128)}, f32[5,128,128]{2,1,0:T(8,128)S(1)}, u32[]{:S(2)}, u32[]{:S(2)}) collective-permute-start(f32[5,128,128]{2,1,0:T(8,128)} %get-tuple-element.25), channel_id=1, source_target_pairs={{0,8},{8,16},{16,24},{24,32},{32,40},{40,48},{48,56},{56,64},{64,7... | collective-permute-start | bytes 983048 | tf_op jit(solution)/shard_map/ppermute | solution.py:629
  6.9 8.6 %collective-permute-start.1 = (f32[5,128,128]{2,1,0:T(8,128)}, f32[5,128,128]{2,1,0:T(8,128)S(1)}, u32[]{:S(2)}, u32[]{:S(2)}) collective-permute-start(f32[5,128,128]{2,1,0:T(8,128)} %get-tuple-element.26), channel_id=1, source_target_pairs={{8,0},{16,8},{24,16},{32,24},{40,32},{48,40},{56,48},{64,56},{72,6... | collective-permute-start | bytes 983048 | tf_op jit(solution)/shard_map/ppermute | solution.py:630
  12.7 16.5 %copy-start.2 = (f32[5,128,128]{2,1,0:T(8,128)}, f32[5,128,128]{2,1,0:T(8,128)S(1)}, u32[]{:S(2)}) copy-start(f32[5,128,128]{2,1,0:T(8,128)S(1)} %collective-permute-done.below) | copy-start | bytes 983044
  15.5 0.7 copy-start.3
  16.2 13.0 %copy-start.8 = (s32[9]{0:T(128)S(1)}, s32[9]{0:T(128)}, u32[]{:S(2)}) copy-start(s32[9]{0:T(128)} %constant.15.clone) | copy-start | bytes 112
  16.2 13.0 %copy-start = (f32[8,128,128]{2,1,0:T(8,128)S(1)}, f32[8,128,128]{2,1,0:T(8,128)}, u32[]{:S(2)}) copy-start(f32[8,128,128]{2,1,0:T(8,128)} %get-tuple-element.29.own) | copy-start | bytes 1572868
  16.2 13.0 %copy-start.4 = (f32[5,128,128]{2,1,0:T(8,128)S(1)}, f32[5,128,128]{2,1,0:T(8,128)}, u32[]{:S(2)}) copy-start(f32[5,128,128]{2,1,0:T(8,128)} %copy-done.3) | copy-start | bytes 983044
  16.2 48.4 %all-to-all-start = ((f32[128,40,128]{2,1,0:T(8,128)}), f32[128,40,128]{2,1,0:T(8,128)}, u32[]{:S(2)}, u32[]{:S(2)}) async-start(f32[128,40,128]{2,1,0:T(8,128)} %bitcast.9), calls=%async_computation | async-start | bytes 5242880 | tf_op jit(solution)/shard_map/all_to_all | solution.py:642
  29.2 5.4 %copy-start.5 = (s32[128,128]{1,0:T(8,128)S(1)}, s32[128,128]{1,0:T(8,128)}, u32[]{:S(2)}) copy-start(s32[128,128]{1,0:T(8,128)} %block_map.1) | copy-start | bytes 196612
  29.9 26.0 %collective-permute-start.2 = (f32[18,8,128]{2,1,0:T(8,128)}, f32[18,8,128]{2,1,0:T(8,128)S(1)}, u32[]{:S(2)}, u32[]{:S(2)}) collective-permute-start(f32[18,8,128]{2,1,0:T(8,128)} %get-tuple-element.31), channel_id=1, source_target_pairs={{0,1},{1,2},{2,3},{3,4},{4,5},{5,6},{6,7},{8,9},{9,10},{10,11},{11... | collective-permute-start | bytes 221192 | tf_op jit(solution)/shard_map/ppermute | solution.py:652
  33.3 23.4 %collective-permute-start.3 = (f32[18,8,128]{2,1,0:T(8,128)S(1)}, f32[18,8,128]{2,1,0:T(8,128)S(1)}, u32[]{:S(2)}, u32[]{:S(2)}) collective-permute-start(f32[18,8,128]{2,1,0:T(8,128)S(1)} %get-tuple-element.32), channel_id=1, source_target_pairs={{1,0},{2,1},{3,2},{4,3},{5,4},{6,5},{7,6},{9,8},{10,9},{11,10},{12... | collective-permute-start | bytes 221192 | tf_op jit(solution)/shard_map/ppermute | solution.py:653
  55.9 8.7 %copy-start.6 = (f32[18,8,128]{2,1,0:T(8,128)}, f32[18,8,128]{2,1,0:T(8,128)S(1)}, u32[]{:S(2)}) copy-start(f32[18,8,128]{2,1,0:T(8,128)S(1)} %collective-permute-done.2.y_low) | copy-start | bytes 221188
  56.7 7.9 %copy-start.7 = (f32[18,8,128]{2,1,0:T(8,128)}, f32[18,8,128]{2,1,0:T(8,128)S(1)}, u32[]{:S(2)}) copy-start(f32[18,8,128]{2,1,0:T(8,128)S(1)} %collective-permute-done.3.y_high) | copy-start | bytes 221188
  87.0 15.7 %all-to-all-start.1 = ((f32[128,1,128]{2,1,0:T(1,128)}), f32[128,1,128]{2,1,0:T(1,128)S(1)}, u32[]{:S(2)}, u32[]{:S(2)}) async-start(f32[128,1,128]{2,1,0:T(1,128)} %bitcast.11), calls=%async_computation.1 | async-start | bytes 131072 | tf_op jit(solution)/shard_map/all_to_all | solution.py:676
  93.2 1.6 %copy-start.1 = (f32[4,8,128,128]{3,2,1,0:T(8,128)S(1)}, f32[4,8,128,128]{3,2,1,0:T(8,128)}, u32[]{:S(2)}) copy-start(f32[4,8,128,128]{3,2,1,0:T(8,128)} %get-tuple-element.42.kept) | copy-start | bytes 6291460

commit v5 on v4

--- a/solution.py
+++ b/solution.py
@@ -86,25 +86,42 @@
     copy.wait()
 
 
-def turn_ids_kernel(block_map, ids, slot_of, out, first, last):
+def is_even():
+    return lax.axis_index("gx") % 2 == 0
+
+
+def turn_ids_kernel(block_map, ids, slot_of, inner, outer, turned):
     row = jnp.broadcast_to(block_map[pl.ds(lax.axis_index(AXES), 1), :], (128, 128))
     match = row == iota((128, 128), 0)
     slot = jnp.sum(jnp.where(match, iota((128, 128), 1), 0).astype(jnp.float32), axis=1, keepdims=True)
     slot_of[...] = jnp.broadcast_to(slot, (128, 128)).T[0:8].astype(jnp.int32)
     for x in range(8):
-        plane = ids[pl.ds(x, 128, stride=8), :].astype(jnp.float32).T
-        out[x] = plane
-        if x < DEPTH:
-            first[x] = plane
-        if x >= 8 - DEPTH:
-            last[x - 8 + DEPTH] = plane
-
-
-def edge_ids_kernel(below, own, above, first, last):
-    for k, part in ((0, below), (5, own), (13, above)):
-        for x in range(part.shape[0]):
-            first[k + x] = part[x, 0:8, :]
-            last[k + x] = part[x, 120:128, :]
+        turned[x] = ids[pl.ds(x, 128, stride=8), :].astype(jnp.float32).T
+    first = jnp.where(is_even(), 8 - DEPTH, 0)
+    for k in range(DEPTH):
+        inner[k] = turned[first + k]
+        outer[k] = turned[8 - DEPTH - first + k]
+
+
+def id_rows(inner, outer, inner_in, outer_in):
+    even = is_even()
+
+    def read(k, low, high, at):
+        return jnp.where(even, low[k, at, :], high[k, at, :])
+
+    return (
+        (0, DEPTH, lambda k, at: read(k, outer_in, inner_in, at)),
+        (DEPTH, DEPTH, lambda k, at: read(k, outer, inner, at)),
+        (2 * DEPTH, 8 - DEPTH, lambda k, at: read(k + 2 * DEPTH - 8, inner, outer, at)),
+        (8 + DEPTH, DEPTH, lambda k, at: read(k, inner_in, outer_in, at)),
+    )
+
+
+def edge_ids_kernel(inner, outer, inner_in, outer_in, first, last):
+    for start, count, read in id_rows(inner, outer, inner_in, outer_in):
+        for k in range(count):
+            first[start + k] = read(k, slice(0, 8))
+            last[start + k] = read(k, slice(120, 128))
 
 
 def tables_of(conductivity, vg_alpha, vg_n, capacity):
@@ -146,7 +163,7 @@
 
 
 def properties_kernel(
-    conductivity, vg_alpha, vg_n, capacity, below, own, above,
+    conductivity, vg_alpha, vg_n, capacity, inner, outer, inner_in, outer_in,
     out_a, out_n, out_m, out_c, out_x, out_y, out_z, out_e,
     alpha, expo, exponent, cap, trans_x, trans_y, trans_z, edges, cond_x, cond_y, sems,
 ):
@@ -157,10 +174,10 @@
 
     tables = tables_of(conductivity, vg_alpha, vg_n, capacity)
 
-    def fill_row(xi, source, x):
+    def fill_row(xi, read, k):
         for t in range(16):
             at = slice(8 * t, 8 * t + 8)
-            kx, ky, kz, a, n, c = lookup(tables, source[x, at, :])
+            kx, ky, kz, a, n, c = lookup(tables, read(k, at))
             alpha[xi, at, :] = a
             expo[xi, at, :] = n
             exponent[xi, at, :] = 1.0 - 1.0 / n
@@ -171,9 +188,8 @@
             if t in (0, 15):
                 edges[xi, t // 15] = ky
 
-    loop(5, lambda x: fill_row(x, below, x))
-    loop(8, lambda x: fill_row(x + 5, own, x))
-    loop(5, lambda x: fill_row(x + 13, above, x))
+    for start, count, read in id_rows(inner, outer, inner_in, outer_in):
+        loop(count, lambda k: fill_row(start + k, read, k))
     for copy in copies(0, 4):
         copy.start()
 
@@ -263,17 +279,13 @@
     q = a[0] / b[0]
     zero = jnp.zeros_like(q)
     r = df_add(a, df_neg(df_mul((q, zero), b)))
-    q2 = r[0] / b[0]
-    r = df_add(r, df_neg(df_mul((q2, zero), b)))
-    q3 = r[0] / b[0]
-    s, e = two_sum(q, q2)
-    return two_sum(s, e + q3)
+    return two_sum(q, r[0] / b[0])
 
 
 def main_kernel(
     source, conductivity, vg_alpha, vg_n, capacity,
-    recv, y_low, y_high, edges, in_a, in_n, in_m, in_c, in_x, in_y, in_z, kept, sums,
-    alpha, expo, exponent, cap, trans_x, trans_y, trans_z, sems, ordered, head, old, rel, d_rel, own_c, cxp, cxm, cyp, cym, czp, czm, k0, k1, k2, k3, k4,
+    arrived, y_low, y_high, edges, in_a, in_n, in_m, in_c, in_x, in_y, in_z, kept, sums,
+    recv, alpha, expo, exponent, cap, trans_x, trans_y, trans_z, sems, ordered, head, old, rel, d_rel, own_c, cxp, cxm, cyp, cym, czp, czm, k0, k1, k2, k3, k4,
     side_x, side_y,
 ):
     sub = iota((8, 128), 0)
@@ -286,10 +298,31 @@
         pltpu.make_async_copy(a, b.at[:, 16:144] if b is trans_y else b.at[:, 8:136], sems.at[k])
         for k, (a, b) in enumerate(refs)
     ]
+    arrival = pltpu.make_async_copy(arrived, recv, sems.at[11])
+    arrival.start()
     for copy in copies:
         copy.start()
 
     low = lane % 16 < 8
+
+    tables = tables_of(conductivity, vg_alpha, vg_n, capacity)
+
+    def side_rows(xi):
+        for source_ids, at in ((y_low, slice(0, 8)), (y_high, slice(136, 144))):
+            to = slice(at.start + 8, at.stop + 8)
+            kx, ky, kz, a, n, c = lookup(tables, source_ids[xi])
+            alpha[xi, at, :] = a
+            expo[xi, at, :] = n
+            exponent[xi, at, :] = 1.0 - 1.0 / n
+            cap[xi, at, :] = STORE * c
+            trans_z[xi, at, :] = upward_faces(kz)
+            side_x[xi, at.start // 17 : at.start // 17 + 8, :] = kx
+            side_y[xi, to, :] = ky
+        side_y[xi, 16:24, :] = edges[xi, 0]
+        side_y[xi, 136:144, :] = edges[xi, 1]
+
+    loop(EX, side_rows, 3)
+    arrival.wait()
 
     def layer(z):
         def tile(k, t):
@@ -348,23 +381,6 @@
             d_rel[xi, to, :] = drel_v
             own_c[xi, to, :] = cap[xi, at, :] * dsat_v
 
-    tables = tables_of(conductivity, vg_alpha, vg_n, capacity)
-
-    def side_rows(xi):
-        for source_ids, at in ((y_low, slice(0, 8)), (y_high, slice(136, 144))):
-            to = slice(at.start + 8, at.stop + 8)
-            kx, ky, kz, a, n, c = lookup(tables, source_ids[xi])
-            alpha[xi, at, :] = a
-            expo[xi, at, :] = n
-            exponent[xi, at, :] = 1.0 - 1.0 / n
-            cap[xi, at, :] = STORE * c
-            trans_z[xi, at, :] = upward_faces(kz)
-            side_x[xi, at.start // 17 : at.start // 17 + 8, :] = kx
-            side_y[xi, to, :] = ky
-        side_y[xi, 16:24, :] = edges[xi, 0]
-        side_y[xi, 136:144, :] = edges[xi, 1]
-
-    loop(EX, side_rows, 3)
     for copy in copies[:4]:
         copy.wait()
     loop(EX, curves, 2)
@@ -613,21 +629,21 @@
     numbers = jnp.arange(devices, dtype=jnp.int32)
     scratch = lambda *shape: pltpu.VMEM(shape, jnp.float32)
 
-    up_x = [(i, i + 1) for i in range(count_x - 1)]
-    down_x = [(i + 1, i) for i in range(count_x - 1)]
+    beside = [(i, i ^ 1) for i in range(count_x)]
+    across = [pair for i in range(1, count_x - 1, 2) for pair in ((i, i + 1), (i + 1, i))]
     up_y = [(i, i + 1) for i in range(count_y - 1)]
     down_y = [(i + 1, i) for i in range(count_y - 1)]
-    slot_of, ids, first, last = call(
+    slot_of, inner, outer = call(
         turn_ids_kernel,
-        [jax.ShapeDtypeStruct((8, 128), jnp.int32), f32(8, 128, 128)] + [f32(DEPTH, 128, 128)] * 2,
+        [jax.ShapeDtypeStruct((8, 128), jnp.int32)] + [f32(DEPTH, 128, 128)] * 2,
         [VMEM, VMEM],
-        [VMEM] * 4,
-        [],
+        [VMEM] * 3,
+        [scratch(8, 128, 128)],
         63,
         (10**6, 10**6),
     )(block_map, material_ids.reshape(1024, 128))
-    below = lax.ppermute(last, "gx", up_x)
-    above = lax.ppermute(first, "gx", down_x)
+    outer_in = lax.ppermute(outer, "gx", across)
+    inner_in = lax.ppermute(inner, "gx", beside)
 
     packed = call(
         pack_kernel,
@@ -638,7 +654,7 @@
         63,
         (10**6, 4 * 10**6),
     )(slot_of, held_head, held_head_old)
-    packed, below, above = lax.optimization_barrier((packed, below, above))
+    packed, inner_in, outer_in = lax.optimization_barrier((packed, inner_in, outer_in))
     arrived = lax.all_to_all(packed, AXES, split_axis=0, concat_axis=0, tiled=True)
 
     offsets = (0, -count_y, count_y, -1, 1, count_y - 1, -count_y - 1, count_y + 1, -count_y + 1)
@@ -647,28 +663,28 @@
         jnp.where(block_map[None] == bricks[:, None, None], numbers[None, :, None], 0), axis=1
     )
     first, last = call(
-        edge_ids_kernel, [f32(EX, 8, 128)] * 2, [VMEM] * 3, [VMEM] * 2, [], 8, (10**5, 10**6)
-    )(below, ids, above)
+        edge_ids_kernel, [f32(EX, 8, 128)] * 2, [VMEM] * 4, [VMEM] * 2, [], 8, (10**5, 10**6)
+    )(inner, outer, inner_in, outer_in)
     y_low = lax.ppermute(last, "gy", up_y)
     y_high = lax.ppermute(first, "gy", down_y)
     *fields, edges = call(
         properties_kernel,
         [f32(EX, 128, 128)] * 7 + [f32(EX, 2, 8, 128)],
-        [SMEM] * 4 + [VMEM] * 3,
+        [SMEM] * 4 + [VMEM] * 4,
         [HBM] * 8,
         [scratch(EX, 128, 128)] * 7 + [scratch(EX, 2, 8, 128), scratch(EX, 128, 128), scratch(EX, 136, 128)]
         + [pltpu.SemaphoreType.DMA((8,))],
         63,
         (40 * 10**6, 12 * 10**6),
-    )(conductivity, vg_alpha, vg_n, capacity, below, ids, above)
+    )(conductivity, vg_alpha, vg_n, capacity, inner, outer, inner_in, outer_in)
 
     kept, sums = call(
         main_kernel,
         [f32(4, 8, 128, 128), f32(devices, 128)],
-        [SMEM] * 5 + [VMEM] * 4 + [HBM] * 7,
+        [SMEM] * 5 + [HBM] + [VMEM] * 3 + [HBM] * 7,
         [HBM, VMEM],
-        [scratch(EX, EY, 128)] * 5 + [scratch(EX, PY, 128), scratch(EX, EY, 128)]
-        + [pltpu.SemaphoreType.DMA((11,)), scratch(devices * PIECE, 128)] + [scratch(EX, PY, 128)] * 16
+        [scratch(devices * PIECE, 128)] + [scratch(EX, EY, 128)] * 5 + [scratch(EX, PY, 128), scratch(EX, EY, 128)]
+        + [pltpu.SemaphoreType.DMA((12,)), scratch(devices * PIECE, 128)] + [scratch(EX, PY, 128)] * 16
         + [scratch(EX, 16, 128), scratch(EX, PY, 128)],
         63,
         (200 * 10**6, 16 * 10**6),

time: 105 us -> 101 us (0.962)
  starting transfers between devices: 30.2 us -> 27.7 us
  waiting for transfers between devices: 28.4 us -> 27.1 us
    ppermute x2, starting transfers between devices: 6.42 us -> 4.5 us  [the longest x1 3.08 us: body(): outer_in = lax.ppermute(outer, 'gx', across)]
    ppermute x2, waiting for transfers between devices: 2.8 us -> 1.63 us  [the longest x1 1.63 us: body(): outer_in = lax.ppermute(outer, 'gx', across)]
    unnamed x18 -> x20, local copies, waits for them, and re-layouts: 2.34 us -> 2.34 us
  transfers between devices with their start and end apart: 6 -> 6, of which waited for: 5 -> 5; matrix products, arithmetic and copies ran while one was open for 1% -> 1% of each run, Pallas kernels for 15% -> 16%
where the time goes in v5:
time: 101 us
  Pallas kernels  42.7 us (42%)
  starting transfers between devices  27.7 us (27%)
  waiting for transfers between devices  27.1 us (27%)
  local copies, waits for them, and re-layouts  2.34 us (2%)
    pallas_call x1, Pallas kernels, body(): call(main_kernel, [f32(4, 8, 128, 128), f32(devices, 128)], [SMEM] * 5 +...  22.3 us
    all_to_all x1, starting transfers between devices, body(): lax.all_to_all(packed, AXES, split_axis=0, concat_axis=0, tiled=True)  12.3 us
    pallas_call x1, Pallas kernels, body(): call(properties_kernel, [f32(EX, 128, 128)] * 7 + [f32(EX, 2, 8, 128)], [...  11.1 us
    ppermute x1, waiting for transfers between devices, body(): y_low = lax.ppermute(last, 'gy', up_y)  9.38 us
    all_to_all x1, waiting for transfers between devices, body(): lax.all_to_all(packed, AXES, split_axis=0, concat_axis=0, tiled=True)  7.89 us
    all_to_all x1, waiting for transfers between devices, body(): lax.all_to_all(sums.reshape(devices, 1, 128), AXES, split_axis=0, concat_...  7.4 us
    all_to_all x1, starting transfers between devices, body(): lax.all_to_all(sums.reshape(devices, 1, 128), AXES, split_axis=0, concat_...  6.12 us
    pallas_call x1, Pallas kernels, body(): call(pack_kernel, f32(devices * PIECE, 128), [SMEM, VMEM, VMEM], HBM, [sc...  3.85 us
  transfers between devices with their start and end apart: 6, of which 5 were waited for; matrix products, arithmetic and copies ran while one was open for 1% of the time, Pallas kernels for 16%

profile of v5, /device:TPU:1, one launch (start us, length us, event | category | flops | bytes accessed | tf_op | source)
XLA Modules:
  0.0 100.8 jit_solution(2013970948690509115)
XLA Ops:
  0.0 2.3 %shard_map.91 = (s32[8,128]{1,0:T(8,128)}, f32[5,128,128]{2,1,0:T(8,128)}, f32[5,128,128]{2,1,0:T(8,128)}) custom-call(s32[128,128]{1,0:T(8,128)} %block_map.1, s32[1024,128]{1,0:T(8,128)} %bitcast.10), custom_call_target="tpu_custom_call" | custom-call | flops 1000000 | bytes 1000000 | tf_op jit(solution)/shard_map/pallas_call | solution.py:636
  2.3 1.4 %collective-permute-start = (f32[5,128,128]{2,1,0:T(8,128)}, f32[5,128,128]{2,1,0:T(8,128)S(1)}, u32[]{:S(2)}, u32[]{:S(2)}) collective-permute-start(f32[5,128,128]{2,1,0:T(8,128)} %get-tuple-element.24.inner), channel_id=1, source_target_pairs={{0,8},{8,0},{16,24},{24,16},{32,40},{40,32},{48,56},{56,48},{64,72... | collective-permute-start | bytes 983048 | tf_op jit(solution)/shard_map/ppermute | solution.py:646
  3.7 3.1 %collective-permute-start.1 = (f32[5,128,128]{2,1,0:T(8,128)}, f32[5,128,128]{2,1,0:T(8,128)S(1)}, u32[]{:S(2)}, u32[]{:S(2)}) collective-permute-start(f32[5,128,128]{2,1,0:T(8,128)} %get-tuple-element.25.outer), channel_id=1, source_target_pairs={{8,16},{16,8},{24,32},{32,24},{40,48},{48,40},{56,64},{64,56},{72,... | collective-permute-start | bytes 983048 | tf_op jit(solution)/shard_map/ppermute | solution.py:645
  6.8 3.9 %shard_map.92 = f32[5120,128]{1,0:T(8,128)} custom-call(s32[8,128]{1,0:T(8,128)} %get-tuple-element.23.slot_of, f32[128,8,128]{2,1,0:T(8,128)} %head.1, f32[128,8,128]{2,1,0:T(8,128)} %old.1), custom_call_target="tpu_custom_call" | custom-call | flops 1000000 | bytes 4000000 | tf_op jit(solution)/shard_map/pallas_call | solution.py:648
  10.7 0.0 collective-permute-done.inner_in
  10.7 0.0 copy-start.3
  10.7 1.6 %collective-permute-done.1.outer_in = f32[5,128,128]{2,1,0:T(8,128)S(1)} collective-permute-done((f32[5,128,128]{2,1,0:T(8,128)}, f32[5,128,128]{2,1,0:T(8,128)S(1)}, u32[]{:S(2)}, u32[]{:S(2)}) %collective-permute-start.1) | collective-permute-done | bytes 327712 | tf_op jit(solution)/shard_map/ppermute | solution.py:645
  12.3 0.0 copy-start.4
  12.3 0.7 copy-done.4
  13.0 0.0 copy-start.9
  13.0 0.0 copy-start.1
  13.0 0.0 copy-start.2
  13.0 0.0 copy-start.5
  13.0 12.3 %all-to-all-start = ((f32[128,40,128]{2,1,0:T(8,128)}), f32[128,40,128]{2,1,0:T(8,128)}, u32[]{:S(2)}, u32[]{:S(2)}) async-start(f32[128,40,128]{2,1,0:T(8,128)} %bitcast.9), calls=%async_computation | async-start | bytes 5242880 | tf_op jit(solution)/shard_map/all_to_all | solution.py:658
  25.4 0.0 copy-start.6
  25.4 0.0 copy-done.9
  25.4 0.0 copy-done.3
  25.4 0.0 copy-done.1
  25.4 0.0 copy-done.2
  25.4 0.0 copy-done.5
  25.5 0.7 shard_map.93
  26.1 3.4 %collective-permute-start.2 = (f32[18,8,128]{2,1,0:T(8,128)}, f32[18,8,128]{2,1,0:T(8,128)S(1)}, u32[]{:S(2)}, u32[]{:S(2)}) collective-permute-start(f32[18,8,128]{2,1,0:T(8,128)} %get-tuple-element.29), channel_id=1, source_target_pairs={{0,1},{1,2},{2,3},{3,4},{4,5},{5,6},{6,7},{8,9},{9,10},{10,11},{11... | collective-permute-start | bytes 221192 | tf_op jit(solution)/shard_map/ppermute | solution.py:668
  29.6 1.3 %collective-permute-start.3 = (f32[18,8,128]{2,1,0:T(8,128)}, f32[18,8,128]{2,1,0:T(8,128)S(1)}, u32[]{:S(2)}, u32[]{:S(2)}) collective-permute-start(f32[18,8,128]{2,1,0:T(8,128)} %get-tuple-element.30), channel_id=1, source_target_pairs={{1,0},{2,1},{3,2},{4,3},{5,4},{6,5},{7,6},{9,8},{10,9},{11,10},{12... | collective-permute-start | bytes 221192 | tf_op jit(solution)/shard_map/ppermute | solution.py:669
  30.9 0.0 copy-done.6
  30.9 0.7 select_reduce_fusion.source
  31.6 11.1 %shard_map.94 = (f32[18,128,128]{2,1,0:T(8,128)}, f32[18,128,128]{2,1,0:T(8,128)}, f32[18,128,128]{2,1,0:T(8,128)}, f32[18,128,128]{2,1,0:T(8,128)}, f32[18,128,...) custom-call(f32[3,16]{1,0:T(4,128)} %conductivity.3, ...), custom_call_target="tpu_custom_call" | custom-call | flops 40000000 | bytes 12000000 | tf_op jit(solution)/shard_map/pallas_call | solution.py:670
  42.7 9.4 %collective-permute-done.2.y_low = f32[18,8,128]{2,1,0:T(8,128)S(1)} collective-permute-done((f32[18,8,128]{2,1,0:T(8,128)}, f32[18,8,128]{2,1,0:T(8,128)S(1)}, u32[]{:S(2)}, u32[]{:S(2)}) %collective-permute-start.2) | collective-permute-done | bytes 73760 | tf_op jit(solution)/shard_map/ppermute | solution.py:668
  52.1 0.0 copy-start.7
  52.1 0.8 collective-permute-done.3.y_high
  52.9 0.0 copy-start.8
  52.9 7.9 %all-to-all-done = f32[128,40,128]{2,1,0:T(8,128)} async-done(((f32[128,40,128]{2,1,0:T(8,128)}), f32[128,40,128]{2,1,0:T(8,128)}, u32[]{:S(2)}, u32[]{:S(2)}) %all-to-all-start) | async-done | bytes 2621472 | tf_op jit(solution)/shard_map/all_to_all | solution.py:658
  60.8 0.0 copy-done.7
  60.8 0.0 copy-done.8
  60.8 22.3 %shard_map.95 = (f32[4,8,128,128]{3,2,1,0:T(8,128)}, f32[128,128]{1,0:T(8,128)}) custom-call(s32[9,128]{1,0:T(8,128)} %select_reduce_fusion.source, f32[3,16]{1,0:T(4,128)} %conductivity.3, f32[16]{0:T(128)} %vg_alpha.3, f32[16]{0:T(128)} %vg_n.3, f32[16]{0:T(128)} %capacity.3, f32[5120,128]{1,0:T(8,128)} %bitcast.2.arrived, f32[18,8,128]{2,1,0:T(8,128)} %copy-done.7, ...), custom_call_target="tpu_custom_call" | custom-call | flops 200000000 | bytes 16000000 | tf_op jit(solution)/shard_map/pallas_call | solution.py:681
  83.1 6.1 %all-to-all-start.1 = ((f32[128,1,128]{2,1,0:T(1,128)}), f32[128,1,128]{2,1,0:T(1,128)S(1)}, u32[]{:S(2)}, u32[]{:S(2)}) async-start(f32[128,1,128]{2,1,0:T(1,128)} %bitcast.11), calls=%async_computation.1 | async-start | bytes 131072 | tf_op jit(solution)/shard_map/all_to_all | solution.py:692
  89.3 0.0 copy-start
  89.3 1.6 %copy-done = f32[4,8,128,128]{3,2,1,0:T(8,128)S(1)} copy-done((f32[4,8,128,128]{3,2,1,0:T(8,128)S(1)}, f32[4,8,128,128]{3,2,1,0:T(8,128)}, u32[]{:S(2)}) %copy-start) | copy-done | bytes 2097176
  90.9 0.6 shard_map.96.vectors
  91.5 7.4 %all-to-all-done.1 = f32[128,1,128]{2,1,0:T(1,128)S(1)} async-done(((f32[128,1,128]{2,1,0:T(1,128)}), f32[128,1,128]{2,1,0:T(1,128)S(1)}, u32[]{:S(2)}, u32[]{:S(2)}) %all-to-all-start.1) | async-done | bytes 65568 | tf_op jit(solution)/shard_map/all_to_all | solution.py:692
  98.9 1.9 %shard_map.97 = f32[1024,128]{1,0:T(8,128)} custom-call(f32[128,128]{1,0:T(8,128)S(1)} %bitcast.8, f32[4,1024,128]{2,1,0:T(8,128)S(1)} %shard_map.96.vectors), custom_call_target="tpu_custom_call" | custom-call | flops 1000000 | bytes 3000000 | tf_op jit(solution)/shard_map/pallas_call | solution.py:694
  (1 shorter events, 0.0 us)
Async XLA Ops:
  2.3 8.4 %collective-permute-start = (f32[5,128,128]{2,1,0:T(8,128)}, f32[5,128,128]{2,1,0:T(8,128)S(1)}, u32[]{:S(2)}, u32[]{:S(2)}) collective-permute-start(f32[5,128,128]{2,1,0:T(8,128)} %get-tuple-element.24.inner), channel_id=1, source_target_pairs={{0,8},{8,0},{16,24},{24,16},{32,40},{40,32},{48,56},{56,48},{64,72... | collective-permute-start | bytes 983048 | tf_op jit(solution)/shard_map/ppermute | solution.py:646
  3.7 8.6 %collective-permute-start.1 = (f32[5,128,128]{2,1,0:T(8,128)}, f32[5,128,128]{2,1,0:T(8,128)S(1)}, u32[]{:S(2)}, u32[]{:S(2)}) collective-permute-start(f32[5,128,128]{2,1,0:T(8,128)} %get-tuple-element.25.outer), channel_id=1, source_target_pairs={{8,16},{16,8},{24,32},{32,24},{40,48},{48,40},{56,64},{64,56},{72,... | collective-permute-start | bytes 983048 | tf_op jit(solution)/shard_map/ppermute | solution.py:645
  10.7 14.8 %copy-start.3 = (f32[5,128,128]{2,1,0:T(8,128)}, f32[5,128,128]{2,1,0:T(8,128)S(1)}, u32[]{:S(2)}) copy-start(f32[5,128,128]{2,1,0:T(8,128)S(1)} %collective-permute-done.inner_in) | copy-start | bytes 983044
  12.3 0.7 copy-start.4
  13.0 12.4 %copy-start.9 = (s32[9]{0:T(128)S(1)}, s32[9]{0:T(128)}, u32[]{:S(2)}) copy-start(s32[9]{0:T(128)} %constant.15.clone) | copy-start | bytes 112
  13.0 12.4 %copy-start.1 = (f32[5,128,128]{2,1,0:T(8,128)S(1)}, f32[5,128,128]{2,1,0:T(8,128)}, u32[]{:S(2)}) copy-start(f32[5,128,128]{2,1,0:T(8,128)} %get-tuple-element.24.inner) | copy-start | bytes 983044
  13.0 12.4 %copy-start.2 = (f32[5,128,128]{2,1,0:T(8,128)S(1)}, f32[5,128,128]{2,1,0:T(8,128)}, u32[]{:S(2)}) copy-start(f32[5,128,128]{2,1,0:T(8,128)} %get-tuple-element.25.outer) | copy-start | bytes 983044
  13.0 12.4 %copy-start.5 = (f32[5,128,128]{2,1,0:T(8,128)S(1)}, f32[5,128,128]{2,1,0:T(8,128)}, u32[]{:S(2)}) copy-start(f32[5,128,128]{2,1,0:T(8,128)} %copy-done.4) | copy-start | bytes 983044
  13.0 47.8 %all-to-all-start = ((f32[128,40,128]{2,1,0:T(8,128)}), f32[128,40,128]{2,1,0:T(8,128)}, u32[]{:S(2)}, u32[]{:S(2)}) async-start(f32[128,40,128]{2,1,0:T(8,128)} %bitcast.9), calls=%async_computation | async-start | bytes 5242880 | tf_op jit(solution)/shard_map/all_to_all | solution.py:658
  25.4 5.5 %copy-start.6 = (s32[128,128]{1,0:T(8,128)S(1)}, s32[128,128]{1,0:T(8,128)}, u32[]{:S(2)}) copy-start(s32[128,128]{1,0:T(8,128)} %block_map.1) | copy-start | bytes 196612
  26.1 25.9 %collective-permute-start.2 = (f32[18,8,128]{2,1,0:T(8,128)}, f32[18,8,128]{2,1,0:T(8,128)S(1)}, u32[]{:S(2)}, u32[]{:S(2)}) collective-permute-start(f32[18,8,128]{2,1,0:T(8,128)} %get-tuple-element.29), channel_id=1, source_target_pairs={{0,1},{1,2},{2,3},{3,4},{4,5},{5,6},{6,7},{8,9},{9,10},{10,11},{11... | collective-permute-start | bytes 221192 | tf_op jit(solution)/shard_map/ppermute | solution.py:668
  29.6 23.4 %collective-permute-start.3 = (f32[18,8,128]{2,1,0:T(8,128)}, f32[18,8,128]{2,1,0:T(8,128)S(1)}, u32[]{:S(2)}, u32[]{:S(2)}) collective-permute-start(f32[18,8,128]{2,1,0:T(8,128)} %get-tuple-element.30), channel_id=1, source_target_pairs={{1,0},{2,1},{3,2},{4,3},{5,4},{6,5},{7,6},{9,8},{10,9},{11,10},{12... | collective-permute-start | bytes 221192 | tf_op jit(solution)/shard_map/ppermute | solution.py:669
  52.1 8.7 %copy-start.7 = (f32[18,8,128]{2,1,0:T(8,128)}, f32[18,8,128]{2,1,0:T(8,128)S(1)}, u32[]{:S(2)}) copy-start(f32[18,8,128]{2,1,0:T(8,128)S(1)} %collective-permute-done.2.y_low) | copy-start | bytes 221188
  52.9 7.9 %copy-start.8 = (f32[18,8,128]{2,1,0:T(8,128)}, f32[18,8,128]{2,1,0:T(8,128)S(1)}, u32[]{:S(2)}) copy-start(f32[18,8,128]{2,1,0:T(8,128)S(1)} %collective-permute-done.3.y_high) | copy-start | bytes 221188
  83.1 15.7 %all-to-all-start.1 = ((f32[128,1,128]{2,1,0:T(1,128)}), f32[128,1,128]{2,1,0:T(1,128)S(1)}, u32[]{:S(2)}, u32[]{:S(2)}) async-start(f32[128,1,128]{2,1,0:T(1,128)} %bitcast.11), calls=%async_computation.1 | async-start | bytes 131072 | tf_op jit(solution)/shard_map/all_to_all | solution.py:692
  89.3 1.6 %copy-start = (f32[4,8,128,128]{3,2,1,0:T(8,128)S(1)}, f32[4,8,128,128]{3,2,1,0:T(8,128)}, u32[]{:S(2)}) copy-start(f32[4,8,128,128]{3,2,1,0:T(8,128)} %get-tuple-element.40.kept) | copy-start | bytes 6291460

commit v6 on v5

--- a/solution.py
+++ b/solution.py
@@ -9,7 +9,8 @@
 STORE = 4.0
 AXES = ("gx", "gy")
 
-PIECE = 40
+PIECE = 37
+LAYER = 40
 DEPTH = 5
 EX = 8 + 2 * DEPTH
 EY = 144
@@ -56,7 +57,7 @@
         old_below, old_above = old[below], old[above]
 
         def put(tile, value):
-            out[pl.ds(pl.multiple_of(b * PIECE + 8 * tile, 8), 8), :] = value
+            out[pl.ds(b * PIECE + 8 * tile, 8), :] = value
 
         put(0, head[own])
         put(1, old[own])
@@ -69,19 +70,24 @@
     low = lane % 16 < 8
     edge[0:16, :] = jnp.full((16, 128), -1.0, jnp.float32)
     edge[144:160, :] = jnp.full((16, 128), -1.0, jnp.float32)
-    for field, (y_row, corner_row) in enumerate(((32, 34), (33, 37))):
+    corners = []
+    for field in range(2):
         columns = jnp.zeros((128, 128), jnp.float32)
         for x in range(8):
             rows = out[pl.ds(8 * field + x, 128, stride=PIECE), :]
             columns = jnp.where(lane // 16 == x, pltpu.roll(rows, 16 * x + 8, 1), columns)
         edge[16:144, :] = columns
-        out[pl.ds(y_row, 128, stride=PIECE), :] = jnp.where(low, edge[15:143, :], edge[17:145, :])
-        out[pl.ds(corner_row, 128, stride=PIECE), :] = jnp.where(
-            lane < 64,
-            jnp.where(low, edge[23:151, :], edge[25:153, :]),
-            jnp.where(low, edge[7:135, :], edge[9:137, :]),
+        out[pl.ds(32 + field, 128, stride=PIECE), :] = jnp.where(low, edge[15:143, :], edge[17:145, :])
+        corners.append(
+            jnp.where(
+                lane < 64,
+                jnp.where(low, edge[23:151, :], edge[25:153, :]),
+                jnp.where(low, edge[7:135, :], edge[9:137, :]),
+            )
         )
-    copy = pltpu.make_async_copy(out, packed, sem)
+    from_old = jnp.where(low, pltpu.roll(corners[1], 124, 1), pltpu.roll(corners[1], 4, 1))
+    out[pl.ds(34, 128, stride=PIECE), :] = jnp.where((lane % 16 >= 4) & (lane % 16 < 12), corners[0], from_old)
+    copy = pltpu.make_async_copy(out.at[0 : packed.shape[0]], packed, sem)
     copy.start()
     copy.wait()
 
@@ -298,7 +304,7 @@
         pltpu.make_async_copy(a, b.at[:, 16:144] if b is trans_y else b.at[:, 8:136], sems.at[k])
         for k, (a, b) in enumerate(refs)
     ]
-    arrival = pltpu.make_async_copy(arrived, recv, sems.at[11])
+    arrival = pltpu.make_async_copy(arrived, recv.at[0 : arrived.shape[0]], sems.at[11])
     arrival.start()
     for copy in copies:
         copy.start()
@@ -326,10 +332,10 @@
 
     def layer(z):
         def tile(k, t):
-            return recv[pl.ds(pl.multiple_of(source[k, z] * PIECE + 8 * t, 8), 8), :]
+            return recv[pl.ds(source[k, z] * PIECE + 8 * t, 8), :]
 
         def put(t, value):
-            ordered[pl.ds(pl.multiple_of(z * PIECE + 8 * t, 8), 8), :] = value
+            ordered[pl.ds(pl.multiple_of(z * LAYER + 8 * t, 8), 8), :] = value
 
         put(0, tile(0, 0))
         put(1, tile(0, 1))
@@ -349,22 +355,24 @@
     loop(128, layer, 4)
 
     def plane(r):
-        return ordered[pl.ds(r, 128, stride=PIECE), :].T
+        return ordered[pl.ds(r, 128, stride=LAYER), :].T
 
     for xi, r in enumerate([19, 20, 21, 22, 23] + list(range(8)) + [16, 17, 18, 27, 28]):
         head[xi, 16:144, :] = plane(r)
     for xi, r in enumerate([36, 29, 30, 31] + list(range(8, 16)) + [24, 25, 26, 35]):
         old[xi + 1, 16:144, :] = plane(r)
-    for field, (y_row, corner_row) in ((head, (32, 34)), (old, (33, 37))):
+    corners = plane(34)
+    for field, y_row in ((head, 32), (old, 33)):
         sides = plane(y_row)
         for x in range(8):
             field[5 + x, 8:16, :] = sides[16 * x : 16 * x + 8]
             field[5 + x, 144:152, :] = sides[16 * x + 8 : 16 * x + 16]
-        corners = plane(corner_row)
         for x in range(8):
             xi = 13 + x if x < 4 else x - 3
-            field[xi, 8:16, :] = corners[16 * x : 16 * x + 8]
-            field[xi, 144:152, :] = corners[16 * x + 8 : 16 * x + 16]
+            beside = (corners[16 * x : 16 * x + 8], corners[16 * x + 8 : 16 * x + 16])
+            if field is old:
+                beside = [pltpu.roll(tile, 4, 0) for tile in beside]
+            field[xi, 8:16, :], field[xi, 144:152, :] = beside
     for xi in (0, 17):
         head[xi, 8:16, :] = jnp.full((8, 128), -1.0, jnp.float32)
         head[xi, 144:152, :] = jnp.full((8, 128), -1.0, jnp.float32)
@@ -398,28 +406,14 @@
 
     loop(EX, side_faces, 3)
 
-    def face(half, h_a, h_b, r_a, r_b, d_a, d_b, rise):
+    def face(half, low, high, rise):
+        (h_a, r_a, d_a), (h_b, r_b, d_b) = low, high
         potential = h_b - h_a
         if rise:
             potential = potential + rise
         along = half * (r_a + r_b)
         slope = half * potential
         return along + slope * d_b, along - slope * d_a, along * potential, slope * (d_a + d_b)
-
-    def x_faces(xi, to, at, h, r, d):
-        c_p, c_m, flux, both = face(
-            trans_x[xi, at, :], h, head[xi + 1, to, :], r, rel[xi + 1, to, :], d, d_rel[xi + 1, to, :], 0.0
-        )
-        cxp[xi, to, :] = c_p
-        cxm[xi + 1, to, :] = c_m
-        k1[xi, to, :] = flux
-        k2[xi, to, :] = both
-        return flux, both
-
-    for c in range(CHUNKS):
-        at = slice(CHUNK * c, CHUNK * (c + 1))
-        to = slice(8 + CHUNK * c, 8 + CHUNK * (c + 1))
-        x_faces(0, to, at, head[0, to, :], rel[0, to, :], d_rel[0, to, :])
 
     def coefficients(i):
         xi = i + 1
@@ -431,28 +425,30 @@
             _, log_old = wetness(old[xi, to, :], alpha[xi, at, :], expo[xi, at, :], exponent[xi, at, :])
             old_sat = jnp.exp(exponent[xi, at, :] * log_old)
             start = cap[xi, at, :] * (old_sat - k0[xi, to, :])
-            h, r, d = head[xi, to, :], rel[xi, to, :], d_rel[xi, to, :]
-            flux, both = x_faces(xi, to, at, h, r, d)
-            start = start + (flux - k1[xi - 1, to, :])
-            centre = own_c[xi, to, :] - (both - k2[xi - 1, to, :])
-            c_p, c_m, flux, both = face(
-                trans_y[xi, to, :], h, head[xi, up, :], r, rel[xi, up, :], d, d_rel[xi, up, :], 0.0
-            )
-            cyp[xi, to, :] = c_p
-            cym[xi, up, :] = c_m
-            k3[xi, to, :] = flux
-            k4[xi, to, :] = both
-            start = start + (flux - k3[xi, down, :])
-            centre = centre - (both - k4[xi, down, :])
-            c_p, c_m, flux, both = face(
-                trans_z[xi, at, :], h, pltpu.roll(h, 127, 1), r, pltpu.roll(r, 127, 1), d, pltpu.roll(d, 127, 1), 1.0
-            )
-            czp[xi, to, :] = c_p
-            czm[xi, to, :] = pltpu.roll(c_m, 1, 1)
-            own_c[xi, to, :] = centre - (both - pltpu.roll(both, 1, 1))
-            k0[xi, to, :] = start + (flux - pltpu.roll(flux, 1, 1))
-
-    loop(16, coefficients, 2)
+            centre = own_c[xi, to, :]
+            here = [f[xi, to, :] for f in (head, rel, d_rel)]
+            above_x = [f[xi + 1, to, :] for f in (head, rel, d_rel)]
+            below_x = [f[xi - 1, to, :] for f in (head, rel, d_rel)]
+            above_y = [f[xi, up, :] for f in (head, rel, d_rel)]
+            below_y = [f[xi, down, :] for f in (head, rel, d_rel)]
+            half_z = trans_z[xi, at, :]
+            above_z = [pltpu.roll(f, 127, 1) for f in here]
+            below_z = [pltpu.roll(f, 1, 1) for f in here]
+            for c_up, c_down, half_up, half_down, above, below, rise in (
+                (cxp, cxm, trans_x[xi, at, :], trans_x[xi - 1, at, :], above_x, below_x, 0.0),
+                (cyp, cym, trans_y[xi, to, :], trans_y[xi, down, :], above_y, below_y, 0.0),
+                (czp, czm, half_z, pltpu.roll(half_z, 1, 1), above_z, below_z, 1.0),
+            ):
+                c_p, _, flux, both = face(half_up, here, above, rise)
+                _, c_m, flux_m, both_m = face(half_down, below, here, rise)
+                c_up[xi, to, :] = c_p
+                c_down[xi, to, :] = c_m
+                start = start + (flux - flux_m)
+                centre = centre - (both - both_m)
+            own_c[xi, to, :] = centre
+            k0[xi, to, :] = start
+
+    loop(16, coefficients, 4)
 
     vectors = (k0, k1, k2, k3, k4)
     for step in range(4):
@@ -650,12 +646,14 @@
         f32(devices * PIECE, 128),
         [SMEM, VMEM, VMEM],
         HBM,
-        [scratch(devices * PIECE, 128), scratch(PY, 128), pltpu.SemaphoreType.DMA],
+        [scratch(devices * PIECE + 8, 128), scratch(PY, 128), pltpu.SemaphoreType.DMA],
         63,
         (10**6, 4 * 10**6),
     )(slot_of, held_head, held_head_old)
     packed, inner_in, outer_in = lax.optimization_barrier((packed, inner_in, outer_in))
-    arrived = lax.all_to_all(packed, AXES, split_axis=0, concat_axis=0, tiled=True)
+    arrived = lax.all_to_all(
+        packed.reshape(devices, PIECE, 1, 128), AXES, split_axis=0, concat_axis=0, tiled=True
+    ).reshape(devices * PIECE, 128)
 
     offsets = (0, -count_y, count_y, -1, 1, count_y - 1, -count_y - 1, count_y + 1, -count_y + 1)
     bricks = own_index + jnp.array(offsets, jnp.int32)
@@ -683,8 +681,8 @@
         [f32(4, 8, 128, 128), f32(devices, 128)],
         [SMEM] * 5 + [HBM] + [VMEM] * 3 + [HBM] * 7,
         [HBM, VMEM],
-        [scratch(devices * PIECE, 128)] + [scratch(EX, EY, 128)] * 5 + [scratch(EX, PY, 128), scratch(EX, EY, 128)]
-        + [pltpu.SemaphoreType.DMA((12,)), scratch(devices * PIECE, 128)] + [scratch(EX, PY, 128)] * 16
+        [scratch(devices * PIECE + 8, 128)] + [scratch(EX, EY, 128)] * 5 + [scratch(EX, PY, 128), scratch(EX, EY, 128)]
+        + [pltpu.SemaphoreType.DMA((12,)), scratch(128 * LAYER, 128)] + [scratch(EX, PY, 128)] * 16
         + [scratch(EX, 16, 128), scratch(EX, PY, 128)],
         63,
         (200 * 10**6, 16 * 10**6),

time: 101 us -> 97.1 us (0.961)
  waiting for transfers between devices: 27.1 us -> 25.1 us
  Pallas kernels: 42.7 us -> 40.8 us
    all_to_all x1, waiting for transfers between devices: 7.89 us -> 4.14 us  [body(): lax.all_to_all(packed.reshape(devices, PIECE, 1, 128), AXES, split_axis=0...]
    ppermute x1, waiting for transfers between devices: 0.83 us -> 3.15 us  [body(): y_high = lax.ppermute(first, 'gy', down_y)]
    pallas_call x1, Pallas kernels: 22.3 us -> 20.4 us  [body(): call(main_kernel, [f32(4, 8, 128, 128), f32(devices, 128)], [SMEM] * 5 +...]
  transfers between devices with their start and end apart: 6 -> 6, of which waited for: 5 -> 5; matrix products, arithmetic and copies ran while one was open for 1% -> 1% of each run, Pallas kernels for 16% -> 17%
where the time goes in v6:
time: 97.1 us; the launch traced here: 96.8 us
  Pallas kernels  40.8 us (42%)
  starting transfers between devices  27.6 us (28%)
  waiting for transfers between devices  25.1 us (26%)
  local copies, waits for them, and re-layouts  2.33 us (2%)
    pallas_call x1, Pallas kernels, body(): call(main_kernel, [f32(4, 8, 128, 128), f32(devices, 128)], [SMEM] * 5 +...  20.4 us
    all_to_all x1, starting transfers between devices, body(): lax.all_to_all(packed.reshape(devices, PIECE, 1, 128), AXES, split_axis=0...  12.3 us
    pallas_call x1, Pallas kernels, body(): call(properties_kernel, [f32(EX, 128, 128)] * 7 + [f32(EX, 2, 8, 128)], [...  11 us
    ppermute x1, waiting for transfers between devices, body(): y_low = lax.ppermute(last, 'gy', up_y)  8.79 us
    all_to_all x1, waiting for transfers between devices, body(): lax.all_to_all(sums.reshape(devices, 1, 128), AXES, split_axis=0, concat_...  7.4 us
    all_to_all x1, starting transfers between devices, body(): lax.all_to_all(sums.reshape(devices, 1, 128), AXES, split_axis=0, concat_...  6.05 us
    all_to_all x1, waiting for transfers between devices, body(): lax.all_to_all(packed.reshape(devices, PIECE, 1, 128), AXES, split_axis=0...  4.14 us
    pallas_call x1, Pallas kernels, body(): call(pack_kernel, f32(devices * PIECE, 128), [SMEM, VMEM, VMEM], HBM, [sc...  3.87 us
  transfers between devices with their start and end apart: 6, of which 5 were waited for; matrix products, arithmetic and copies ran while one was open for 1% of the time, Pallas kernels for 17%

profile of v6, /device:TPU:1, one launch (start us, length us, event | category | flops | bytes accessed | tf_op | source)
XLA Modules:
  0.0 96.8 jit_solution(3199072751451798114)
XLA Ops:
  0.0 2.3 %shard_map.91 = (s32[8,128]{1,0:T(8,128)}, f32[5,128,128]{2,1,0:T(8,128)}, f32[5,128,128]{2,1,0:T(8,128)}) custom-call(s32[128,128]{1,0:T(8,128)} %block_map.1, s32[1024,128]{1,0:T(8,128)} %bitcast.10), custom_call_target="tpu_custom_call" | custom-call | flops 1000000 | bytes 1000000 | tf_op jit(solution)/shard_map/pallas_call | solution.py:632
  2.3 1.4 %collective-permute-start = (f32[5,128,128]{2,1,0:T(8,128)}, f32[5,128,128]{2,1,0:T(8,128)S(1)}, u32[]{:S(2)}, u32[]{:S(2)}) collective-permute-start(f32[5,128,128]{2,1,0:T(8,128)} %get-tuple-element.24.inner), channel_id=1, source_target_pairs={{0,8},{8,0},{16,24},{24,16},{32,40},{40,32},{48,56},{56,48},{64,72... | collective-permute-start | bytes 983048 | tf_op jit(solution)/shard_map/ppermute | solution.py:642
  3.7 3.1 %collective-permute-start.1 = (f32[5,128,128]{2,1,0:T(8,128)}, f32[5,128,128]{2,1,0:T(8,128)S(1)}, u32[]{:S(2)}, u32[]{:S(2)}) collective-permute-start(f32[5,128,128]{2,1,0:T(8,128)} %get-tuple-element.25.outer), channel_id=1, source_target_pairs={{8,16},{16,8},{24,32},{32,24},{40,48},{48,40},{56,64},{64,56},{72,... | collective-permute-start | bytes 983048 | tf_op jit(solution)/shard_map/ppermute | solution.py:641
  6.8 3.9 %shard_map.92 = f32[4736,128]{1,0:T(8,128)} custom-call(s32[8,128]{1,0:T(8,128)} %get-tuple-element.23.slot_of, f32[128,8,128]{2,1,0:T(8,128)} %head.1, f32[128,8,128]{2,1,0:T(8,128)} %old.1), custom_call_target="tpu_custom_call" | custom-call | flops 1000000 | bytes 4000000 | tf_op jit(solution)/shard_map/pallas_call | solution.py:644
  10.7 0.0 collective-permute-done.inner_in
  10.7 0.0 copy-start.3
  10.7 1.6 %collective-permute-done.1.outer_in = f32[5,128,128]{2,1,0:T(8,128)S(1)} collective-permute-done((f32[5,128,128]{2,1,0:T(8,128)}, f32[5,128,128]{2,1,0:T(8,128)S(1)}, u32[]{:S(2)}, u32[]{:S(2)}) %collective-permute-start.1) | collective-permute-done | bytes 327712 | tf_op jit(solution)/shard_map/ppermute | solution.py:641
  12.3 0.0 copy-start.4
  12.3 0.7 copy-done.4
  13.1 0.0 copy-start.9
  13.1 0.0 copy-start.1
  13.1 0.0 copy-start.2
  13.1 0.0 copy-start.5
  13.1 12.3 %all-to-all-start = ((f32[128,37,1,128]{3,2,1,0:T(1,128)}), f32[128,37,1,128]{3,2,1,0:T(1,128)}, u32[]{:S(2)}, u32[]{:S(2)}) async-start(f32[128,37,1,128]{3,2,1,0:T(1,128)} %bitcast.9), calls=%async_computation | async-start | bytes 4849664 | tf_op jit(solution)/shard_map/all_to_all | solution.py:654
  25.4 0.0 copy-start.6
  25.4 0.0 copy-done.9
  25.4 0.0 copy-done.3
  25.5 0.0 copy-done.1
  25.5 0.0 copy-done.2
  25.5 0.0 copy-done.5
  25.5 0.7 shard_map.93
  26.2 3.4 %collective-permute-start.2 = (f32[18,8,128]{2,1,0:T(8,128)}, f32[18,8,128]{2,1,0:T(8,128)S(1)}, u32[]{:S(2)}, u32[]{:S(2)}) collective-permute-start(f32[18,8,128]{2,1,0:T(8,128)} %get-tuple-element.29), channel_id=1, source_target_pairs={{0,1},{1,2},{2,3},{3,4},{4,5},{5,6},{6,7},{8,9},{9,10},{10,11},{11... | collective-permute-start | bytes 221192 | tf_op jit(solution)/shard_map/ppermute | solution.py:666
  29.6 1.3 %collective-permute-start.3 = (f32[18,8,128]{2,1,0:T(8,128)}, f32[18,8,128]{2,1,0:T(8,128)S(1)}, u32[]{:S(2)}, u32[]{:S(2)}) collective-permute-start(f32[18,8,128]{2,1,0:T(8,128)} %get-tuple-element.30), channel_id=1, source_target_pairs={{1,0},{2,1},{3,2},{4,3},{5,4},{6,5},{7,6},{9,8},{10,9},{11,10},{12... | collective-permute-start | bytes 221192 | tf_op jit(solution)/shard_map/ppermute | solution.py:667
  30.9 0.0 copy-done.6
  30.9 0.7 select_reduce_fusion.source
  31.6 11.0 %shard_map.94 = (f32[18,128,128]{2,1,0:T(8,128)}, f32[18,128,128]{2,1,0:T(8,128)}, f32[18,128,128]{2,1,0:T(8,128)}, f32[18,128,128]{2,1,0:T(8,128)}, f32[18,128,...) custom-call(f32[3,16]{1,0:T(4,128)} %conductivity.3, ...), custom_call_target="tpu_custom_call" | custom-call | flops 40000000 | bytes 12000000 | tf_op jit(solution)/shard_map/pallas_call | solution.py:668
  42.7 8.8 %collective-permute-done.2.y_low = f32[18,8,128]{2,1,0:T(8,128)S(1)} collective-permute-done((f32[18,8,128]{2,1,0:T(8,128)}, f32[18,8,128]{2,1,0:T(8,128)S(1)}, u32[]{:S(2)}, u32[]{:S(2)}) %collective-permute-start.2) | collective-permute-done | bytes 73760 | tf_op jit(solution)/shard_map/ppermute | solution.py:666
  51.5 0.0 copy-start.7
  51.5 3.2 %collective-permute-done.3.y_high = f32[18,8,128]{2,1,0:T(8,128)S(1)} collective-permute-done((f32[18,8,128]{2,1,0:T(8,128)}, f32[18,8,128]{2,1,0:T(8,128)S(1)}, u32[]{:S(2)}, u32[]{:S(2)}) %collective-permute-start.3) | collective-permute-done | bytes 73760 | tf_op jit(solution)/shard_map/ppermute | solution.py:667
  54.6 0.0 copy-start.8
  54.6 4.1 %all-to-all-done = f32[128,37,1,128]{3,2,1,0:T(1,128)} async-done(((f32[128,37,1,128]{3,2,1,0:T(1,128)}), f32[128,37,1,128]{3,2,1,0:T(1,128)}, u32[]{:S(2)}, u32[]{:S(2)}) %all-to-all-start) | async-done | bytes 2424864 | tf_op jit(solution)/shard_map/all_to_all | solution.py:654
  58.8 0.0 copy-done.7
  58.8 0.0 copy-done.8
  58.8 20.4 %shard_map.95 = (f32[4,8,128,128]{3,2,1,0:T(8,128)}, f32[128,128]{1,0:T(8,128)}) custom-call(s32[9,128]{1,0:T(8,128)} %select_reduce_fusion.source, f32[3,16]{1,0:T(4,128)} %conductivity.3, f32[16]{0:T(128)} %vg_alpha.3, f32[16]{0:T(128)} %vg_n.3, f32[16]{0:T(128)} %capacity.3, f32[4736,128]{1,0:T(8,128)} %bitcast.2.arrived, f32[18,8,128]{2,1,0:T(8,128)} %copy-done.7, ...), custom_call_target="tpu_custom_call" | custom-call | flops 200000000 | bytes 16000000 | tf_op jit(solution)/shard_map/pallas_call | solution.py:679
  79.2 6.1 %all-to-all-start.1 = ((f32[128,1,128]{2,1,0:T(1,128)}), f32[128,1,128]{2,1,0:T(1,128)S(1)}, u32[]{:S(2)}, u32[]{:S(2)}) async-start(f32[128,1,128]{2,1,0:T(1,128)} %bitcast.11), calls=%async_computation.1 | async-start | bytes 131072 | tf_op jit(solution)/shard_map/all_to_all | solution.py:690
  85.3 0.0 copy-start
  85.3 1.6 %copy-done = f32[4,8,128,128]{3,2,1,0:T(8,128)S(1)} copy-done((f32[4,8,128,128]{3,2,1,0:T(8,128)S(1)}, f32[4,8,128,128]{3,2,1,0:T(8,128)}, u32[]{:S(2)}) %copy-start) | copy-done | bytes 2097176
  86.9 0.6 shard_map.96.vectors
  87.5 7.4 %all-to-all-done.1 = f32[128,1,128]{2,1,0:T(1,128)S(1)} async-done(((f32[128,1,128]{2,1,0:T(1,128)}), f32[128,1,128]{2,1,0:T(1,128)S(1)}, u32[]{:S(2)}, u32[]{:S(2)}) %all-to-all-start.1) | async-done | bytes 65568 | tf_op jit(solution)/shard_map/all_to_all | solution.py:690
  94.9 1.9 %shard_map.97 = f32[1024,128]{1,0:T(8,128)} custom-call(f32[128,128]{1,0:T(8,128)S(1)} %bitcast.8, f32[4,1024,128]{2,1,0:T(8,128)S(1)} %shard_map.96.vectors), custom_call_target="tpu_custom_call" | custom-call | flops 1000000 | bytes 3000000 | tf_op jit(solution)/shard_map/pallas_call | solution.py:692
  (1 shorter events, 0.0 us)
Async XLA Ops:
  2.3 8.4 %collective-permute-start = (f32[5,128,128]{2,1,0:T(8,128)}, f32[5,128,128]{2,1,0:T(8,128)S(1)}, u32[]{:S(2)}, u32[]{:S(2)}) collective-permute-start(f32[5,128,128]{2,1,0:T(8,128)} %get-tuple-element.24.inner), channel_id=1, source_target_pairs={{0,8},{8,0},{16,24},{24,16},{32,40},{40,32},{48,56},{56,48},{64,72... | collective-permute-start | bytes 983048 | tf_op jit(solution)/shard_map/ppermute | solution.py:642
  3.7 8.6 %collective-permute-start.1 = (f32[5,128,128]{2,1,0:T(8,128)}, f32[5,128,128]{2,1,0:T(8,128)S(1)}, u32[]{:S(2)}, u32[]{:S(2)}) collective-permute-start(f32[5,128,128]{2,1,0:T(8,128)} %get-tuple-element.25.outer), channel_id=1, source_target_pairs={{8,16},{16,8},{24,32},{32,24},{40,48},{48,40},{56,64},{64,56},{72,... | collective-permute-start | bytes 983048 | tf_op jit(solution)/shard_map/ppermute | solution.py:641
  10.7 14.7 %copy-start.3 = (f32[5,128,128]{2,1,0:T(8,128)}, f32[5,128,128]{2,1,0:T(8,128)S(1)}, u32[]{:S(2)}) copy-start(f32[5,128,128]{2,1,0:T(8,128)S(1)} %collective-permute-done.inner_in) | copy-start | bytes 983044
  12.3 0.7 copy-start.4
  13.1 12.4 %copy-start.9 = (s32[9]{0:T(128)S(1)}, s32[9]{0:T(128)}, u32[]{:S(2)}) copy-start(s32[9]{0:T(128)} %constant.15.clone) | copy-start | bytes 112
  13.1 12.4 %copy-start.1 = (f32[5,128,128]{2,1,0:T(8,128)S(1)}, f32[5,128,128]{2,1,0:T(8,128)}, u32[]{:S(2)}) copy-start(f32[5,128,128]{2,1,0:T(8,128)} %get-tuple-element.24.inner) | copy-start | bytes 983044
  13.1 12.4 %copy-start.2 = (f32[5,128,128]{2,1,0:T(8,128)S(1)}, f32[5,128,128]{2,1,0:T(8,128)}, u32[]{:S(2)}) copy-start(f32[5,128,128]{2,1,0:T(8,128)} %get-tuple-element.25.outer) | copy-start | bytes 983044
  13.1 12.4 %copy-start.5 = (f32[5,128,128]{2,1,0:T(8,128)S(1)}, f32[5,128,128]{2,1,0:T(8,128)}, u32[]{:S(2)}) copy-start(f32[5,128,128]{2,1,0:T(8,128)} %copy-done.4) | copy-start | bytes 983044
  13.1 45.7 %all-to-all-start = ((f32[128,37,1,128]{3,2,1,0:T(1,128)}), f32[128,37,1,128]{3,2,1,0:T(1,128)}, u32[]{:S(2)}, u32[]{:S(2)}) async-start(f32[128,37,1,128]{3,2,1,0:T(1,128)} %bitcast.9), calls=%async_computation | async-start | bytes 4849664 | tf_op jit(solution)/shard_map/all_to_all | solution.py:654
  25.4 5.5 %copy-start.6 = (s32[128,128]{1,0:T(8,128)S(1)}, s32[128,128]{1,0:T(8,128)}, u32[]{:S(2)}) copy-start(s32[128,128]{1,0:T(8,128)} %block_map.1) | copy-start | bytes 196612
  26.2 25.3 %collective-permute-start.2 = (f32[18,8,128]{2,1,0:T(8,128)}, f32[18,8,128]{2,1,0:T(8,128)S(1)}, u32[]{:S(2)}, u32[]{:S(2)}) collective-permute-start(f32[18,8,128]{2,1,0:T(8,128)} %get-tuple-element.29), channel_id=1, source_target_pairs={{0,1},{1,2},{2,3},{3,4},{4,5},{5,6},{6,7},{8,9},{9,10},{10,11},{11... | collective-permute-start | bytes 221192 | tf_op jit(solution)/shard_map/ppermute | solution.py:666
  29.6 25.0 %collective-permute-start.3 = (f32[18,8,128]{2,1,0:T(8,128)}, f32[18,8,128]{2,1,0:T(8,128)S(1)}, u32[]{:S(2)}, u32[]{:S(2)}) collective-permute-start(f32[18,8,128]{2,1,0:T(8,128)} %get-tuple-element.30), channel_id=1, source_target_pairs={{1,0},{2,1},{3,2},{4,3},{5,4},{6,5},{7,6},{9,8},{10,9},{11,10},{12... | collective-permute-start | bytes 221192 | tf_op jit(solution)/shard_map/ppermute | solution.py:667
  51.5 7.3 %copy-start.7 = (f32[18,8,128]{2,1,0:T(8,128)}, f32[18,8,128]{2,1,0:T(8,128)S(1)}, u32[]{:S(2)}) copy-start(f32[18,8,128]{2,1,0:T(8,128)S(1)} %collective-permute-done.2.y_low) | copy-start | bytes 221188
  54.6 4.2 %copy-start.8 = (f32[18,8,128]{2,1,0:T(8,128)}, f32[18,8,128]{2,1,0:T(8,128)S(1)}, u32[]{:S(2)}) copy-start(f32[18,8,128]{2,1,0:T(8,128)S(1)} %collective-permute-done.3.y_high) | copy-start | bytes 221188
  79.2 15.7 %all-to-all-start.1 = ((f32[128,1,128]{2,1,0:T(1,128)}), f32[128,1,128]{2,1,0:T(1,128)S(1)}, u32[]{:S(2)}, u32[]{:S(2)}) async-start(f32[128,1,128]{2,1,0:T(1,128)} %bitcast.11), calls=%async_computation.1 | async-start | bytes 131072 | tf_op jit(solution)/shard_map/all_to_all | solution.py:690
  85.3 1.6 %copy-start = (f32[4,8,128,128]{3,2,1,0:T(8,128)S(1)}, f32[4,8,128,128]{3,2,1,0:T(8,128)}, u32[]{:S(2)}) copy-start(f32[4,8,128,128]{3,2,1,0:T(8,128)} %get-tuple-element.40.kept) | copy-start | bytes 6291460

commit v7 on v6

--- a/solution.py
+++ b/solution.py
@@ -25,7 +25,7 @@
 
 
 def params(mib):
-    return pltpu.CompilerParams(vmem_limit_bytes=mib << 20)
+    return pltpu.CompilerParams(vmem_limit_bytes=int(mib * 2**20))
 
 
 VMEM = pl.BlockSpec(memory_space=pltpu.VMEM)
@@ -508,8 +508,8 @@
             halves = [split(value, 65537.0) for value in values]
             leading, rest = list(leading), list(rest)
             for e, (p, q) in enumerate(PAIRS):
-                leading[e] = leading[e] + halves[p][0] * halves[q][0]
-                rest[e] = rest[e] + (halves[p][0] * halves[q][1] + halves[p][1] * values[q])
+                leading[e], lost = two_sum(leading[e], halves[p][0] * halves[q][0])
+                rest[e] = rest[e] + ((halves[p][0] * halves[q][1] + halves[p][1] * values[q]) + lost)
         return leading, rest
 
     zeros = [jnp.zeros((8, 128), jnp.float32) for _ in PAIRS]
@@ -647,7 +647,7 @@
         [SMEM, VMEM, VMEM],
         HBM,
         [scratch(devices * PIECE + 8, 128), scratch(PY, 128), pltpu.SemaphoreType.DMA],
-        63,
+        63.75,
         (10**6, 4 * 10**6),
     )(slot_of, held_head, held_head_old)
     packed, inner_in, outer_in = lax.optimization_barrier((packed, inner_in, outer_in))

time: 97.1 us -> 97.9 us (level)
  Pallas kernels: 40.8 us -> 42.7 us
    pallas_call x1, Pallas kernels: 20.4 us -> 21.9 us  [body(): call(main_kernel, [f32(4, 8, 128, 128), f32(devices, 128)], [SMEM] * 5 +...]
    unnamed x20 -> x14, local copies, waits for them, and re-layouts: 2.33 us -> 1.61 us
where the time goes in v7:
time: 97.9 us; the launch traced here: 97.6 us
  Pallas kernels  42.7 us (44%)
  starting transfers between devices  27.6 us (28%)
  waiting for transfers between devices  24.8 us (25%)
  local copies, waits for them, and re-layouts  1.61 us (2%)
    pallas_call x1, Pallas kernels, body(): call(main_kernel, [f32(4, 8, 128, 128), f32(devices, 128)], [SMEM] * 5 +...  21.9 us
    all_to_all x1, starting transfers between devices, body(): lax.all_to_all(packed.reshape(devices, PIECE, 1, 128), AXES, split_axis=0...  12.3 us
    pallas_call x1, Pallas kernels, body(): call(properties_kernel, [f32(EX, 128, 128)] * 7 + [f32(EX, 2, 8, 128)], [...  11.1 us
    ppermute x1, waiting for transfers between devices, body(): y_low = lax.ppermute(last, 'gy', up_y)  8.24 us
    all_to_all x1, waiting for transfers between devices, body(): lax.all_to_all(sums.reshape(devices, 1, 128), AXES, split_axis=0, concat_...  7.38 us
    all_to_all x1, starting transfers between devices, body(): lax.all_to_all(sums.reshape(devices, 1, 128), AXES, split_axis=0, concat_...  6.06 us
    all_to_all x1, waiting for transfers between devices, body(): lax.all_to_all(packed.reshape(devices, PIECE, 1, 128), AXES, split_axis=0...  4.14 us
    pallas_call x1, Pallas kernels, body(): call(pack_kernel, f32(devices * PIECE, 128), [SMEM, VMEM, VMEM], HBM, [sc...  3.86 us
  transfers between devices with their start and end apart: 6, of which 5 were waited for; matrix products, arithmetic and copies ran while one was open for 1% of the time, Pallas kernels for 17%

profile of v7, /device:TPU:1, one launch (start us, length us, event | category | flops | bytes accessed | tf_op | source)
XLA Modules:
  0.0 97.6 jit_solution(17246136452658549105)
XLA Ops:
  0.0 2.3 %shard_map.91 = (s32[8,128]{1,0:T(8,128)}, f32[5,128,128]{2,1,0:T(8,128)}, f32[5,128,128]{2,1,0:T(8,128)}) custom-call(s32[128,128]{1,0:T(8,128)} %block_map.1, s32[1024,128]{1,0:T(8,128)} %bitcast.10), custom_call_target="tpu_custom_call" | custom-call | flops 1000000 | bytes 1000000 | tf_op jit(solution)/shard_map/pallas_call | solution.py:632
  2.3 1.4 %collective-permute-start = (f32[5,128,128]{2,1,0:T(8,128)}, f32[5,128,128]{2,1,0:T(8,128)}, u32[]{:S(2)}, u32[]{:S(2)}) collective-permute-start(f32[5,128,128]{2,1,0:T(8,128)} %get-tuple-element.24.inner), channel_id=1, source_target_pairs={{0,8},{8,0},{16,24},{24,16},{32,40},{40,32},{48,56},{56,48},{64,72... | collective-permute-start | bytes 983048 | tf_op jit(solution)/shard_map/ppermute | solution.py:642
  3.7 3.1 %collective-permute-start.1 = (f32[5,128,128]{2,1,0:T(8,128)}, f32[5,128,128]{2,1,0:T(8,128)}, u32[]{:S(2)}, u32[]{:S(2)}) collective-permute-start(f32[5,128,128]{2,1,0:T(8,128)} %get-tuple-element.25.outer), channel_id=1, source_target_pairs={{8,16},{16,8},{24,32},{32,24},{40,48},{48,40},{56,64},{64,56},{72,... | collective-permute-start | bytes 983048 | tf_op jit(solution)/shard_map/ppermute | solution.py:641
  6.8 3.9 %shard_map.92 = f32[4736,128]{1,0:T(8,128)} custom-call(s32[8,128]{1,0:T(8,128)} %get-tuple-element.23.slot_of, f32[128,8,128]{2,1,0:T(8,128)} %head.1, f32[128,8,128]{2,1,0:T(8,128)} %old.1), custom_call_target="tpu_custom_call" | custom-call | flops 1000000 | bytes 4000000 | tf_op jit(solution)/shard_map/pallas_call | solution.py:644
  10.7 0.0 collective-permute-done.inner_in
  10.7 1.7 %collective-permute-done.1.outer_in = f32[5,128,128]{2,1,0:T(8,128)} collective-permute-done((f32[5,128,128]{2,1,0:T(8,128)}, f32[5,128,128]{2,1,0:T(8,128)}, u32[]{:S(2)}, u32[]{:S(2)}) %collective-permute-start.1) | collective-permute-done | bytes 327712 | tf_op jit(solution)/shard_map/ppermute | solution.py:641
  12.4 0.0 copy-start.6
  12.4 0.0 copy-start.1
  12.4 0.0 copy-start.2
  12.4 12.3 %all-to-all-start = ((f32[128,37,1,128]{3,2,1,0:T(1,128)}), f32[128,37,1,128]{3,2,1,0:T(1,128)}, u32[]{:S(2)}, u32[]{:S(2)}) async-start(f32[128,37,1,128]{3,2,1,0:T(1,128)} %bitcast.9), calls=%async_computation | async-start | bytes 4849664 | tf_op jit(solution)/shard_map/all_to_all | solution.py:654
  24.8 0.0 copy-start.3
  24.8 0.0 copy-done.6
  24.8 0.0 copy-done.1
  24.8 0.0 copy-done.2
  24.8 1.1 %shard_map.93 = (f32[18,8,128]{2,1,0:T(8,128)S(1)}, f32[18,8,128]{2,1,0:T(8,128)S(1)}) custom-call(f32[5,128,128]{2,1,0:T(8,128)S(1)} %copy-done.1, f32[5,128,128]{2,1,0:T(8,128)S(1)} %copy-done.2, f32[5,128,128]{2,1,0:T(8,128)} %collective-permute-done.inner_in, f32[5,128,128]{2,1,0:T(8,128)} %collective-permute-done.1.outer_in), custom_call_target="tpu_custom_call" | custom-call | flops 100000 | bytes 1000000 | tf_op jit(solution)/shard_map/pallas_call | solution.py:663
  25.9 3.4 %collective-permute-start.2 = (f32[18,8,128]{2,1,0:T(8,128)S(1)}, f32[18,8,128]{2,1,0:T(8,128)S(1)}, u32[]{:S(2)}, u32[]{:S(2)}) collective-permute-start(f32[18,8,128]{2,1,0:T(8,128)S(1)} %get-tuple-element.29), channel_id=1, source_target_pairs={{0,1},{1,2},{2,3},{3,4},{4,5},{5,6},{6,7},{8,9},{9,10},{10,11},{11... | collective-permute-start | bytes 221192 | tf_op jit(solution)/shard_map/ppermute | solution.py:666
  29.4 1.3 %collective-permute-start.3 = (f32[18,8,128]{2,1,0:T(8,128)S(1)}, f32[18,8,128]{2,1,0:T(8,128)S(1)}, u32[]{:S(2)}, u32[]{:S(2)}) collective-permute-start(f32[18,8,128]{2,1,0:T(8,128)S(1)} %get-tuple-element.30), channel_id=1, source_target_pairs={{1,0},{2,1},{3,2},{4,3},{5,4},{6,5},{7,6},{9,8},{10,9},{11,10},{12... | collective-permute-start | bytes 221192 | tf_op jit(solution)/shard_map/ppermute | solution.py:667
  30.7 0.0 copy-done.3
  30.7 0.7 select_reduce_fusion.source
  31.4 11.1 %shard_map.94 = (f32[18,128,128]{2,1,0:T(8,128)}, f32[18,128,128]{2,1,0:T(8,128)}, f32[18,128,128]{2,1,0:T(8,128)}, f32[18,128,128]{2,1,0:T(8,128)}, f32[18,128,...) custom-call(f32[3,16]{1,0:T(4,128)} %conductivity.3, ...), custom_call_target="tpu_custom_call" | custom-call | flops 40000000 | bytes 12000000 | tf_op jit(solution)/shard_map/pallas_call | solution.py:668
  42.5 8.2 %collective-permute-done.2.y_low = f32[18,8,128]{2,1,0:T(8,128)S(1)} collective-permute-done((f32[18,8,128]{2,1,0:T(8,128)S(1)}, f32[18,8,128]{2,1,0:T(8,128)S(1)}, u32[]{:S(2)}, u32[]{:S(2)}) %collective-permute-start.2) | collective-permute-done | bytes 73760 | tf_op jit(solution)/shard_map/ppermute | solution.py:666
  50.7 0.0 copy-start.4
  50.7 3.3 %collective-permute-done.3.y_high = f32[18,8,128]{2,1,0:T(8,128)S(1)} collective-permute-done((f32[18,8,128]{2,1,0:T(8,128)S(1)}, f32[18,8,128]{2,1,0:T(8,128)S(1)}, u32[]{:S(2)}, u32[]{:S(2)}) %collective-permute-start.3) | collective-permute-done | bytes 73760 | tf_op jit(solution)/shard_map/ppermute | solution.py:667
  54.0 0.0 copy-start.5
  54.0 4.1 %all-to-all-done = f32[128,37,1,128]{3,2,1,0:T(1,128)} async-done(((f32[128,37,1,128]{3,2,1,0:T(1,128)}), f32[128,37,1,128]{3,2,1,0:T(1,128)}, u32[]{:S(2)}, u32[]{:S(2)}) %all-to-all-start) | async-done | bytes 2424864 | tf_op jit(solution)/shard_map/all_to_all | solution.py:654
  58.1 0.0 copy-done.4
  58.1 0.0 copy-done.5
  58.1 21.9 %shard_map.95 = (f32[4,8,128,128]{3,2,1,0:T(8,128)}, f32[128,128]{1,0:T(8,128)}) custom-call(s32[9,128]{1,0:T(8,128)} %select_reduce_fusion.source, f32[3,16]{1,0:T(4,128)} %conductivity.3, f32[16]{0:T(128)} %vg_alpha.3, f32[16]{0:T(128)} %vg_n.3, f32[16]{0:T(128)} %capacity.3, f32[4736,128]{1,0:T(8,128)} %bitcast.2.arrived, f32[18,8,128]{2,1,0:T(8,128)} %copy-done.4, ...), custom_call_target="tpu_custom_call" | custom-call | flops 200000000 | bytes 16000000 | tf_op jit(solution)/shard_map/pallas_call | solution.py:679
  80.0 6.1 %all-to-all-start.1 = ((f32[128,1,128]{2,1,0:T(1,128)}), f32[128,1,128]{2,1,0:T(1,128)S(1)}, u32[]{:S(2)}, u32[]{:S(2)}) async-start(f32[128,1,128]{2,1,0:T(1,128)} %bitcast.11), calls=%async_computation.1 | async-start | bytes 131072 | tf_op jit(solution)/shard_map/all_to_all | solution.py:690
  86.1 0.0 copy-start
  86.1 1.6 %copy-done = f32[4,8,128,128]{3,2,1,0:T(8,128)S(1)} copy-done((f32[4,8,128,128]{3,2,1,0:T(8,128)S(1)}, f32[4,8,128,128]{3,2,1,0:T(8,128)}, u32[]{:S(2)}) %copy-start) | copy-done | bytes 2097176
  87.7 0.6 shard_map.96.vectors
  88.3 7.4 %all-to-all-done.1 = f32[128,1,128]{2,1,0:T(1,128)S(1)} async-done(((f32[128,1,128]{2,1,0:T(1,128)}), f32[128,1,128]{2,1,0:T(1,128)S(1)}, u32[]{:S(2)}, u32[]{:S(2)}) %all-to-all-start.1) | async-done | bytes 65568 | tf_op jit(solution)/shard_map/all_to_all | solution.py:690
  95.7 1.9 %shard_map.97 = f32[1024,128]{1,0:T(8,128)} custom-call(f32[128,128]{1,0:T(8,128)S(1)} %bitcast.8, f32[4,1024,128]{2,1,0:T(8,128)S(1)} %shard_map.96.vectors), custom_call_target="tpu_custom_call" | custom-call | flops 1000000 | bytes 3000000 | tf_op jit(solution)/shard_map/pallas_call | solution.py:692
  (1 shorter events, 0.0 us)
Async XLA Ops:
  2.3 8.4 %collective-permute-start = (f32[5,128,128]{2,1,0:T(8,128)}, f32[5,128,128]{2,1,0:T(8,128)}, u32[]{:S(2)}, u32[]{:S(2)}) collective-permute-start(f32[5,128,128]{2,1,0:T(8,128)} %get-tuple-element.24.inner), channel_id=1, source_target_pairs={{0,8},{8,0},{16,24},{24,16},{32,40},{40,32},{48,56},{56,48},{64,72... | collective-permute-start | bytes 983048 | tf_op jit(solution)/shard_map/ppermute | solution.py:642
  3.7 8.7 %collective-permute-start.1 = (f32[5,128,128]{2,1,0:T(8,128)}, f32[5,128,128]{2,1,0:T(8,128)}, u32[]{:S(2)}, u32[]{:S(2)}) collective-permute-start(f32[5,128,128]{2,1,0:T(8,128)} %get-tuple-element.25.outer), channel_id=1, source_target_pairs={{8,16},{16,8},{24,32},{32,24},{40,48},{48,40},{56,64},{64,56},{72,... | collective-permute-start | bytes 983048 | tf_op jit(solution)/shard_map/ppermute | solution.py:641
  12.4 12.4 %copy-start.6 = (s32[9]{0:T(128)S(1)}, s32[9]{0:T(128)}, u32[]{:S(2)}) copy-start(s32[9]{0:T(128)} %constant.15.clone) | copy-start | bytes 112
  12.4 12.4 %copy-start.1 = (f32[5,128,128]{2,1,0:T(8,128)S(1)}, f32[5,128,128]{2,1,0:T(8,128)}, u32[]{:S(2)}) copy-start(f32[5,128,128]{2,1,0:T(8,128)} %get-tuple-element.24.inner) | copy-start | bytes 983044
  12.4 12.4 %copy-start.2 = (f32[5,128,128]{2,1,0:T(8,128)S(1)}, f32[5,128,128]{2,1,0:T(8,128)}, u32[]{:S(2)}) copy-start(f32[5,128,128]{2,1,0:T(8,128)} %get-tuple-element.25.outer) | copy-start | bytes 983044
  12.4 45.7 %all-to-all-start = ((f32[128,37,1,128]{3,2,1,0:T(1,128)}), f32[128,37,1,128]{3,2,1,0:T(1,128)}, u32[]{:S(2)}, u32[]{:S(2)}) async-start(f32[128,37,1,128]{3,2,1,0:T(1,128)} %bitcast.9), calls=%async_computation | async-start | bytes 4849664 | tf_op jit(solution)/shard_map/all_to_all | solution.py:654
  24.8 5.9 %copy-start.3 = (s32[128,128]{1,0:T(8,128)S(1)}, s32[128,128]{1,0:T(8,128)}, u32[]{:S(2)}) copy-start(s32[128,128]{1,0:T(8,128)} %block_map.1) | copy-start | bytes 196612
  25.9 24.8 %collective-permute-start.2 = (f32[18,8,128]{2,1,0:T(8,128)S(1)}, f32[18,8,128]{2,1,0:T(8,128)S(1)}, u32[]{:S(2)}, u32[]{:S(2)}) collective-permute-start(f32[18,8,128]{2,1,0:T(8,128)S(1)} %get-tuple-element.29), channel_id=1, source_target_pairs={{0,1},{1,2},{2,3},{3,4},{4,5},{5,6},{6,7},{8,9},{9,10},{10,11},{11... | collective-permute-start | bytes 221192 | tf_op jit(solution)/shard_map/ppermute | solution.py:666
  29.4 24.6 %collective-permute-start.3 = (f32[18,8,128]{2,1,0:T(8,128)S(1)}, f32[18,8,128]{2,1,0:T(8,128)S(1)}, u32[]{:S(2)}, u32[]{:S(2)}) collective-permute-start(f32[18,8,128]{2,1,0:T(8,128)S(1)} %get-tuple-element.30), channel_id=1, source_target_pairs={{1,0},{2,1},{3,2},{4,3},{5,4},{6,5},{7,6},{9,8},{10,9},{11,10},{12... | collective-permute-start | bytes 221192 | tf_op jit(solution)/shard_map/ppermute | solution.py:667
  50.7 7.4 %copy-start.4 = (f32[18,8,128]{2,1,0:T(8,128)}, f32[18,8,128]{2,1,0:T(8,128)S(1)}, u32[]{:S(2)}) copy-start(f32[18,8,128]{2,1,0:T(8,128)S(1)} %collective-permute-done.2.y_low) | copy-start | bytes 221188
  54.0 4.2 %copy-start.5 = (f32[18,8,128]{2,1,0:T(8,128)}, f32[18,8,128]{2,1,0:T(8,128)S(1)}, u32[]{:S(2)}) copy-start(f32[18,8,128]{2,1,0:T(8,128)S(1)} %collective-permute-done.3.y_high) | copy-start | bytes 221188
  80.0 15.6 %all-to-all-start.1 = ((f32[128,1,128]{2,1,0:T(1,128)}), f32[128,1,128]{2,1,0:T(1,128)S(1)}, u32[]{:S(2)}, u32[]{:S(2)}) async-start(f32[128,1,128]{2,1,0:T(1,128)} %bitcast.11), calls=%async_computation.1 | async-start | bytes 131072 | tf_op jit(solution)/shard_map/all_to_all | solution.py:690
  86.1 1.6 %copy-start = (f32[4,8,128,128]{3,2,1,0:T(8,128)S(1)}, f32[4,8,128,128]{3,2,1,0:T(8,128)}, u32[]{:S(2)}) copy-start(f32[4,8,128,128]{3,2,1,0:T(8,128)} %get-tuple-element.40.kept) | copy-start | bytes 6291460

commit v8 on v7

--- a/solution.py
+++ b/solution.py
@@ -352,7 +352,7 @@
             ),
         )
 
-    loop(128, layer, 4)
+    loop(128, layer, 8)
 
     def plane(r):
         return ordered[pl.ds(r, 128, stride=LAYER), :].T
@@ -391,7 +391,7 @@
 
     for copy in copies[:4]:
         copy.wait()
-    loop(EX, curves, 2)
+    loop(EX, curves, 3)
     for copy in copies[4:]:
         copy.wait()
 
@@ -500,9 +500,9 @@
 
     def products(i, totals):
         leading, rest = totals
-        xi = 5 + i // 8
-        first = 16 + 16 * (i % 8)
-        for k in range(2):
+        xi = 5 + i // 4
+        first = 16 + 32 * (i % 4)
+        for k in range(4):
             at = pl.ds(pl.multiple_of(first + 8 * k, 8), 8)
             values = [v[xi, at, :] * scale for v, scale in zip(vectors, scales)]
             halves = [split(value, 65537.0) for value in values]
@@ -513,7 +513,7 @@
         return leading, rest
 
     zeros = [jnp.zeros((8, 128), jnp.float32) for _ in PAIRS]
-    leading, rest = lax.fori_loop(0, 64, products, (zeros, list(zeros)))
+    leading, rest = lax.fori_loop(0, 32, products, (zeros, list(zeros)))
     groups = []
     for g in range(2):
         high = jnp.zeros((8, 128), jnp.float32)
@@ -596,14 +596,14 @@
     weights = [(coeffs[k][0] * scale_of(41 + k)) * inverse_first for k in range(4)]
 
     def rows_of(t):
-        for k in range(4):
-            at = pl.ds(pl.multiple_of(32 * t + 8 * k, 8), 8)
+        for k in range(16):
+            at = pl.ds(pl.multiple_of(128 * t + 8 * k, 8), 8)
             total = weights[0] * vectors[0, at, :]
             for j in range(1, 4):
                 total = total + weights[j] * vectors[j, at, :]
             out[at, :] = total
 
-    loop(32, rows_of)
+    loop(8, rows_of)
 
 
 def call(kernel, out_shape, in_specs, out_specs, scratch, mib, cost):

time: 97.9 us -> 97.2 us (level)
  no operation moved by 1% of the time
where the time goes in v8:
time: 97.2 us; the launch traced here: 96.8 us
  Pallas kernels  41.9 us (43%)
  starting transfers between devices  27.6 us (28%)
  waiting for transfers between devices  24.8 us (26%)
  local copies, waits for them, and re-layouts  1.61 us (2%)
    pallas_call x1, Pallas kernels, body(): call(main_kernel, [f32(4, 8, 128, 128), f32(devices, 128)], [SMEM] * 5 +...  21.2 us
    all_to_all x1, starting transfers between devices, body(): lax.all_to_all(packed.reshape(devices, PIECE, 1, 128), AXES, split_axis=0...  12.3 us
    pallas_call x1, Pallas kernels, body(): call(properties_kernel, [f32(EX, 128, 128)] * 7 + [f32(EX, 2, 8, 128)], [...  11.1 us
    ppermute x1, waiting for transfers between devices, body(): y_low = lax.ppermute(last, 'gy', up_y)  8.24 us
    all_to_all x1, waiting for transfers between devices, body(): lax.all_to_all(sums.reshape(devices, 1, 128), AXES, split_axis=0, concat_...  7.38 us
    all_to_all x1, starting transfers between devices, body(): lax.all_to_all(sums.reshape(devices, 1, 128), AXES, split_axis=0, concat_...  6.06 us
    all_to_all x1, waiting for transfers between devices, body(): lax.all_to_all(packed.reshape(devices, PIECE, 1, 128), AXES, split_axis=0...  4.14 us
    pallas_call x1, Pallas kernels, body(): call(pack_kernel, f32(devices * PIECE, 128), [SMEM, VMEM, VMEM], HBM, [sc...  3.86 us
  transfers between devices with their start and end apart: 6, of which 5 were waited for; matrix products, arithmetic and copies ran while one was open for 1% of the time, Pallas kernels for 17%

profile of v8, /device:TPU:1, one launch (start us, length us, event | category | flops | bytes accessed | tf_op | source)
XLA Modules:
  0.0 96.8 jit_solution(2807112741769731665)
XLA Ops:
  0.0 2.3 %shard_map.91 = (s32[8,128]{1,0:T(8,128)}, f32[5,128,128]{2,1,0:T(8,128)}, f32[5,128,128]{2,1,0:T(8,128)}) custom-call(s32[128,128]{1,0:T(8,128)} %block_map.1, s32[1024,128]{1,0:T(8,128)} %bitcast.10), custom_call_target="tpu_custom_call" | custom-call | flops 1000000 | bytes 1000000 | tf_op jit(solution)/shard_map/pallas_call | solution.py:632
  2.3 1.4 %collective-permute-start = (f32[5,128,128]{2,1,0:T(8,128)}, f32[5,128,128]{2,1,0:T(8,128)}, u32[]{:S(2)}, u32[]{:S(2)}) collective-permute-start(f32[5,128,128]{2,1,0:T(8,128)} %get-tuple-element.24.inner), channel_id=1, source_target_pairs={{0,8},{8,0},{16,24},{24,16},{32,40},{40,32},{48,56},{56,48},{64,72... | collective-permute-start | bytes 983048 | tf_op jit(solution)/shard_map/ppermute | solution.py:642
  3.7 3.1 %collective-permute-start.1 = (f32[5,128,128]{2,1,0:T(8,128)}, f32[5,128,128]{2,1,0:T(8,128)}, u32[]{:S(2)}, u32[]{:S(2)}) collective-permute-start(f32[5,128,128]{2,1,0:T(8,128)} %get-tuple-element.25.outer), channel_id=1, source_target_pairs={{8,16},{16,8},{24,32},{32,24},{40,48},{48,40},{56,64},{64,56},{72,... | collective-permute-start | bytes 983048 | tf_op jit(solution)/shard_map/ppermute | solution.py:641
  6.8 3.9 %shard_map.92 = f32[4736,128]{1,0:T(8,128)} custom-call(s32[8,128]{1,0:T(8,128)} %get-tuple-element.23.slot_of, f32[128,8,128]{2,1,0:T(8,128)} %head.1, f32[128,8,128]{2,1,0:T(8,128)} %old.1), custom_call_target="tpu_custom_call" | custom-call | flops 1000000 | bytes 4000000 | tf_op jit(solution)/shard_map/pallas_call | solution.py:644
  10.7 0.0 collective-permute-done.inner_in
  10.7 1.7 %collective-permute-done.1.outer_in = f32[5,128,128]{2,1,0:T(8,128)} collective-permute-done((f32[5,128,128]{2,1,0:T(8,128)}, f32[5,128,128]{2,1,0:T(8,128)}, u32[]{:S(2)}, u32[]{:S(2)}) %collective-permute-start.1) | collective-permute-done | bytes 327712 | tf_op jit(solution)/shard_map/ppermute | solution.py:641
  12.4 0.0 copy-start.6
  12.4 0.0 copy-start.1
  12.4 0.0 copy-start.2
  12.4 12.3 %all-to-all-start = ((f32[128,37,1,128]{3,2,1,0:T(1,128)}), f32[128,37,1,128]{3,2,1,0:T(1,128)}, u32[]{:S(2)}, u32[]{:S(2)}) async-start(f32[128,37,1,128]{3,2,1,0:T(1,128)} %bitcast.9), calls=%async_computation | async-start | bytes 4849664 | tf_op jit(solution)/shard_map/all_to_all | solution.py:654
  24.8 0.0 copy-start.3
  24.8 0.0 copy-done.6
  24.8 0.0 copy-done.1
  24.8 0.0 copy-done.2
  24.8 1.1 %shard_map.93 = (f32[18,8,128]{2,1,0:T(8,128)S(1)}, f32[18,8,128]{2,1,0:T(8,128)S(1)}) custom-call(f32[5,128,128]{2,1,0:T(8,128)S(1)} %copy-done.1, f32[5,128,128]{2,1,0:T(8,128)S(1)} %copy-done.2, f32[5,128,128]{2,1,0:T(8,128)} %collective-permute-done.inner_in, f32[5,128,128]{2,1,0:T(8,128)} %collective-permute-done.1.outer_in), custom_call_target="tpu_custom_call" | custom-call | flops 100000 | bytes 1000000 | tf_op jit(solution)/shard_map/pallas_call | solution.py:663
  25.9 3.4 %collective-permute-start.2 = (f32[18,8,128]{2,1,0:T(8,128)S(1)}, f32[18,8,128]{2,1,0:T(8,128)S(1)}, u32[]{:S(2)}, u32[]{:S(2)}) collective-permute-start(f32[18,8,128]{2,1,0:T(8,128)S(1)} %get-tuple-element.29), channel_id=1, source_target_pairs={{0,1},{1,2},{2,3},{3,4},{4,5},{5,6},{6,7},{8,9},{9,10},{10,11},{11... | collective-permute-start | bytes 221192 | tf_op jit(solution)/shard_map/ppermute | solution.py:666
  29.4 1.3 %collective-permute-start.3 = (f32[18,8,128]{2,1,0:T(8,128)S(1)}, f32[18,8,128]{2,1,0:T(8,128)S(1)}, u32[]{:S(2)}, u32[]{:S(2)}) collective-permute-start(f32[18,8,128]{2,1,0:T(8,128)S(1)} %get-tuple-element.30), channel_id=1, source_target_pairs={{1,0},{2,1},{3,2},{4,3},{5,4},{6,5},{7,6},{9,8},{10,9},{11,10},{12... | collective-permute-start | bytes 221192 | tf_op jit(solution)/shard_map/ppermute | solution.py:667
  30.7 0.0 copy-done.3
  30.7 0.7 select_reduce_fusion.source
  31.4 11.1 %shard_map.94 = (f32[18,128,128]{2,1,0:T(8,128)}, f32[18,128,128]{2,1,0:T(8,128)}, f32[18,128,128]{2,1,0:T(8,128)}, f32[18,128,128]{2,1,0:T(8,128)}, f32[18,128,...) custom-call(f32[3,16]{1,0:T(4,128)} %conductivity.3, ...), custom_call_target="tpu_custom_call" | custom-call | flops 40000000 | bytes 12000000 | tf_op jit(solution)/shard_map/pallas_call | solution.py:668
  42.5 8.2 %collective-permute-done.2.y_low = f32[18,8,128]{2,1,0:T(8,128)S(1)} collective-permute-done((f32[18,8,128]{2,1,0:T(8,128)S(1)}, f32[18,8,128]{2,1,0:T(8,128)S(1)}, u32[]{:S(2)}, u32[]{:S(2)}) %collective-permute-start.2) | collective-permute-done | bytes 73760 | tf_op jit(solution)/shard_map/ppermute | solution.py:666
  50.7 0.0 copy-start.4
  50.7 3.3 %collective-permute-done.3.y_high = f32[18,8,128]{2,1,0:T(8,128)S(1)} collective-permute-done((f32[18,8,128]{2,1,0:T(8,128)S(1)}, f32[18,8,128]{2,1,0:T(8,128)S(1)}, u32[]{:S(2)}, u32[]{:S(2)}) %collective-permute-start.3) | collective-permute-done | bytes 73760 | tf_op jit(solution)/shard_map/ppermute | solution.py:667
  54.0 0.0 copy-start.5
  54.0 4.1 %all-to-all-done = f32[128,37,1,128]{3,2,1,0:T(1,128)} async-done(((f32[128,37,1,128]{3,2,1,0:T(1,128)}), f32[128,37,1,128]{3,2,1,0:T(1,128)}, u32[]{:S(2)}, u32[]{:S(2)}) %all-to-all-start) | async-done | bytes 2424864 | tf_op jit(solution)/shard_map/all_to_all | solution.py:654
  58.1 0.0 copy-done.4
  58.1 0.0 copy-done.5
  58.1 21.2 %shard_map.95 = (f32[4,8,128,128]{3,2,1,0:T(8,128)}, f32[128,128]{1,0:T(8,128)}) custom-call(s32[9,128]{1,0:T(8,128)} %select_reduce_fusion.source, f32[3,16]{1,0:T(4,128)} %conductivity.3, f32[16]{0:T(128)} %vg_alpha.3, f32[16]{0:T(128)} %vg_n.3, f32[16]{0:T(128)} %capacity.3, f32[4736,128]{1,0:T(8,128)} %bitcast.2.arrived, f32[18,8,128]{2,1,0:T(8,128)} %copy-done.4, ...), custom_call_target="tpu_custom_call" | custom-call | flops 200000000 | bytes 16000000 | tf_op jit(solution)/shard_map/pallas_call | solution.py:679
  79.4 6.1 %all-to-all-start.1 = ((f32[128,1,128]{2,1,0:T(1,128)}), f32[128,1,128]{2,1,0:T(1,128)S(1)}, u32[]{:S(2)}, u32[]{:S(2)}) async-start(f32[128,1,128]{2,1,0:T(1,128)} %bitcast.11), calls=%async_computation.1 | async-start | bytes 131072 | tf_op jit(solution)/shard_map/all_to_all | solution.py:690
  85.5 0.0 copy-start
  85.5 1.6 %copy-done = f32[4,8,128,128]{3,2,1,0:T(8,128)S(1)} copy-done((f32[4,8,128,128]{3,2,1,0:T(8,128)S(1)}, f32[4,8,128,128]{3,2,1,0:T(8,128)}, u32[]{:S(2)}) %copy-start) | copy-done | bytes 2097176
  87.0 0.6 shard_map.96.vectors
  87.7 7.4 %all-to-all-done.1 = f32[128,1,128]{2,1,0:T(1,128)S(1)} async-done(((f32[128,1,128]{2,1,0:T(1,128)}), f32[128,1,128]{2,1,0:T(1,128)S(1)}, u32[]{:S(2)}, u32[]{:S(2)}) %all-to-all-start.1) | async-done | bytes 65568 | tf_op jit(solution)/shard_map/all_to_all | solution.py:690
  95.0 1.8 %shard_map.97 = f32[1024,128]{1,0:T(8,128)} custom-call(f32[128,128]{1,0:T(8,128)S(1)} %bitcast.8, f32[4,1024,128]{2,1,0:T(8,128)S(1)} %shard_map.96.vectors), custom_call_target="tpu_custom_call" | custom-call | flops 1000000 | bytes 3000000 | tf_op jit(solution)/shard_map/pallas_call | solution.py:692
  (1 shorter events, 0.0 us)
Async XLA Ops:
  2.3 8.4 %collective-permute-start = (f32[5,128,128]{2,1,0:T(8,128)}, f32[5,128,128]{2,1,0:T(8,128)}, u32[]{:S(2)}, u32[]{:S(2)}) collective-permute-start(f32[5,128,128]{2,1,0:T(8,128)} %get-tuple-element.24.inner), channel_id=1, source_target_pairs={{0,8},{8,0},{16,24},{24,16},{32,40},{40,32},{48,56},{56,48},{64,72... | collective-permute-start | bytes 983048 | tf_op jit(solution)/shard_map/ppermute | solution.py:642
  3.7 8.7 %collective-permute-start.1 = (f32[5,128,128]{2,1,0:T(8,128)}, f32[5,128,128]{2,1,0:T(8,128)}, u32[]{:S(2)}, u32[]{:S(2)}) collective-permute-start(f32[5,128,128]{2,1,0:T(8,128)} %get-tuple-element.25.outer), channel_id=1, source_target_pairs={{8,16},{16,8},{24,32},{32,24},{40,48},{48,40},{56,64},{64,56},{72,... | collective-permute-start | bytes 983048 | tf_op jit(solution)/shard_map/ppermute | solution.py:641
  12.4 12.4 %copy-start.6 = (s32[9]{0:T(128)S(1)}, s32[9]{0:T(128)}, u32[]{:S(2)}) copy-start(s32[9]{0:T(128)} %constant.15.clone) | copy-start | bytes 112
  12.4 12.4 %copy-start.1 = (f32[5,128,128]{2,1,0:T(8,128)S(1)}, f32[5,128,128]{2,1,0:T(8,128)}, u32[]{:S(2)}) copy-start(f32[5,128,128]{2,1,0:T(8,128)} %get-tuple-element.24.inner) | copy-start | bytes 983044
  12.4 12.4 %copy-start.2 = (f32[5,128,128]{2,1,0:T(8,128)S(1)}, f32[5,128,128]{2,1,0:T(8,128)}, u32[]{:S(2)}) copy-start(f32[5,128,128]{2,1,0:T(8,128)} %get-tuple-element.25.outer) | copy-start | bytes 983044
  12.4 45.7 %all-to-all-start = ((f32[128,37,1,128]{3,2,1,0:T(1,128)}), f32[128,37,1,128]{3,2,1,0:T(1,128)}, u32[]{:S(2)}, u32[]{:S(2)}) async-start(f32[128,37,1,128]{3,2,1,0:T(1,128)} %bitcast.9), calls=%async_computation | async-start | bytes 4849664 | tf_op jit(solution)/shard_map/all_to_all | solution.py:654
  24.8 5.9 %copy-start.3 = (s32[128,128]{1,0:T(8,128)S(1)}, s32[128,128]{1,0:T(8,128)}, u32[]{:S(2)}) copy-start(s32[128,128]{1,0:T(8,128)} %block_map.1) | copy-start | bytes 196612
  25.9 24.8 %collective-permute-start.2 = (f32[18,8,128]{2,1,0:T(8,128)S(1)}, f32[18,8,128]{2,1,0:T(8,128)S(1)}, u32[]{:S(2)}, u32[]{:S(2)}) collective-permute-start(f32[18,8,128]{2,1,0:T(8,128)S(1)} %get-tuple-element.29), channel_id=1, source_target_pairs={{0,1},{1,2},{2,3},{3,4},{4,5},{5,6},{6,7},{8,9},{9,10},{10,11},{11... | collective-permute-start | bytes 221192 | tf_op jit(solution)/shard_map/ppermute | solution.py:666
  29.4 24.6 %collective-permute-start.3 = (f32[18,8,128]{2,1,0:T(8,128)S(1)}, f32[18,8,128]{2,1,0:T(8,128)S(1)}, u32[]{:S(2)}, u32[]{:S(2)}) collective-permute-start(f32[18,8,128]{2,1,0:T(8,128)S(1)} %get-tuple-element.30), channel_id=1, source_target_pairs={{1,0},{2,1},{3,2},{4,3},{5,4},{6,5},{7,6},{9,8},{10,9},{11,10},{12... | collective-permute-start | bytes 221192 | tf_op jit(solution)/shard_map/ppermute | solution.py:667
  50.7 7.4 %copy-start.4 = (f32[18,8,128]{2,1,0:T(8,128)}, f32[18,8,128]{2,1,0:T(8,128)S(1)}, u32[]{:S(2)}) copy-start(f32[18,8,128]{2,1,0:T(8,128)S(1)} %collective-permute-done.2.y_low) | copy-start | bytes 221188
  54.0 4.2 %copy-start.5 = (f32[18,8,128]{2,1,0:T(8,128)}, f32[18,8,128]{2,1,0:T(8,128)S(1)}, u32[]{:S(2)}) copy-start(f32[18,8,128]{2,1,0:T(8,128)S(1)} %collective-permute-done.3.y_high) | copy-start | bytes 221188
  79.4 15.6 %all-to-all-start.1 = ((f32[128,1,128]{2,1,0:T(1,128)}), f32[128,1,128]{2,1,0:T(1,128)S(1)}, u32[]{:S(2)}, u32[]{:S(2)}) async-start(f32[128,1,128]{2,1,0:T(1,128)} %bitcast.11), calls=%async_computation.1 | async-start | bytes 131072 | tf_op jit(solution)/shard_map/all_to_all | solution.py:690
  85.5 1.6 %copy-start = (f32[4,8,128,128]{3,2,1,0:T(8,128)S(1)}, f32[4,8,128,128]{3,2,1,0:T(8,128)}, u32[]{:S(2)}) copy-start(f32[4,8,128,128]{3,2,1,0:T(8,128)} %get-tuple-element.40.kept) | copy-start | bytes 6291460
